TPU v7x, 32 devices: a whole 2x2x4 slice. The times are simulated.
32 devices in a mesh: batch: 8 (over y, x, core), seq: 4 (over z).
Axes of the slice: x: 2, y: 2, z: 4, core: 2. Of those that a mesh axis runs over, the one named last changes fastest.
Arguments:
- inputs: bfloat16 [16, 512, 1536], P('batch', 'seq'), may hold values from -6 to 6
- output_grad: bfloat16 [16, 512, 1536], P('batch', 'seq'), may hold values from -6 to 6
- source_tags: int32 [16], P('batch'), may hold values from 0 to 7
- source_counts: int32 [8], replicated, may hold values from 256 to 1023
- gain_in: bfloat16 [1536], P(('batch', 'seq')), may hold values from 0.099609375 to 1.8984375
- w_query: bfloat16 [1536, 1536], P(('batch', 'seq')), may hold values from -0.15625 to 0.15625
- w_key: bfloat16 [1536, 1536], P(('batch', 'seq')), may hold values from -0.15625 to 0.15625
- w_value: bfloat16 [1536, 1536], P(('batch', 'seq')), may hold values from -0.15625 to 0.15625
- kernel: float32 [16, 6, 11], replicated, may hold values from -1.25 to 1.25
- mixing: float32 [16, 2], replicated, may hold values from 0.25 to 1.25
- gain_head: bfloat16 [1536], P(('batch', 'seq')), may hold values from 0.099609375 to 1.8984375
- w_out: bfloat16 [1536, 1536], P(('batch', 'seq')), may hold values from -0.15625 to 0.15625
- gain_mid: bfloat16 [1536], P(('batch', 'seq')), may hold values from 0.099609375 to 1.8984375
- w_gate: bfloat16 [1536, 4096], P('batch', 'seq'), may hold values from -0.15625 to 0.15625
- w_up: bfloat16 [1536, 4096], P('batch', 'seq'), may hold values from -0.15625 to 0.15625
- w_down: bfloat16 [4096, 1536], P('seq', 'batch'), may hold values from -0.09375 to 0.09375
Outputs:
- output: bfloat16 [16, 512, 1536], P('batch', 'seq')
- input_grad: bfloat16 [16, 512, 1536], P('batch', 'seq')
- grad_gain_in: float32 [1536], P(('batch', 'seq'))
- grad_query: float32 [1536, 1536], P(('batch', 'seq'))
- grad_key: float32 [1536, 1536], P(('batch', 'seq'))
- grad_value: float32 [1536, 1536], P(('batch', 'seq'))
- grad_kernel: float32 [16, 6, 11], replicated
- grad_mixing: float32 [16, 2], replicated
- grad_gain_head: float32 [1536], P(('batch', 'seq'))
- grad_out: float32 [1536, 1536], P(('batch', 'seq'))
- grad_gain_mid: float32 [1536], P(('batch', 'seq'))
- grad_gate: float32 [1536, 4096], P('batch', 'seq')
- grad_up: float32 [1536, 4096], P('batch', 'seq')
- grad_down: float32 [4096, 1536], P('seq', 'batch')
All inputs are finite; a program needn't handle non-finite values.
Results may differ from a plain program's by a relative error of at most 0.018.
The roundings to bfloat16 on the way count: a program that leaves them out, or rounds other values in their place, can miss the bound.
Values may be sent and summed in bfloat16 or wider, within the bound.
No kernel may reach another device: no remote copies, remote signals or barrier semaphores. Data moves between devices by JAX's collectives and lax.ppermute only.
A program may use at most 384 MiB of HBM per device.

v0:
```python
import math

import jax
import jax.numpy as jnp
from jax import lax
from jax.sharding import PartitionSpec as P

H = 16
DH = 96
QUERY_TAPS = 6
KEY_TAPS = 11


def project(left, right):
    return jnp.dot(left, right, preferred_element_type=jnp.float32)


def project_tn(left, right):
    return lax.dot_general(
        left, right, (((0,), (0,)), ((), ())), preferred_element_type=jnp.float32
    )


def project_nt(left, right):
    return lax.dot_general(
        left, right, (((1,), (1,)), ((), ())), preferred_element_type=jnp.float32
    )


def rms_scale(values, gain):
    return values * lax.rsqrt(jnp.mean(values * values, axis=-1, keepdims=True) + 1e-06) * gain


def head_norm(values, gain):
    row_count = values.shape[0]
    grouped = values.reshape(row_count, H, DH)
    centred = grouped - jnp.mean(grouped, axis=-1, keepdims=True)
    spread = jnp.mean(centred * centred, axis=-1, keepdims=True)
    return (centred * lax.rsqrt(spread + 1e-05)).reshape(row_count, H * DH) * gain


def swiglu(gate_in, up_in):
    return jax.nn.silu(gate_in) * up_in


def mixed_probs(raw_scores, kernel_pair, mixing_pair, first_row):
    rim = QUERY_TAPS - 1
    reach = KEY_TAPS // 2
    row_count = raw_scores.shape[1] - rim
    key_count = raw_scores.shape[2]
    key_pos = jnp.arange(key_count, dtype=jnp.int32)[None, :]
    query_pos = jnp.arange(row_count + rim, dtype=jnp.int32)[:, None] + (first_row - rim)
    masked = jnp.where(key_pos <= query_pos, raw_scores, 0.0)
    padded = jnp.pad(masked, ((0, 0), (0, 0), (reach, reach)))
    total = jnp.zeros((2, row_count, key_count), jnp.float32)
    for row_lag in range(QUERY_TAPS):
        for key_lag in range(KEY_TAPS):
            window = padded[
                :,
                rim - row_lag : rim - row_lag + row_count,
                2 * reach - key_lag : 2 * reach - key_lag + key_count,
            ]
            total = total + kernel_pair[:, row_lag, key_lag][:, None, None] * window
    valid = key_pos <= query_pos[rim:]
    filled = jnp.where(valid, total, -1e30)
    top = jnp.max(filled, axis=-1, keepdims=True)
    expon = jnp.where(valid, jnp.exp(filled - top), 0.0)
    probs = expon / jnp.sum(expon, axis=-1, keepdims=True)
    return (
        mixing_pair[:, 0][:, None, None] * probs[0][None]
        + mixing_pair[:, 1][:, None, None] * probs[1][None]
    )


def per_device(
    inputs,
    output_grad,
    source_tags,
    source_counts,
    gain_in,
    w_query,
    w_key,
    w_value,
    kernel,
    mixing,
    gain_head,
    w_out,
    gain_mid,
    w_gate,
    w_up,
    w_down,
):
    seq_group = inputs.shape[0]
    seg_rows = inputs.shape[1]
    width = inputs.shape[2]
    tok_rows = seq_group * seg_rows
    seq_parts = lax.axis_size("seq")
    position = lax.axis_index("seq")
    first_row = position * seg_rows
    seq_span = seg_rows * seq_parts
    rim_rows = QUERY_TAPS - 1
    score_scale = 1.0 / math.sqrt(DH)
    groups = H // 2
    pair_width = 2 * DH
    loop_count = seq_group * groups
    attn_full = (
        lax.all_gather(w_query, ("batch", "seq"), axis=0, tiled=True),
        lax.all_gather(w_key, ("batch", "seq"), axis=0, tiled=True),
        lax.all_gather(w_value, ("batch", "seq"), axis=0, tiled=True),
        lax.all_gather(w_out, ("batch", "seq"), axis=0, tiled=True),
        lax.all_gather(gain_in, ("batch", "seq"), axis=0, tiled=True),
        lax.all_gather(gain_head, ("batch", "seq"), axis=0, tiled=True),
        lax.all_gather(gain_mid, ("batch", "seq"), axis=0, tiled=True),
    )
    full_query, full_key, full_value, full_out, full_gain_in, full_gain_head, full_gain_mid = (
        attn_full
    )
    gain_in32 = full_gain_in.astype(jnp.float32)
    gain_head32 = full_gain_head.astype(jnp.float32)
    gain_mid32 = full_gain_mid.astype(jnp.float32)
    inputs32 = inputs.reshape(tok_rows, width).astype(jnp.float32)
    normed = rms_scale(inputs32, gain_in32).astype(jnp.bfloat16)
    queries = project(normed, full_query).astype(jnp.bfloat16).reshape(seq_group, seg_rows, width)
    keys_here = project(normed, full_key).astype(jnp.bfloat16).reshape(seq_group, seg_rows, width)
    values_here = (
        project(normed, full_value).astype(jnp.bfloat16).reshape(seq_group, seg_rows, width)
    )
    below_index = jnp.maximum(position - 1, 0)
    keys_all, values_all, tails = (
        lax.all_gather(keys_here, "seq", axis=1, tiled=True),
        lax.all_gather(values_here, "seq", axis=1, tiled=True),
        lax.all_gather(queries[:, seg_rows - rim_rows :], "seq", axis=1, tiled=True),
    )
    before = lax.dynamic_slice_in_dim(tails, below_index * rim_rows, rim_rows, 1)
    before = jnp.where(position > 0, before, jnp.zeros_like(before))
    query_ext = jnp.concatenate([before, queries], axis=1)

    def group_slices(loop_index):
        seq_index = loop_index // groups
        group_index = loop_index % groups
        start = group_index * pair_width
        query_group = lax.dynamic_slice(
            query_ext, (seq_index, 0, start), (1, seg_rows + rim_rows, pair_width)
        ).reshape(seg_rows + rim_rows, 2, DH)
        key_group = lax.dynamic_slice(
            keys_all, (seq_index, 0, start), (1, seq_span, pair_width)
        ).reshape(seq_span, 2, DH)
        value_group = lax.dynamic_slice(
            values_all, (seq_index, 0, start), (1, seq_span, pair_width)
        ).reshape(seq_span, 2, DH)
        kernel_pair = lax.dynamic_slice_in_dim(kernel, group_index * 2, 2, 0)
        mixing_pair = lax.dynamic_slice_in_dim(mixing, group_index * 2, 2, 0)
        return (
            seq_index,
            group_index,
            start,
            query_group,
            key_group,
            value_group,
            kernel_pair,
            mixing_pair,
        )

    def group_forward(loop_index, heads_out):
        (
            seq_index,
            group_index,
            start,
            query_group,
            key_group,
            value_group,
            kernel_pair,
            mixing_pair,
        ) = group_slices(loop_index)
        raw_scores = (
            jnp.einsum("qhd,khd->hqk", query_group, key_group, preferred_element_type=jnp.float32)
            * score_scale
        )
        mixed = mixed_probs(raw_scores, kernel_pair, mixing_pair, first_row).astype(jnp.bfloat16)
        head_values = jnp.einsum(
            "hqk,khd->qhd", mixed, value_group, preferred_element_type=jnp.float32
        )
        return lax.dynamic_update_slice(
            heads_out, head_values.reshape(1, seg_rows, pair_width), (seq_index, 0, start)
        )

    heads = lax.fori_loop(
        0, loop_count, group_forward, jnp.zeros((seq_group, seg_rows, width), jnp.float32)
    ).reshape(tok_rows, width)
    joined = head_norm(heads, gain_head32).astype(jnp.bfloat16)
    middle = inputs32 + project(joined, full_out)
    normed_mid = rms_scale(middle, gain_mid32).astype(jnp.bfloat16)
    source_ids = jnp.arange(source_counts.shape[0], dtype=jnp.int32)
    tag_count = jnp.sum(
        jnp.where(source_tags[:, None] == source_ids[None, :], source_counts[None, :], 0), axis=1
    )
    seq_factor = seq_span / tag_count.astype(jnp.float32)
    cotangent = (output_grad.astype(jnp.float32) * seq_factor[:, None, None]).reshape(
        tok_rows, width
    )
    down_in = cotangent.astype(jnp.bfloat16)
    gate_part, up_part, down_part = (
        lax.all_gather(w_gate, "batch", axis=0, tiled=True),
        lax.all_gather(w_up, "batch", axis=0, tiled=True),
        lax.all_gather(w_down, "batch", axis=1, tiled=True),
    )
    full_gate, full_up, full_down = (
        lax.all_gather(gate_part, "seq", axis=1, tiled=True),
        lax.all_gather(up_part, "seq", axis=1, tiled=True),
        lax.all_gather(down_part, "seq", axis=0, tiled=True),
    )
    gate = project(normed_mid, full_gate)
    upward = project(normed_mid, full_up)
    hidden = swiglu(gate, upward).astype(jnp.bfloat16)
    result = middle + project(hidden, full_down)
    whole_down = project_tn(hidden, down_in)
    hidden_grad = project_nt(down_in, full_down)
    gate_raw, up_raw = jax.vjp(swiglu, gate, upward)[1](hidden_grad)
    gate_grad = gate_raw.astype(jnp.bfloat16)
    up_grad = up_raw.astype(jnp.bfloat16)
    whole_gate = project_tn(normed_mid, gate_grad)
    whole_up = project_tn(normed_mid, up_grad)
    mid_grad_n = project_nt(gate_grad, full_gate) + project_nt(up_grad, full_up)
    grad_gate, grad_up, grad_down = (
        lax.psum_scatter(
            whole_gate.astype(jnp.bfloat16), "seq", scatter_dimension=1, tiled=True
        ).astype(jnp.float32),
        lax.psum_scatter(
            whole_up.astype(jnp.bfloat16), "seq", scatter_dimension=1, tiled=True
        ).astype(jnp.float32),
        lax.psum_scatter(
            whole_down.astype(jnp.bfloat16), "seq", scatter_dimension=0, tiled=True
        ).astype(jnp.float32),
    )
    output = result.astype(jnp.bfloat16)
    ffn_sums = (
        lax.psum_scatter(
            grad_gate.astype(jnp.bfloat16), "batch", scatter_dimension=0, tiled=True
        ).astype(jnp.float32),
        lax.psum_scatter(
            grad_up.astype(jnp.bfloat16), "batch", scatter_dimension=0, tiled=True
        ).astype(jnp.float32),
        lax.psum_scatter(
            grad_down.astype(jnp.bfloat16), "batch", scatter_dimension=1, tiled=True
        ).astype(jnp.float32),
    )
    middle_norm_grad, gain_mid_term = jax.vjp(rms_scale, middle, gain_mid32)[1](mid_grad_n)
    middle_grad = cotangent + middle_norm_grad
    attn_in = middle_grad.astype(jnp.bfloat16)
    grad_out = project_tn(joined, attn_in)
    joined_grad = project_nt(attn_in, full_out)
    heads_raw, gain_head_term = jax.vjp(head_norm, heads, gain_head32)[1](joined_grad)
    heads_grad = heads_raw.astype(jnp.bfloat16).reshape(seq_group, seg_rows, width)

    def group_backward(loop_index, carry):
        query_grad, key_grad, value_grad, kernel_grad, mixing_grad = carry
        (
            seq_index,
            group_index,
            start,
            query_group,
            key_group,
            value_group,
            kernel_pair,
            mixing_pair,
        ) = group_slices(loop_index)
        raw_scores = (
            jnp.einsum("qhd,khd->hqk", query_group, key_group, preferred_element_type=jnp.float32)
            * score_scale
        )

        def local_probs(raw_in, kernel_in, mixing_in):
            return mixed_probs(raw_in, kernel_in, mixing_in, first_row)

        mixed_full, probs_back = jax.vjp(local_probs, raw_scores, kernel_pair, mixing_pair)
        mixed = mixed_full.astype(jnp.bfloat16)
        head_grad_group = lax.dynamic_slice(
            heads_grad, (seq_index, 0, start), (1, seg_rows, pair_width)
        ).reshape(seg_rows, 2, DH)
        mixed_grad = jnp.einsum(
            "qhd,khd->hqk", head_grad_group, value_group, preferred_element_type=jnp.float32
        )
        value_part = jnp.einsum(
            "hqk,qhd->khd", mixed, head_grad_group, preferred_element_type=jnp.float32
        )
        raw_grad_full, kernel_part, mixing_part = probs_back(mixed_grad)
        raw_grad = raw_grad_full.astype(jnp.bfloat16)
        query_part = (
            jnp.einsum("hqk,khd->qhd", raw_grad, key_group, preferred_element_type=jnp.float32)
            * score_scale
        )
        key_part = (
            jnp.einsum("hqk,qhd->khd", raw_grad, query_group, preferred_element_type=jnp.float32)
            * score_scale
        )
        query_grad = lax.dynamic_update_slice(
            query_grad,
            query_part.reshape(1, seg_rows + rim_rows, pair_width),
            (seq_index, 0, start),
        )
        key_grad = lax.dynamic_update_slice(
            key_grad, key_part.reshape(1, seq_span, pair_width), (seq_index, 0, start)
        )
        value_grad = lax.dynamic_update_slice(
            value_grad, value_part.reshape(1, seq_span, pair_width), (seq_index, 0, start)
        )
        kernel_prior = lax.dynamic_slice_in_dim(kernel_grad, group_index * 2, 2, 0)
        mixing_prior = lax.dynamic_slice_in_dim(mixing_grad, group_index * 2, 2, 0)
        kernel_grad = lax.dynamic_update_slice_in_dim(
            kernel_grad, kernel_prior + kernel_part, group_index * 2, 0
        )
        mixing_grad = lax.dynamic_update_slice_in_dim(
            mixing_grad, mixing_prior + mixing_part, group_index * 2, 0
        )
        return (query_grad, key_grad, value_grad, kernel_grad, mixing_grad)

    start_carry = (
        jnp.zeros((seq_group, seg_rows + rim_rows, width), jnp.float32),
        jnp.zeros((seq_group, seq_span, width), jnp.float32),
        jnp.zeros((seq_group, seq_span, width), jnp.float32),
        jnp.zeros(kernel.shape, jnp.float32),
        jnp.zeros(mixing.shape, jnp.float32),
    )
    query_grad, key_grad, value_grad, kernel_grad, mixing_grad = lax.fori_loop(
        0, loop_count, group_backward, start_carry
    )
    own_rim = jnp.where(position > 0, query_grad[:, :rim_rows], 0.0)
    slot_rows = lax.dynamic_update_slice_in_dim(
        jnp.zeros((seq_group, seq_parts * rim_rows, width), jnp.float32),
        own_rim,
        below_index * rim_rows,
        1,
    )
    key_sum, value_sum, rim_back = (
        lax.psum_scatter(
            key_grad.astype(jnp.bfloat16), "seq", scatter_dimension=1, tiled=True
        ).astype(jnp.float32),
        lax.psum_scatter(
            value_grad.astype(jnp.bfloat16), "seq", scatter_dimension=1, tiled=True
        ).astype(jnp.float32),
        lax.psum_scatter(
            slot_rows.astype(jnp.bfloat16), "seq", scatter_dimension=1, tiled=True
        ).astype(jnp.float32),
    )
    query_total = query_grad[:, rim_rows:] + jnp.pad(
        rim_back, ((0, 0), (seg_rows - rim_rows, 0), (0, 0))
    )
    queries_grad = query_total.astype(jnp.bfloat16).reshape(tok_rows, width)
    keys_grad = key_sum.astype(jnp.bfloat16).reshape(tok_rows, width)
    values_grad = value_sum.astype(jnp.bfloat16).reshape(tok_rows, width)
    grad_query = project_tn(normed, queries_grad)
    grad_key = project_tn(normed, keys_grad)
    grad_value = project_tn(normed, values_grad)
    normed_grad = (
        project_nt(queries_grad, full_query)
        + project_nt(keys_grad, full_key)
        + project_nt(values_grad, full_value)
    )
    input_norm_grad, gain_in_term = jax.vjp(rms_scale, inputs32, gain_in32)[1](normed_grad)
    input_grad = (
        (middle_grad + input_norm_grad).astype(jnp.bfloat16).reshape(seq_group, seg_rows, width)
    )
    attn_sums = (
        lax.psum_scatter(grad_query, ("batch", "seq"), scatter_dimension=0, tiled=True),
        lax.psum_scatter(grad_key, ("batch", "seq"), scatter_dimension=0, tiled=True),
        lax.psum_scatter(grad_value, ("batch", "seq"), scatter_dimension=0, tiled=True),
        lax.psum_scatter(grad_out, ("batch", "seq"), scatter_dimension=0, tiled=True),
        lax.psum_scatter(gain_in_term, ("batch", "seq"), scatter_dimension=0, tiled=True),
        lax.psum_scatter(gain_head_term, ("batch", "seq"), scatter_dimension=0, tiled=True),
        lax.psum_scatter(gain_mid_term, ("batch", "seq"), scatter_dimension=0, tiled=True),
    )
    kernel_sum, mixing_sum = lax.psum((kernel_grad, mixing_grad), ("batch", "seq"))
    output = output.reshape(seq_group, seg_rows, width)
    return (
        output,
        input_grad,
        attn_sums[4],
        attn_sums[0],
        attn_sums[1],
        attn_sums[2],
        kernel_sum,
        mixing_sum,
        attn_sums[5],
        attn_sums[3],
        attn_sums[6],
        ffn_sums[0],
        ffn_sums[1],
        ffn_sums[2],
    )


def solution(mesh):
    in_specs = (
        P("batch", "seq", None),
        P("batch", "seq", None),
        P("batch"),
        P(),
        P(("batch", "seq")),
        P(("batch", "seq"), None),
        P(("batch", "seq"), None),
        P(("batch", "seq"), None),
        P(),
        P(),
        P(("batch", "seq")),
        P(("batch", "seq"), None),
        P(("batch", "seq")),
        P("batch", "seq"),
        P("batch", "seq"),
        P("seq", "batch"),
    )
    out_specs = (
        P("batch", "seq", None),
        P("batch", "seq", None),
        P(("batch", "seq")),
        P(("batch", "seq"), None),
        P(("batch", "seq"), None),
        P(("batch", "seq"), None),
        P(),
        P(),
        P(("batch", "seq")),
        P(("batch", "seq"), None),
        P(("batch", "seq")),
        P("batch", "seq"),
        P("batch", "seq"),
        P("seq", "batch"),
    )
    return jax.shard_map(
        per_device, mesh=mesh, in_specs=in_specs, out_specs=out_specs, check_vma=False
    )
```

profile of v0, /device:TPU:0, one launch (start us, length us, event | category | flops | bytes accessed | tf_op | source)
XLA Modules:
  0.0 3110.3 jit_solution(10391139723678051745)
XLA Ops:
  12.0 42.2 %all-reduce.147 = (bf16[1536]{0:T(1024)(128)(2,1)S(1)}, bf16[1536]{0:T(1024)(128)(2,1)S(1)}, bf16[1536]{0:T(1024)(128)(2,1)S(1)}) all-reduce(bf16[1536]{0:T(1024)(128)(2,1)S(1)} %dynamic-update-slice, bf16[1536]{0:T(1024)(128)(2,1)S(1)} %dynamic-update-slice.1, ...), channel_id=1, replica_groups=mesh['batch'=8,'seq'=4] {'batch','seq'}, use_global_device_ids=true, to_apply=%add.139 | all-reduce | flops 4608 | bytes 18432
  55.8 21.3 all-gather.13.cloned.1.call-done
  82.1 59.8 %all-gather.19.cloned.1.call-done = bf16[1536,1536]{1,0:T(8,128)(2,1)} async-done(((bf16[48,1536]{1,0:T(8,128)(2,1)}), bf16[1536,1536]{1,0:T(8,128)(2,1)}) %all-gather.19.cloned.1.call-update) | async-done | bytes 4718608 | tf_op jit(solution)/shard_map/all_gather | solution.py:108
  147.6 26.7 all-gather.25.cloned.1.call-done
  174.4 33.9 %all-gather.29.cloned.1.call-done = bf16[1536,1024]{1,0:T(8,128)(2,1)} async-done(((bf16[192,1024]{1,0:T(8,128)(2,1)}), bf16[1536,1024]{1,0:T(8,128)(2,1)}) %all-gather.29.cloned.1.call-update) | async-done | bytes 3145744 | tf_op jit(solution)/shard_map/all_gather | solution.py:204
  210.9 31.3 %all-gather.33.cloned.1.call-done = bf16[1024,1536]{0,1:T(8,128)(2,1)} async-done(((bf16[1024,192]{0,1:T(8,128)(2,1)}), bf16[1024,1536]{0,1:T(8,128)(2,1)}) %all-gather.33.cloned.1.call-update) | async-done | bytes 3145744 | tf_op jit(solution)/shard_map/all_gather | solution.py:205
  242.3 66.2 %all-gather.17.cloned.1.call-done = bf16[1536,1536]{1,0:T(8,128)(2,1)} async-done(((bf16[48,1536]{1,0:T(8,128)(2,1)}), bf16[1536,1536]{1,0:T(8,128)(2,1)}) %all-gather.17.cloned.1.call-update) | async-done | bytes 4718608 | tf_op jit(solution)/shard_map/all_gather | solution.py:107
  327.8 47.2 %all-gather.15.cloned.1.call-done = bf16[2,512,1536]{1,2,0:T(8,128)(2,1)} async-done(((bf16[2,128,1536]{1,2,0:T(8,128)(2,1)}), bf16[2,512,1536]{1,2,0:T(8,128)(2,1)}) %all-gather.15.cloned.1.call-update) | async-done | bytes 3145744 | tf_op jit(solution)/shard_map/all_gather | solution.py:131
  375.0 61.9 %all-gather.21.cloned.1.call-done = bf16[2,512,1536]{1,2,0:T(8,128)(2,1)} async-done(((bf16[2,128,1536]{1,2,0:T(8,128)(2,1)}), bf16[2,512,1536]{1,2,0:T(8,128)(2,1)}) %all-gather.21.cloned.1.call-update) | async-done | bytes 3145744 | tf_op jit(solution)/shard_map/all_gather | solution.py:130
  438.2 391.5 %while.38 = (s32[]{:T(128)}, f32[2,128,1536]{1,2,0:T(8,128)}, bf16[2,512,1536]{1,2,0:T(8,128)(2,1)}, f32[16,2]{0,1:T(2,128)S(1)}, s32[]{:T(128)}, /*index=5*/f32...) while((s32[]{:T(128)}, f32[2,128,1536]{1,2,0:T(8,128)}, ...), condition=%wide.region_4.5_spmd, body=%wide.region_1.4_spmd.sunk | while | flops 70071704 | bytes 9495758 | solution.py:187
  454.9 19.5 fusion.305
  478.5 19.5 fusion.305
  502.1 19.5 fusion.305
  525.7 19.5 fusion.305
  549.3 19.5 fusion.305
  572.8 19.5 fusion.305
  596.4 19.5 fusion.305
  643.5 19.5 fusion.305
  667.1 19.5 fusion.305
  690.7 19.5 fusion.305
  869.3 68.2 %all-gather.31.cloned.1.call-done = bf16[1536,4096]{1,0:T(8,128)(2,1)} async-done(((bf16[1536,1024]{1,0:T(8,128)(2,1)}), bf16[1536,4096]{1,0:T(8,128)(2,1)}) %all-gather.31.cloned.1.call-update) | async-done | bytes 12582928 | tf_op jit(solution)/shard_map/all_gather | solution.py:209
  947.0 208.3 %all-gather.35.cloned.1.call-done = bf16[4096,1536]{0,1:T(8,128)(2,1)} async-done(((bf16[1024,1536]{0,1:T(8,128)(2,1)}), bf16[4096,1536]{0,1:T(8,128)(2,1)}) %all-gather.35.cloned.1.call-update) | async-done | bytes 12582928 | tf_op jit(solution)/shard_map/all_gather | solution.py:210
  1240.5 985.1 %while.39 = (s32[]{:T(128)}, f32[2,133,1536]{2,1,0:T(8,128)}, bf16[2,512,1536]{1,2,0:T(8,128)(2,1)}, bf16[2,512,1536]{1,2,0:T(8,128)(2,1)}, f32[16,6,11]{0,1,2:T...) while((s32[]{:T(128)}, f32[2,133,1536]{2,1,0:T(8,128)}, ...), condition=%wide.region_88.89_spmd, body=%wide.region_12.88_spmd.sunk | while | flops 186800608 | bytes 105276824 | solution.py:324
  2269.9 54.9 %reduce-scatter.15.cloned.1.call-done = bf16[2,128,1536]{2,1,0:T(8,128)(2,1)} async-done(((bf16[2,512,1536]{2,1,0:T(8,128)(2,1)}), bf16[2,128,1536]{2,1,0:T(8,128)(2,1)}) %reduce-scatter.15.cloned.1.call-update) | async-done | bytes 786448 | tf_op jit(solution)/shard_map/reduce_scatter | solution.py:335
  2331.3 56.0 %reduce-scatter.17.cloned.1.call-done = bf16[2,128,1536]{2,1,0:T(8,128)(2,1)} async-done(((bf16[2,512,1536]{2,1,0:T(8,128)(2,1)}), bf16[2,128,1536]{2,1,0:T(8,128)(2,1)}) %reduce-scatter.17.cloned.1.call-update) | async-done | bytes 786448 | tf_op jit(solution)/shard_map/reduce_scatter | solution.py:338
  2415.1 42.0 %all-reduce.146 = (f32[1536]{0:T(1024)S(1)}, f32[16,6,11]{0,1,2:T(8,128)}, f32[16,2]{0,1:T(2,128)}, f32[1536]{0:T(1024)S(1)}, f32[1536]{0:T(1024)S(1)}) all-reduce(f32[1536]{0:T(1024)S(1)} %get-tuple-element.791, f32[16,6,11]{0,1,2:T(8,128)S(1)} %copy-done.26, ...), channel_id=5, replica_groups=mesh['batch'=8,'seq'=4] {'batch','seq'}, use_global_device_ids=true, to_apply=%region_94.95.clone | all-reduce | flops 5696 | bytes 45568
  2463.9 22.5 reduce-scatter.29.cloned.1.call-done
  2488.4 47.5 %reduce-scatter.33.cloned.1.call-done = bf16[192,1024]{1,0:T(8,128)(2,1)} async-done(((bf16[1536,1024]{1,0:T(8,128)(2,1)}), bf16[192,1024]{1,0:T(8,128)(2,1)}) %reduce-scatter.33.cloned.1.call-update) | async-done | bytes 393232 | tf_op jit(solution)/shard_map/reduce_scatter | solution.py:240
  2537.9 141.0 %reduce-scatter.25.cloned.1.call-done = f32[48,1536]{1,0:T(8,128)} async-done(((f32[1536,1536]{1,0:T(8,128)}), f32[48,1536]{1,0:T(8,128)}) %reduce-scatter.25.cloned.1.call-update) | async-done | bytes 294928 | tf_op jit(solution)/shard_map/reduce_scatter | solution.py:367
  2678.9 141.6 %reduce-scatter.19.cloned.1.call-done = f32[48,1536]{1,0:T(8,128)} async-done(((f32[1536,1536]{1,0:T(8,128)}), f32[48,1536]{1,0:T(8,128)}) %reduce-scatter.19.cloned.1.call-update) | async-done | bytes 294928 | tf_op jit(solution)/shard_map/reduce_scatter | solution.py:364
  2820.5 141.5 %reduce-scatter.21.cloned.1.call-done = f32[48,1536]{1,0:T(8,128)} async-done(((f32[1536,1536]{1,0:T(8,128)}), f32[48,1536]{1,0:T(8,128)}) %reduce-scatter.21.cloned.1.call-update) | async-done | bytes 294928 | tf_op jit(solution)/shard_map/reduce_scatter | solution.py:365
  2962.0 141.6 %reduce-scatter.23.cloned.1.call-done = f32[48,1536]{1,0:T(8,128)} async-done(((f32[1536,1536]{1,0:T(8,128)}), f32[48,1536]{1,0:T(8,128)}) %reduce-scatter.23.cloned.1.call-update) | async-done | bytes 294928 | tf_op jit(solution)/shard_map/reduce_scatter | solution.py:366
  (2188 shorter events, 1402.2 us)
Async XLA Ops:
  7.2 47.0 %copy-start = (bf16[2,128,1536]{2,1,0:T(8,128)(2,1)S(1)}, bf16[2,128,1536]{2,1,0:T(8,128)(2,1)}, u32[]{:S(2)}) copy-start(bf16[2,128,1536]{2,1,0:T(8,128)(2,1)} %param.20) | copy-start | bytes 2359300
  7.2 69.9 %all-gather.13.cloned.1.call-start = ((), (), s32[]{:S(2)}) async-start(), calls=%async_computation.12 | async-start | bytes 4866048 | tf_op jit(solution)/shard_map/all_gather | solution.py:109
  8.0 133.9 %all-gather.19.cloned.1.call-start = ((), (), s32[]{:S(2)}) async-start(), calls=%async_computation.15 | async-start | bytes 4866048 | tf_op jit(solution)/shard_map/all_gather | solution.py:108
  8.7 165.6 %all-gather.25.cloned.1.call-start = ((), (), s32[]{:S(2)}) async-start(), calls=%async_computation.18 | async-start | bytes 3538944 | tf_op jit(solution)/shard_map/all_gather | solution.py:203
  9.4 198.8 %all-gather.29.cloned.1.call-start = ((), (), s32[]{:S(2)}) async-start(), calls=%async_computation.20 | async-start | bytes 3538944 | tf_op jit(solution)/shard_map/all_gather | solution.py:204
  10.0 232.2 %all-gather.33.cloned.1.call-start = ((), (), s32[]{:S(2)}) async-start(), calls=%async_computation.22 | async-start | bytes 3538944 | tf_op jit(solution)/shard_map/all_gather | solution.py:205
  10.6 297.9 %all-gather.17.cloned.1.call-start = ((), (), s32[]{:S(2)}) async-start(), calls=%async_computation.14 | async-start | bytes 4866048 | tf_op jit(solution)/shard_map/all_gather | solution.py:107
  11.2 363.8 %all-gather.15.cloned.1.call-start = ((), (), s32[]{:S(2)}) async-start(), calls=%async_computation.13 | async-start | bytes 3932160 | tf_op jit(solution)/shard_map/all_gather | solution.py:131
  82.1 354.9 %all-gather.21.cloned.1.call-start = ((), (), s32[]{:S(2)}) async-start(), calls=%async_computation.16 | async-start | bytes 3932160 | tf_op jit(solution)/shard_map/all_gather | solution.py:130
  146.8 706.9 %all-gather.23.cloned.1.call-start = ((), (), s32[]{:S(2)}) async-start(), calls=%async_computation.17 | async-start | bytes 4866048 | tf_op jit(solution)/shard_map/all_gather | solution.py:110
  147.5 711.9 %all-gather.27.cloned.1.call-start = ((), (), s32[]{:S(2)}) async-start(), calls=%async_computation.19 | async-start | bytes 15728640 | tf_op jit(solution)/shard_map/all_gather | solution.py:208
  174.3 763.2 %all-gather.31.cloned.1.call-start = ((), (), s32[]{:S(2)}) async-start(), calls=%async_computation.21 | async-start | bytes 15728640 | tf_op jit(solution)/shard_map/all_gather | solution.py:209
  208.3 947.1 %all-gather.35.cloned.1.call-start = ((), (), s32[]{:S(2)}) async-start(), calls=%async_computation.23 | async-start | bytes 15728640 | tf_op jit(solution)/shard_map/all_gather | solution.py:210
  209.1 997.3 %copy-start.35 = (f32[1536]{0:T(1024)}, f32[1536]{0:T(1024)S(1)}, u32[]{:S(2)}) copy-start(f32[1536]{0:T(1024)S(1)} %convert_element_type.185) | copy-start | bytes 18436
  242.2 1996.4 %reduce-scatter.35.cloned.1.call-start = ((), (), s32[]{:S(2)}) async-start(), calls=%async_computation.34 | async-start | bytes 15728640 | tf_op jit(solution)/shard_map/reduce_scatter | solution.py:231
  326.7 111.5 %copy-start.37 = (f32[16,2]{0,1:T(2,128)S(1)}, f32[16,2]{0,1:T(2,128)}, u32[]{:S(2)}) copy-start(f32[16,2]{0,1:T(2,128)} %param.29) | copy-start | bytes 388
  859.4 317.5 %copy-start.17 = (bf16[256,1536]{1,0:T(8,128)(2,1)}, bf16[256,1536]{1,0:T(8,128)(2,1)S(1)}, u32[]{:S(2)}) copy-start(bf16[256,1536]{1,0:T(8,128)(2,1)S(1)} %multiply_convert_fusion.2) | copy-start | bytes 2359300
  1176.8 1066.6 %reduce-scatter.27.cloned.1.call-start = ((), (), s32[]{:S(2)}) async-start(), calls=%async_computation.30 | async-start | bytes 15728640 | tf_op jit(solution)/shard_map/reduce_scatter | solution.py:225
  1185.4 1058.6 %reduce-scatter.31.cloned.1.call-start = ((), (), s32[]{:S(2)}) async-start(), calls=%async_computation.32 | async-start | bytes 15728640 | tf_op jit(solution)/shard_map/reduce_scatter | solution.py:228
  1185.8 20.6 slice-start
  1234.0 1028.2 %all-reduce.150.cloned.1.call-start = ((), (), s32[]{:S(2)}) async-start(), calls=%async_computation.36 | async-start | bytes 245760
  1284.9 17.1 copy-start.8
  1405.3 16.7 copy-start.8
  2229.0 95.7 %reduce-scatter.15.cloned.1.call-start = ((), (), s32[]{:S(2)}) async-start(), calls=%async_computation.24 | async-start | bytes 3932160 | tf_op jit(solution)/shard_map/reduce_scatter | solution.py:335
  2233.8 153.5 %reduce-scatter.17.cloned.1.call-start = ((), (), s32[]{:S(2)}) async-start(), calls=%async_computation.25 | async-start | bytes 3932160 | tf_op jit(solution)/shard_map/reduce_scatter | solution.py:338
  2238.6 222.9 %reduce-scatter.37.cloned.1.call-start = ((), (), s32[]{:S(2)}) async-start(), calls=%async_computation.35 | async-start | bytes 3538944
  2243.3 243.1 %reduce-scatter.29.cloned.1.call-start = ((), (), s32[]{:S(2)}) async-start(), calls=%async_computation.31 | async-start | bytes 3538944 | tf_op jit(solution)/shard_map/reduce_scatter | solution.py:237
  2243.9 292.0 %reduce-scatter.33.cloned.1.call-start = ((), (), s32[]{:S(2)}) async-start(), calls=%async_computation.33 | async-start | bytes 3538944 | tf_op jit(solution)/shard_map/reduce_scatter | solution.py:240
  2244.7 434.2 %reduce-scatter.25.cloned.1.call-start = ((), (), s32[]{:S(2)}) async-start(), calls=%async_computation.29 | async-start | bytes 9732096 | tf_op jit(solution)/shard_map/reduce_scatter | solution.py:367
  2251.9 568.5 %reduce-scatter.19.cloned.1.call-start = ((), (), s32[]{:S(2)}) async-start(), calls=%async_computation.26 | async-start | bytes 9732096 | tf_op jit(solution)/shard_map/reduce_scatter | solution.py:364
  2269.8 692.1 %reduce-scatter.21.cloned.1.call-start = ((), (), s32[]{:S(2)}) async-start(), calls=%async_computation.27 | async-start | bytes 9732096 | tf_op jit(solution)/shard_map/reduce_scatter | solution.py:365
  2331.1 772.5 %reduce-scatter.23.cloned.1.call-start = ((), (), s32[]{:S(2)}) async-start(), calls=%async_computation.28 | async-start | bytes 9732096 | tf_op jit(solution)/shard_map/reduce_scatter | solution.py:366
  (517 other events, 2726.8 us)
Sparse Core Ops, SparseCore 0:
  10.8 66.2 all-gather.12
  80.0 61.8 all-gather.18
  143.8 30.4 all-gather.24
  176.0 32.1 all-gather.28
  210.0 32.1 all-gather.32
  244.9 63.5 all-gather.16
  310.6 64.3 all-gather.14
  377.2 59.7 all-gather.20
  439.8 61.7 all-gather.22
  503.0 216.4 all-gather.26
  721.1 216.3 all-gather.30
  939.0 216.3 all-gather.34
  1177.0 210.0 reduce-scatter.34
  1389.3 212.8 reduce-scatter.26
  1604.4 212.9 reduce-scatter.30
  2229.2 32.9 all-reduce.149
  2264.4 60.3 reduce-scatter.14
  2326.9 60.3 reduce-scatter.16
  2390.7 46.4 reduce-scatter.36
  2440.4 45.9 reduce-scatter.28
  2489.8 46.0 reduce-scatter.32
  2542.4 136.4 reduce-scatter.24
  2685.4 135.0 reduce-scatter.18
  2826.8 135.1 reduce-scatter.20
  2968.4 135.0 reduce-scatter.22
where the time goes:
time: 3120 us; the launch traced here: 3110 us
  waiting for transfers between devices  1390 us (45%)
  other arithmetic  1120 us (36%)
  local copies, waits for them, and re-layouts  269 us (9%)
  matrix products  181 us (6%)
  blocking collectives  98.5 us (3%)
  loops' own time  42 us (1%)
    sub x16, other arithmetic, mixed_probs(): expon = jnp.where(valid, jnp.exp(filled - top), 0.0)  312 us
    add_any x16, other arithmetic, mixed_probs(): padded[:, rim - row_lag:rim - row_lag + row_count, 2 * reach - key_lag:2...  266 us
    all_gather x1, waiting for transfers between devices, per_device(): lax.all_gather(down_part, 'seq', axis=0, tiled=True)  208 us
    mul x64, other arithmetic, mixed_probs(): total = total + kernel_pair[:, row_lag, key_lag][:, None, None] * window  169 us
    reduce_sum x64, other arithmetic, mixed_probs(): total = total + kernel_pair[:, row_lag, key_lag][:, None, None] * window  160 us
    reduce_scatter x1, waiting for transfers between devices, per_device(): lax.psum_scatter(grad_value, ('batch', 'seq'), scatter_dimension=0, tiled...  142 us
    reduce_scatter x1, waiting for transfers between devices, per_device(): lax.psum_scatter(grad_query, ('batch', 'seq'), scatter_dimension=0, tiled...  142 us
    reduce_scatter x1, waiting for transfers between devices, per_device(): lax.psum_scatter(grad_key, ('batch', 'seq'), scatter_dimension=0, tiled=T...  141 us
  transfers between devices with their start and end apart: 25, of which 19 were waited for; matrix products, arithmetic and copies ran while one was open for 49% of the time, Pallas kernels for 0%

commit v1 on v0

v1 whole, which is shorter than its diff:
```python
import math

import jax
import jax.numpy as jnp
from jax import lax
from jax.experimental import pallas as pl
from jax.experimental.pallas import tpu as pltpu
from jax.sharding import PartitionSpec as P

H = 16
DH = 96
QT = 6
KT = 11
REACH = KT // 2
TILE = 128
PAIR = 256
PAD = 16
bf16 = jnp.bfloat16
f32 = jnp.float32


def nn(a, b):
    return lax.dot_general(a, b, (((1,), (0,)), ((), ())), preferred_element_type=f32)


def nt(a, b):
    return lax.dot_general(a, b, (((1,), (1,)), ((), ())), preferred_element_type=f32)


def tn(a, b):
    return lax.dot_general(a, b, (((0,), (0,)), ((), ())), preferred_element_type=f32)


def head_lanes(head, width=PAIR):
    lane = lax.broadcasted_iota(jnp.int32, (1, width), 1)
    return jnp.logical_and(lane >= head * DH, lane < (head + 1) * DH).astype(f32)


def split(value):
    high = value.astype(bf16)
    return high, (value - high.astype(f32)).astype(bf16)


def fill_bands(kern_ref, base, bands, low_bands, offset):
    row = lax.broadcasted_iota(jnp.int32, (2 * TILE, TILE), 0)
    col = lax.broadcasted_iota(jnp.int32, (2 * TILE, TILE), 1)
    tap = offset(row, col)
    for lag in range(QT):
        band = jnp.zeros((2 * TILE, TILE), f32)
        for key_lag in range(KT):
            band = jnp.where(tap == key_lag, kern_ref[base + lag * KT + key_lag], band)
        high, low = split(band)
        bands[:, lag * TILE : (lag + 1) * TILE] = high
        if low_bands is not None:
            low_bands[:, lag * TILE : (lag + 1) * TILE] = low


def valid_keys(first_query, rows, first_key):
    query = lax.broadcasted_iota(jnp.int32, (rows, TILE), 0) + first_query
    key = lax.broadcasted_iota(jnp.int32, (rows, TILE), 1) + (first_key - REACH)
    return jnp.logical_and(key >= 0, key <= query)


def shift_keys(keys, kx_ref):
    moved = jnp.concatenate([keys.astype(f32), jnp.zeros((TILE, PAIR), f32)], axis=0)
    kx_ref[...] = pltpu.roll(moved, REACH, 0).astype(bf16)


def norm_parts(heads):
    means = jnp.zeros_like(heads)
    masks = [head_lanes(0), head_lanes(1)]
    for mask in masks:
        means = means + mask * (jnp.sum(heads * mask, axis=1, keepdims=True) / DH)
    used = masks[0] + masks[1]
    centred = (heads - means) * used
    inverse = jnp.zeros_like(heads)
    for mask in masks:
        spread = jnp.sum(centred * centred * mask, axis=1, keepdims=True) / DH
        inverse = inverse + mask * lax.rsqrt(spread + 1e-05)
    return centred, inverse, masks


def attend_fwd_body(kern_ref, mix_ref, qkv_ref, gain_ref, joined_ref, heads_ref, p_ref, high_ref, low_ref, bands_ref, low_bands_ref, kx_ref):
    length = qkv_ref.shape[1]
    tiles = length // TILE
    scale = 1.0 / math.sqrt(DH)
    group = pl.program_id(0)

    @pl.when(jnp.logical_and(group == 0, pl.program_id(1) == 0))
    def _():
        high_ref[...] = jnp.zeros_like(high_ref)
        low_ref[...] = jnp.zeros_like(low_ref)

    shift_keys(qkv_ref[0, :, PAIR : 2 * PAIR], kx_ref)

    def one_head(head, carry):
        base = (group * 2 + head) * (QT * KT)
        fill_bands(kern_ref, base, bands_ref, low_bands_ref, lambda row, col: (KT - 1) - (row - col))
        lanes = head_lanes(head).astype(bf16)
        query = qkv_ref[0, :, :PAIR] * lanes
        for tile in range(tiles + 1):
            first = max(0, tile * TILE - PAD)
            scores = nt(query[first:], kx_ref[tile * TILE : (tile + 1) * TILE, :]) * scale
            masked = jnp.where(valid_keys(first, length - first, tile * TILE), scores, 0.0)
            high, low = split(masked)
            high_ref[first + PAD :, tile * TILE : (tile + 1) * TILE] = high
            low_ref[first + PAD :, tile * TILE : (tile + 1) * TILE] = low
        for tile in range(tiles):
            first = tile * TILE
            high = high_ref[first:, first : first + 2 * TILE]
            low = low_ref[first:, first : first + 2 * TILE]
            bands = bands_ref[...]
            wide = nn(high, bands) + nn(low, bands) + nn(high, low_bands_ref[...])
            total = wide[:, :TILE]
            for lag in range(1, QT):
                total = total + pltpu.roll(wide[:, lag * TILE : (lag + 1) * TILE], lag, 0)
            p_ref[0, 0, head, first:, first : first + TILE] = total[PAD:]
        return carry

    lax.fori_loop(0, 2, one_head, 0)
    for tile in range(tiles):
        first = tile * TILE
        span = first + TILE
        query = lax.broadcasted_iota(jnp.int32, (TILE, span), 0) + first
        key = lax.broadcasted_iota(jnp.int32, (TILE, span), 1)
        valid = key <= query
        probs = []
        for head in range(2):
            logits = jnp.where(valid, p_ref[0, 0, head, first:span, :span], -1e30)
            top = jnp.max(logits, axis=1, keepdims=True)
            expon = jnp.where(valid, jnp.exp(logits - top), 0.0)
            prob = expon / jnp.sum(expon, axis=1, keepdims=True)
            p_ref[0, 0, head, first:span, :span] = prob
            probs.append(prob)
        out = jnp.zeros((TILE, PAIR), f32)
        for head in range(2):
            spot = (group * 2 + head) * 2
            mixed = (mix_ref[spot] * probs[0] + mix_ref[spot + 1] * probs[1]).astype(bf16)
            out = out + nn(mixed, qkv_ref[0, :span, 2 * PAIR :] * head_lanes(head).astype(bf16))
        heads_ref[0, first:span, :] = out
        centred, inverse, _ = norm_parts(out)
        joined_ref[0, first:span, :] = (centred * inverse * gain_ref[...]).astype(bf16)


def attend_bwd_body(kern_ref, mix_ref, qkv_ref, gain_ref, heads_ref, p_ref, dj_ref, dqkv_ref, gk_ref, gmix_ref, ggain_ref, d_ref, dlow_ref, mixed_ref, mt_ref, bands_ref, do_ref, dqa_ref, dka_ref, corr_ref, kx_ref):
    length = qkv_ref.shape[1]
    tiles = length // TILE
    scale = 1.0 / math.sqrt(DH)
    group = pl.program_id(0)

    @pl.when(jnp.logical_and(group == 0, pl.program_id(1) == 0))
    def _():
        d_ref[...] = jnp.zeros_like(d_ref)
        dlow_ref[...] = jnp.zeros_like(dlow_ref)
        mt_ref[...] = jnp.zeros_like(mt_ref)

    @pl.when(pl.program_id(1) == 0)
    def _():
        corr_ref[...] = jnp.zeros_like(corr_ref)
        gmix_ref[...] = jnp.zeros_like(gmix_ref)
        ggain_ref[...] = jnp.zeros_like(ggain_ref)

    gain_total = jnp.zeros((1, PAIR), f32)
    for tile in range(tiles):
        first = tile * TILE
        span = first + TILE
        centred, inverse, masks = norm_parts(heads_ref[0, first:span, :])
        unit = centred * inverse
        outer = dj_ref[0, first:span, :].astype(f32)
        gain_total = gain_total + jnp.sum(outer * unit, axis=0, keepdims=True)
        inner = outer * gain_ref[...]
        result = inner
        for mask in masks:
            mean = jnp.sum(inner * mask, axis=1, keepdims=True) / DH
            along = jnp.sum(inner * unit * mask, axis=1, keepdims=True) / DH
            result = result - mask * (mean + unit * along)
        do_ref[first:span, :] = (result * inverse).astype(bf16)
    ggain_ref[0] = ggain_ref[0] + gain_total

    sums = [[jnp.zeros((1, 1), f32) for _ in range(2)] for _ in range(2)]
    mix = [[mix_ref[(group * 2 + head) * 2 + other] for other in range(2)] for head in range(2)]
    for tile in range(tiles):
        first = tile * TILE
        span = first + TILE
        probs = [jnp.where(lax.broadcasted_iota(jnp.int32, (TILE, span), 1) <= lax.broadcasted_iota(jnp.int32, (TILE, span), 0) + first, p_ref[0, 0, head, first:span, :span], 0.0) for head in range(2)]
        grads = []
        for head in range(2):
            mixed = (mix[head][0] * probs[0] + mix[head][1] * probs[1]).astype(bf16)
            mixed_ref[head, first:span, :span] = mixed
            grads.append(nt(do_ref[first:span, :] * head_lanes(head).astype(bf16), qkv_ref[0, :span, 2 * PAIR :]))
        for other in range(2):
            row_sum = jnp.zeros((TILE, 1), f32)
            for head in range(2):
                along = jnp.sum(grads[head] * probs[other], axis=1, keepdims=True)
                sums[head][other] = sums[head][other] + jnp.sum(along, axis=0, keepdims=True)
                row_sum = row_sum + mix[head][other] * along
            outer = mix[0][other] * grads[0] + mix[1][other] * grads[1]
            d_ref[other, first + PAD : span + PAD, :span] = probs[other] * (outer - row_sum)
            dlow_ref[other, first + PAD : span + PAD, :span] = d_ref[other, first + PAD : span + PAD, :span].astype(bf16)
    lane = lax.broadcasted_iota(jnp.int32, (1, TILE), 1)
    spread = jnp.zeros((1, TILE), f32)
    for head in range(2):
        for other in range(2):
            spread = spread + jnp.where(lane == head * 2 + other, sums[head][other], 0.0)
    gmix_ref[0] = gmix_ref[0] + spread

    for tile in range(tiles):
        first = tile * TILE
        total = jnp.zeros((TILE, PAIR), f32)
        for head in range(2):
            total = total + tn(mixed_ref[head, first:, first : first + TILE], do_ref[first:, :] * head_lanes(head).astype(bf16))
        dqkv_ref[0, first : first + TILE, 2 * PAIR :] = total.astype(bf16)

    dqa_ref[...] = jnp.zeros_like(dqa_ref)
    dka_ref[...] = jnp.zeros_like(dka_ref)

    shift_keys(qkv_ref[0, :, PAIR : 2 * PAIR], kx_ref)

    def one_head(head, carry):
        base = (group * 2 + head) * (QT * KT)
        fill_bands(kern_ref, base, bands_ref, None, lambda row, col: row - TILE - col + (KT - 1))
        lanes = head_lanes(head).astype(bf16)
        query = qkv_ref[0, :, :PAIR] * lanes
        for tile in range(tiles + 1):
            start = max(0, tile - 1) * TILE
            scores = nt(kx_ref[tile * TILE : (tile + 1) * TILE, :], query[start:]) * scale
            key = lax.broadcasted_iota(jnp.int32, (TILE, length - start), 0) + (tile * TILE - REACH)
            pos = lax.broadcasted_iota(jnp.int32, (TILE, length - start), 1) + start
            valid = jnp.logical_and(key >= 0, key <= pos)
            mt_ref[tile * TILE : (tile + 1) * TILE, start:] = jnp.where(valid, scores, 0.0).astype(bf16)
        for tile in range(tiles):
            start = max(0, tile - 1) * TILE
            count = length - start
            source = d_ref[head, start + PAD :, tile * TILE : (tile + 1) * TILE]
            moved = [source[:count].astype(bf16)]
            for lag in range(1, QT):
                moved.append(pltpu.roll(source, source.shape[0] - lag, 0)[:count].astype(bf16))
            stacked = jnp.concatenate(moved, axis=1)
            corr_ref[head] = corr_ref[head] + nn(mt_ref[tile * TILE : (tile + 2) * TILE, start:], stacked)
        for tile in range(tiles + 1):
            first = tile * TILE
            if tile == 0:
                wide = nn(dlow_ref[head, first:, :TILE], bands_ref[TILE:, :])
            elif tile == tiles:
                wide = nn(dlow_ref[head, first:, first - TILE : first], bands_ref[:TILE, :])
            else:
                wide = nn(dlow_ref[head, first:, first - TILE : first + TILE], bands_ref[...])
            total = wide[:, :TILE]
            rows = wide.shape[0]
            for lag in range(1, QT):
                total = total + pltpu.roll(wide[:, lag * TILE : (lag + 1) * TILE], rows - lag, 0)
            begin = max(0, first - PAD)
            total = total[begin - (first - PAD) : rows - PAD]
            grad = jnp.where(valid_keys(begin, length - begin, first), total, 0.0).astype(bf16)
            dqa_ref[begin:, :] = dqa_ref[begin:, :] + nn(grad, kx_ref[first : first + TILE, :] * lanes)
            dka_ref[first : first + TILE, :] = dka_ref[first : first + TILE, :] + tn(grad, query[begin:])
        return carry

    lax.fori_loop(0, 2, one_head, 0)
    dqkv_ref[0, :, :PAIR] = (dqa_ref[...] * scale).astype(bf16)
    keys = dka_ref[...]
    dqkv_ref[0, :, PAIR : 2 * PAIR] = (pltpu.roll(keys, keys.shape[0] - REACH, 0)[:length] * scale).astype(bf16)

    @pl.when(pl.program_id(1) == pl.num_programs(1) - 1)
    def _():
        row = lax.broadcasted_iota(jnp.int32, (2 * TILE, QT * TILE), 0)
        col = lax.broadcasted_iota(jnp.int32, (2 * TILE, QT * TILE), 1) % TILE
        for head in range(2):
            corr = corr_ref[head]
            for key_lag in range(KT):
                gk_ref[0, head, key_lag : key_lag + 1, :] = jnp.sum(jnp.where(row - col == (KT - 1) - key_lag, corr, 0.0), axis=0, keepdims=True)
            gk_ref[0, head, KT:, :] = jnp.zeros((16 - KT, QT * TILE), f32)


def block_specs(length):
    smem = pl.BlockSpec(memory_space=pltpu.SMEM)
    one = pl.BlockSpec((1, length, PAIR), lambda g, s: (s, 0, g))
    three = pl.BlockSpec((1, length, 3 * PAIR), lambda g, s: (s, 0, g))
    gain = pl.BlockSpec((1, PAIR), lambda g, s: (0, g))
    prob = pl.BlockSpec((1, 1, 2, length, length), lambda g, s: (s, g, 0, 0, 0))
    return smem, one, three, gain, prob


def attend_fwd(kern, mix, qkv, gain):
    seqs, length, width = qkv.shape
    groups = width // (3 * PAIR)
    smem, one, three, gspec, prob = block_specs(length)
    rows = (seqs, length, groups * PAIR)
    return pl.pallas_call(
        attend_fwd_body,
        grid=(groups, seqs),
        in_specs=[smem, smem, three, gspec],
        out_specs=[one, one, prob],
        out_shape=[
            jax.ShapeDtypeStruct(rows, bf16),
            jax.ShapeDtypeStruct(rows, f32),
            jax.ShapeDtypeStruct((seqs, groups, 2, length, length), f32),
        ],
        scratch_shapes=[
            pltpu.VMEM((length + PAD, length + TILE), bf16),
            pltpu.VMEM((length + PAD, length + TILE), bf16),
            pltpu.VMEM((2 * TILE, QT * TILE), bf16),
            pltpu.VMEM((2 * TILE, QT * TILE), bf16),
            pltpu.VMEM((length + TILE, PAIR), bf16),
        ],
        name="attend_fwd",
    )(kern, mix, qkv, gain)


def attend_bwd(kern, mix, qkv, gain, heads, probs, outer):
    seqs, length, width = qkv.shape
    groups = width // (3 * PAIR)
    smem, one, three, gspec, prob = block_specs(length)
    return pl.pallas_call(
        attend_bwd_body,
        grid=(groups, seqs),
        in_specs=[smem, smem, three, gspec, one, prob, one],
        out_specs=[
            three,
            pl.BlockSpec((1, 2, 16, QT * TILE), lambda g, s: (g, 0, 0, 0)),
            pl.BlockSpec((1, 1, TILE), lambda g, s: (g, 0, 0)),
            pl.BlockSpec((1, 1, PAIR), lambda g, s: (g, 0, 0)),
        ],
        out_shape=[
            jax.ShapeDtypeStruct(qkv.shape, bf16),
            jax.ShapeDtypeStruct((groups, 2, 16, QT * TILE), f32),
            jax.ShapeDtypeStruct((groups, 1, TILE), f32),
            jax.ShapeDtypeStruct((groups, 1, PAIR), f32),
        ],
        scratch_shapes=[
            pltpu.VMEM((2, length + 2 * PAD, length), f32),
            pltpu.VMEM((2, length + 2 * PAD, length), bf16),
            pltpu.VMEM((2, length, length), bf16),
            pltpu.VMEM((length + TILE, length), bf16),
            pltpu.VMEM((2 * TILE, QT * TILE), bf16),
            pltpu.VMEM((length, PAIR), bf16),
            pltpu.VMEM((length, PAIR), f32),
            pltpu.VMEM((length + TILE, PAIR), f32),
            pltpu.VMEM((2, 2 * TILE, QT * TILE), f32),
            pltpu.VMEM((length + TILE, PAIR), bf16),
        ],
        name="attend_bwd",
    )(kern, mix, qkv, gain, heads, probs, outer)


def xor_perm(count, bit):
    return [(index, index ^ bit) for index in range(count)]


def swap(value, axis, bit):
    return lax.ppermute(value, axis, xor_perm(lax.axis_size(axis), bit))


def place(pieces, count, here):
    rows, cols = pieces[0].shape
    out = jnp.zeros((count * rows, cols), pieces[0].dtype)
    for offset, piece in pieces.items():
        out = lax.dynamic_update_slice(out, piece, ((here ^ offset) * rows, 0))
    return out


def far_bits(count):
    bits = []
    bit = 2
    while bit < count:
        bits.append(bit)
        bit *= 2
    return bits


def batch_gather(value):
    count = lax.axis_size("batch")
    here = lax.axis_index("batch")
    bits = far_bits(count)
    pieces = {0: value}
    if len(bits) == 2:
        half = value.shape[0] // 2
        one, two = bits
        pieces[one] = swap(value, "batch", one)
        pieces[two] = swap(value, "batch", two)
        upper = swap(pieces[one][:half], "batch", two)
        lower = swap(pieces[two][half:], "batch", one)
        near = {offset: swap(piece, "batch", 1) for offset, piece in pieces.items()}
        near_upper = swap(upper, "batch", 1)
        near_lower = swap(lower, "batch", 1)
        rows, cols = value.shape
        out = jnp.zeros((count * rows, cols), value.dtype)
        for offset, piece in pieces.items():
            out = lax.dynamic_update_slice(out, piece, ((here ^ offset) * rows, 0))
            out = lax.dynamic_update_slice(out, near[offset], ((here ^ offset ^ 1) * rows, 0))
        both = one ^ two
        out = lax.dynamic_update_slice(out, upper, ((here ^ both) * rows, 0))
        out = lax.dynamic_update_slice(out, lower, ((here ^ both) * rows + half, 0))
        out = lax.dynamic_update_slice(out, near_upper, ((here ^ both ^ 1) * rows, 0))
        out = lax.dynamic_update_slice(out, near_lower, ((here ^ both ^ 1) * rows + half, 0))
        return out
    for bit in bits + [1]:
        pieces.update({offset ^ bit: swap(piece, "batch", bit) for offset, piece in pieces.items()})
    return place(pieces, count, here)


def batch_scatter(value):
    count = lax.axis_size("batch")
    here = lax.axis_index("batch")
    bits = far_bits(count)
    rows = value.shape[0] // count

    def block(offset):
        return lax.dynamic_slice_in_dim(value, (here ^ offset) * rows, rows, 0)

    def add(left, right):
        return left.astype(f32) + right.astype(f32)

    offsets = [0]
    for bit in bits:
        offsets = offsets + [offset ^ bit for offset in offsets]
    came = {offset: swap(block(offset ^ 1), "batch", 1) for offset in reversed(offsets)}
    sums = {offset: add(block(offset), came[offset]) for offset in offsets}
    if len(bits) == 2:
        one, two = bits
        half = rows // 2
        far = sums[one ^ two].astype(bf16)
        upper = swap(far[:half], "batch", one)
        lower = swap(far[half:], "batch", two)
        via_two = jnp.concatenate([add(sums[two][:half], upper), sums[two][half:]], axis=0)
        via_one = jnp.concatenate([sums[one][:half], add(sums[one][half:], lower)], axis=0)
        from_one = swap(via_one.astype(bf16), "batch", one)
        from_two = swap(via_two.astype(bf16), "batch", two)
        return sums[0] + from_one.astype(f32) + from_two.astype(f32)
    for bit in reversed(bits):
        offsets = [offset for offset in offsets if not offset & bit]
        sums = {
            offset: add(sums[offset], swap(sums[offset ^ bit].astype(bf16), "batch", bit))
            for offset in offsets
        }
    return sums[0]


def line_perms(count):
    up = [(index, index + 1) for index in range(count - 1)]
    down = [(index + 1, index) for index in range(count - 1)]
    return up, down


def seq_gather(value):
    count = lax.axis_size("seq")
    here = lax.axis_index("seq")
    up, down = line_perms(count)
    rows = value.shape[0]
    rising, falling = [value], [value]
    for _ in range(count - 1):
        rising.append(lax.ppermute(rising[-1], "seq", up))
        falling.append(lax.ppermute(falling[-1], "seq", down))
    out = jnp.zeros((count * rows, value.shape[1]), value.dtype)
    out = lax.dynamic_update_slice(out, value, (here * rows, 0))
    for step in range(1, count):
        piece = jnp.where(here >= step, rising[step], falling[count - step])
        out = lax.dynamic_update_slice(out, piece, (((here - step) % count) * rows, 0))
    return out


def seq_scatter(value):
    count = lax.axis_size("seq")
    here = lax.axis_index("seq")
    up, down = line_perms(count)
    rows = value.shape[0] // count

    def block(index):
        return lax.dynamic_slice_in_dim(value, jnp.clip(index, 0, count - 1) * rows, rows, 0)

    rising = falling = None
    for step in range(1, count):
        far = count - step
        top, low = block(here + far), block(here - far)
        if rising is not None:
            top = (top.astype(f32) + rising.astype(f32)).astype(bf16)
            low = (low.astype(f32) + falling.astype(f32)).astype(bf16)
        rising = lax.ppermute(top, "seq", up)
        falling = lax.ppermute(low, "seq", down)
    return block(here).astype(f32) + rising.astype(f32) + falling.astype(f32)


def seq_swap(blocks):
    count = lax.axis_size("seq")
    here = lax.axis_index("seq")
    out = jnp.zeros_like(blocks)
    own = lax.dynamic_index_in_dim(blocks, here, 0, True)
    out = lax.dynamic_update_slice_in_dim(out, own, here, 0)
    for step in range(1, count):
        piece = lax.dynamic_index_in_dim(blocks, (here + step) % count, 0, True)
        perm = [(index, (index + step) % count) for index in range(count)]
        piece = lax.ppermute(piece, "seq", perm)
        out = lax.dynamic_update_slice_in_dim(out, piece, (here - step) % count, 0)
    return out


def all_sum(value):
    for axis in ("batch", "seq"):
        bit = 1
        while bit < lax.axis_size(axis):
            value = value + swap(value, axis, bit)
            bit *= 2
    return value


def pad_pairs(value):
    lead = value.shape[0]
    pairs = value.reshape(lead, -1, 2 * DH)
    return jnp.pad(pairs, ((0, 0), (0, 0), (0, PAIR - 2 * DH))).reshape(lead, -1)


def cut_pairs(value):
    lead = value.shape[0]
    return value.reshape(lead, -1, PAIR)[:, :, : 2 * DH].reshape(lead, -1)


def inverse_rms(values):
    return lax.rsqrt(jnp.mean(values * values, axis=-1, keepdims=True) + 1e-06)


def rms_back(values, inverse, inner):
    along = jnp.mean(values * inner, axis=-1, keepdims=True)
    return inverse * (inner - values * (inverse * inverse) * along)


def per_device(
    inputs,
    output_grad,
    source_tags,
    source_counts,
    gain_in,
    w_query,
    w_key,
    w_value,
    kernel,
    mixing,
    gain_head,
    w_out,
    gain_mid,
    w_gate,
    w_up,
    w_down,
):
    seqs, seg, width = inputs.shape
    parts = lax.axis_size("seq")
    lanes = lax.axis_size("batch")
    place_seq = lax.axis_index("seq")
    place_batch = lax.axis_index("batch")
    length = seg * parts
    groups = H // (2 * parts)
    local = groups * 2 * DH
    own = w_query.shape[0]
    blocks = parts * lanes

    joint = jnp.stack([w_query, w_key, w_value], axis=1).reshape(own, 3, parts, groups, 2 * DH)
    joint = joint.transpose(2, 0, 3, 1, 4).reshape(parts, own, 3 * local)
    gains = jnp.stack([gain_in, gain_head, gain_mid]).reshape(1, 1, 3 * own)
    gains = jnp.pad(gains, ((0, 0), (0, 15), (0, 3 * local - 3 * own)))
    packed = jnp.concatenate([joint, jnp.broadcast_to(gains, (parts, 16, 3 * local))], axis=1)
    packed = seq_swap(packed)
    order = [
        (index, (index % lanes) * parts + index // lanes) for index in range(blocks)
    ]
    out_rows = lax.ppermute(w_out, ("batch", "seq"), order)
    flat_rows = own * width // (3 * local)
    gain_row = packed[:, own, : 3 * own].reshape(1, parts * 3 * own)
    gain_row = jnp.pad(gain_row, ((0, 15), (0, 3 * local - parts * 3 * own)))
    shard = jnp.concatenate(
        [packed[:, :own].reshape(parts * own, 3 * local), gain_row, out_rows.reshape(flat_rows, 3 * local)],
        axis=0,
    )
    gathered = batch_gather(shard).reshape(lanes, -1, 3 * local)
    w_joint = pad_pairs(gathered[:, : parts * own].reshape(width, 3 * local))
    gain_rows = gathered[:, parts * own, : parts * 3 * own].reshape(lanes, parts, 3, own)
    all_gains = gain_rows.transpose(2, 0, 1, 3).reshape(3, 1, width).astype(f32)
    gain_in32, gain_head32, gain_mid32 = all_gains[0], all_gains[1], all_gains[2]
    gain_own = pad_pairs(lax.dynamic_slice_in_dim(gain_head32, place_seq * local, local, 1))
    w_join = gathered[:, parts * own + 16 :].reshape(local, width)
    w_join = jnp.pad(
        w_join.reshape(groups, 2 * DH, width), ((0, 0), (0, PAIR - 2 * DH), (0, 0))
    ).reshape(groups * PAIR, width)
    kern_own = lax.dynamic_slice_in_dim(
        kernel.reshape(-1), place_seq * (2 * groups * QT * KT), 2 * groups * QT * KT, 0
    )
    mix_own = lax.dynamic_slice_in_dim(mixing.reshape(-1), place_seq * 4 * groups, 4 * groups, 0)

    x_all = [seq_gather(inputs[index]) for index in range(seqs)]
    w_gate_up = batch_gather(jnp.concatenate([w_gate, w_up], axis=1))
    w_down_t = batch_gather(w_down.T)
    hidden_width = w_gate.shape[1]
    o_all = [seq_gather(output_grad[index]) for index in range(seqs)]

    source_ids = jnp.arange(source_counts.shape[0], dtype=jnp.int32)
    tag_count = jnp.sum(
        jnp.where(source_tags[:, None] == source_ids[None, :], source_counts[None, :], 0), axis=1
    )
    factor = length / tag_count.astype(f32)

    outputs, input_grads = [], []
    keep = []
    for index in range(seqs):
        x32 = x_all[index].astype(f32)
        x_inverse = inverse_rms(x32)
        normed = (x32 * x_inverse * gain_in32).astype(bf16)
        qkv = nn(normed, w_joint).astype(bf16)[None]
        joined, heads, probs = attend_fwd(kern_own, mix_own, qkv, gain_own)
        middle = inputs[index].astype(f32) + seq_scatter(nn(joined[0], w_join).astype(bf16))
        keep.append([x_inverse, normed, qkv, joined, heads, probs, middle])
    gain_mid_grad = jnp.zeros((1, width), f32)
    gain_in_grad = jnp.zeros((1, width), f32)
    ffn = []
    for index in range(seqs):
        middle = keep[index][-1]
        mid_inverse = inverse_rms(middle)
        n_all = seq_gather((middle * mid_inverse * gain_mid32).astype(bf16))
        both = nn(n_all, w_gate_up)
        gate, upward = both[:, :hidden_width], both[:, hidden_width:]
        sigma = 1.0 / (1.0 + jnp.exp(-gate))
        silu = gate * sigma
        hidden = (silu * upward).astype(bf16)
        down_in = (o_all[index].astype(f32) * factor[index]).astype(bf16)
        hidden_grad = nn(down_in, w_down_t)
        gate_grad = (hidden_grad * upward * (sigma * (1.0 + gate * (1.0 - sigma)))).astype(bf16)
        up_grad = (hidden_grad * silu).astype(bf16)
        grads = jnp.concatenate([gate_grad, up_grad], axis=1)
        mid_grad = seq_scatter(nt(grads, w_gate_up).astype(bf16))
        result = middle + seq_scatter(nt(hidden, w_down_t).astype(bf16))
        outputs.append(result.astype(bf16))
        ffn.append((n_all, hidden, down_in, grads))
        unit = middle * mid_inverse
        gain_mid_grad = gain_mid_grad + jnp.sum(mid_grad * unit, axis=0, keepdims=True)
        cotangent = output_grad[index].astype(f32) * factor[index]
        middle_grad = cotangent + rms_back(middle, mid_inverse, mid_grad * gain_mid32)
        a_all = seq_gather(middle_grad.astype(bf16))
        keep[index] += [middle_grad, a_all]
    cat = lambda place: jnp.concatenate([item[place] for item in ffn], axis=0)
    all_n, all_hidden, all_down, all_grads = cat(0), cat(1), cat(2), cat(3)
    g_gate_up = batch_scatter(tn(all_n, all_grads).astype(bf16))
    g_down_t = batch_scatter(tn(all_down, all_hidden).astype(bf16))
    back = []
    for index in range(seqs):
        x_inverse, normed, qkv, joined, heads, probs, middle, middle_grad, a_all = keep[index]
        outer = nt(a_all, w_join)[None]
        dqkv, corr, mix_sum, head_sum = attend_bwd(
            kern_own, mix_own, qkv, gain_own, heads, probs, outer
        )
        n_part = nt(dqkv[0], w_joint)
        unit_all = x_all[index].astype(f32) * x_inverse
        gain_in_grad = gain_in_grad + jnp.sum(n_part * unit_all, axis=0, keepdims=True)
        n_grad = seq_scatter(n_part.astype(bf16))
        x32 = inputs[index].astype(f32)
        inner = rms_back(x32, inverse_rms(x32), n_grad * gain_in32)
        input_grads.append((middle_grad + inner).astype(bf16))
        back.append((normed, dqkv[0], joined[0], a_all, corr, mix_sum, head_sum))
    cat = lambda place: jnp.concatenate([item[place] for item in back], axis=0)
    all_normed, all_dqkv, all_joined, all_a = cat(0), cat(1), cat(2), cat(3)
    g_out = tn(all_joined, all_a).astype(bf16)
    g_out = g_out.reshape(groups, PAIR, width)[:, : 2 * DH].reshape(local, width)
    g_out = batch_scatter(g_out)
    g_out = lax.ppermute(g_out, ("batch", "seq"), [(there, here) for here, there in order])
    g_joint = batch_scatter(cut_pairs(tn(all_normed, all_dqkv)).astype(bf16))
    g_joint = seq_swap(g_joint.astype(bf16).reshape(parts, own, 3 * local)).astype(f32)
    g_joint = g_joint.reshape(parts, own, groups, 3, 2 * DH).transpose(3, 1, 0, 2, 4)
    g_joint = g_joint.reshape(3, own, width)

    corr = sum(item[4] for item in back)
    mix_sum = sum(item[5] for item in back)
    head_sum = sum(item[6] for item in back)
    kern_grad = corr[:, :, :KT].reshape(2 * groups, KT, QT, TILE).sum(-1).transpose(0, 2, 1)
    mix_grad = mix_sum[:, 0, :4].reshape(-1)
    head_grad = head_sum[:, 0, : 2 * DH].reshape(-1)

    def spread(value, total):
        return lax.dynamic_update_slice_in_dim(
            jnp.zeros((total,), f32), value.reshape(-1), place_seq * value.size, 0
        )

    small = jnp.concatenate(
        [
            gain_in_grad[0],
            gain_mid_grad[0],
            spread(head_grad, width),
            spread(kern_grad, H * QT * KT),
            spread(mix_grad, H * 2),
        ]
    )
    size = small.size
    small = jnp.pad(small, (0, -size % 1024)).reshape(-1, 128)
    small = all_sum(small).reshape(-1)
    start = (place_batch * parts + place_seq) * own
    cuts = [lax.dynamic_slice_in_dim(small, start + step * width, own, 0) for step in range(3)]
    kernel_sum = small[3 * width : 3 * width + H * QT * KT].reshape(kernel.shape)
    mixing_sum = small[3 * width + H * QT * KT : size].reshape(mixing.shape)
    return (
        jnp.stack(outputs),
        jnp.stack(input_grads),
        cuts[0],
        g_joint[0],
        g_joint[1],
        g_joint[2],
        kernel_sum,
        mixing_sum,
        cuts[2],
        g_out,
        cuts[1],
        g_gate_up[:, :hidden_width],
        g_gate_up[:, hidden_width:],
        g_down_t.T,
    )


def solution(mesh):
    rows = P(("batch", "seq"))
    mats = P(("batch", "seq"), None)
    tokens = P("batch", "seq", None)
    in_specs = (
        tokens,
        tokens,
        P("batch"),
        P(),
        rows,
        mats,
        mats,
        mats,
        P(),
        P(),
        rows,
        mats,
        rows,
        P("batch", "seq"),
        P("batch", "seq"),
        P("seq", "batch"),
    )
    out_specs = (
        tokens,
        tokens,
        rows,
        mats,
        mats,
        mats,
        P(),
        P(),
        rows,
        mats,
        rows,
        P("batch", "seq"),
        P("batch", "seq"),
        P("seq", "batch"),
    )
    return jax.shard_map(
        per_device, mesh=mesh, in_specs=in_specs, out_specs=out_specs, check_vma=False
    )
```

time: 3120 us -> 1020 us (0.33)
  waiting for transfers between devices: 1390 us -> 228 us
  other arithmetic: 1120 us -> 73.9 us
  starting transfers between devices: 1.49 us -> 339 us
  blocking collectives: 98.5 us -> 0 us
  local copies, waits for them, and re-layouts: 269 us -> 179 us
  matrix products: 181 us -> 101 us
  Pallas kernels: 0 us -> 75.8 us
  loops' own time: 42 us -> 0 us
    reduce_scatter x11 -> x0, waiting for transfers between devices: 747 us -> none  [the longest x1 142 us: per_device(): lax.psum_scatter(grad_value, ('batch', 'seq'), scatter_dimension=0, tiled...]
    all_gather x12 -> x0, waiting for transfers between devices: 625 us -> none  [the longest x1 208 us: per_device(): lax.all_gather(down_part, 'seq', axis=0, tiled=True)]
    ppermute x0 -> x168, starting transfers between devices: none -> 339 us  [the longest x24 107 us: seq_gather(): rising.append(lax.ppermute(rising[-1], 'seq', up))]
    sub x16 -> x0, other arithmetic: 312 us -> none  [mixed_probs(): expon = jnp.where(valid, jnp.exp(filled - top), 0.0)]
    add_any x16 -> x0, other arithmetic: 266 us -> none  [mixed_probs(): padded[:, rim - row_lag:rim - row_lag + row_count, 2 * reach - key_lag:2...]
    ppermute x0 -> x168, waiting for transfers between devices: none -> 228 us  [the longest x24 62.2 us: seq_scatter(): rising = lax.ppermute(top, 'seq', up)]
    reduce_sum x133 -> x6, other arithmetic: 181 us -> 5.92 us  [the longest x4 4.62 us: inverse_rms(): return lax.rsqrt(jnp.mean(values * values, axis=-1, keepdims=True) + 1e-06)]
    mul x66 -> x2, other arithmetic: 173 us -> 0.01 us  [rms_back(): return inverse * (inner - values * (inverse * inverse) * along)]
  transfers between devices with their start and end apart: 25 -> 168, of which waited for: 19 -> 54; matrix products, arithmetic and copies ran while one was open for 49% -> 27% of each run, Pallas kernels for 0% -> 3%
where the time goes in v1:
time: 1020 us; the launch traced here: 1000 us
  starting transfers between devices  339 us (33%)
  waiting for transfers between devices  228 us (22%)
  local copies, waits for them, and re-layouts  179 us (18%)
  matrix products  101 us (10%)
  Pallas kernels  75.8 us (7%)
  other arithmetic  73.9 us (7%)
    ppermute x24, starting transfers between devices, seq_gather(): rising.append(lax.ppermute(rising[-1], 'seq', up))  107 us
    ppermute x24, starting transfers between devices, seq_scatter(): rising = lax.ppermute(top, 'seq', up)  104 us
    ppermute x24, waiting for transfers between devices, seq_scatter(): rising = lax.ppermute(top, 'seq', up)  62.2 us
    ppermute x24, waiting for transfers between devices, seq_scatter(): falling = lax.ppermute(low, 'seq', down)  54.7 us
    ppermute x64, starting transfers between devices, swap(): return lax.ppermute(value, axis, xor_perm(lax.axis_size(axis), bit))  51.4 us
    ppermute x64, waiting for transfers between devices, swap(): return lax.ppermute(value, axis, xor_perm(lax.axis_size(axis), bit))  48.3 us
    pallas_call x2, Pallas kernels, attend_bwd(): pl.pallas_call(attend_bwd_body, grid=(groups, seqs), in_specs=[smem, smem...  47.2 us
    dot_general x8, matrix products, nt(): lax.dot_general(a, b, (((1,), (1,)), ((), ())), preferred_element_type=f32)  39.6 us
  transfers between devices with their start and end apart: 168, of which 54 were waited for; matrix products, arithmetic and copies ran while one was open for 27% of the time, Pallas kernels for 3%

profile of v1, /device:TPU:0, one launch (start us, length us, event | category | flops | bytes accessed | tf_op | source)
XLA Modules:
  0.0 1001.1 jit_solution(5398302139589952081)
XLA Ops:
  95.9 17.9 %collective-permute-done.45 = bf16[96,1024]{1,0:T(8,128)(2,1)S(1)} collective-permute-done((bf16[96,1024]{1,0:T(8,128)(2,1)S(1)}, bf16[96,1024]{1,0:T(8,128)(2,1)S(1)}, u32[]{:S(2)}, u32[]{:S(2)}) %collective-permute-start.45) | collective-permute-done | bytes 196640 | tf_op jit(solution)/shard_map/ppermute | solution.py:351
  168.9 5.9 collective-permute-done.4
  185.7 12.2 %collective-permute-done.5 = bf16[128,1536]{1,0:T(8,128)(2,1)S(1)} collective-permute-done((bf16[128,1536]{1,0:T(8,128)(2,1)S(1)}, bf16[128,1536]{1,0:T(8,128)(2,1)S(1)}, u32[]{:S(2)}, u32[]{:S(2)}) %collective-permute-start.5) | collective-permute-done | bytes 393248 | tf_op jit(solution)/shard_map/ppermute | solution.py:452
  202.9 6.7 collective-permute-done.106
  263.1 7.0 copy.113
  270.1 8.1 reshape_reshape.6
  295.9 14.3 %attend_fwd.3 = (bf16[1,512,512]{2,1,0:T(8,128)(2,1)}, f32[1,512,512]{2,1,0:T(8,128)}, f32[1,2,2,512,512]{4,3,2,1,0:T(8,128)}) custom-call(f32[264]{0:T(512)} %dynamic_slice.308.kern_ref, f32[8]{0:T(128)} %dynamic_slice.309.mix_ref, bf16[1,512,1536]{2,1,0:T(8,128)(2,1)} %fusion.37.qkv_ref, f32[1,512]{1,0:T(1,128)} %bitcast.164), custom_call_target="tpu_custom_call" | custom-call | tf_op jit(solution)/shard_map/attend_fwd/pallas_call | solution.py:289
  321.5 6.2 fusion.36.qkv_ref
  327.7 14.3 %attend_fwd.2 = (bf16[1,512,512]{2,1,0:T(8,128)(2,1)}, f32[1,512,512]{2,1,0:T(8,128)}, f32[1,2,2,512,512]{4,3,2,1,0:T(8,128)}) custom-call(f32[264]{0:T(512)} %dynamic_slice.308.kern_ref, f32[8]{0:T(128)} %dynamic_slice.309.mix_ref, bf16[1,512,1536]{2,1,0:T(8,128)(2,1)} %fusion.36.qkv_ref, f32[1,512]{1,0:T(1,128)} %bitcast.165), custom_call_target="tpu_custom_call" | custom-call | tf_op jit(solution)/shard_map/attend_fwd/pallas_call | solution.py:289
  365.9 6.1 collective-permute-done.62
  399.7 5.9 collective-permute-done.66
  466.9 6.2 fusion.117
  482.2 6.3 multiply_convert_fusion.5
  498.6 6.3 convolution_convert_fusion.5
  504.9 9.5 convolution_convert_fusion.1
  514.4 7.4 convolution_convert_fusion.6
  531.4 7.2 collective-permute-done.109
  543.1 8.0 collective-permute-done.73
  555.5 7.1 collective-permute-done.49
  567.2 6.2 collective-permute-done.85
  588.8 6.3 collective-permute-start.110
  615.0 6.4 collective-permute-done.50
  663.1 8.7 collective-permute-done.114
  671.9 7.2 collective-permute-done.78
  748.6 23.7 %attend_bwd.3 = (bf16[1,512,1536]{2,1,0:T(8,128)(2,1)}, f32[2,2,16,768]{3,2,1,0:T(8,128)}, f32[2,1,128]{2,1,0:T(1,128)}, f32[2,1,256]{2,1,0:T(1,128)}) custom-call(f32[264]{0:T(512)} %dynamic_slice.308.kern_ref, f32[8]{0:T(128)} %dynamic_slice.309.mix_ref, bf16[1,512,1536]{2,1,0:T(8,128)(2,1)} %fusion.37.qkv_ref, f32[1,512]{1,0:T(1,128)} %bitcast.166, ...), custom_call_target="tpu_custom_call" | custom-call | tf_op jit(solution)/shard_map/attend_bwd/pallas_call | solution.py:314
  772.3 23.5 %attend_bwd.2 = (bf16[1,512,1536]{2,1,0:T(8,128)(2,1)}, f32[2,2,16,768]{3,2,1,0:T(8,128)}, f32[2,1,128]{2,1,0:T(1,128)}, f32[2,1,256]{2,1,0:T(1,128)}) custom-call(f32[264]{0:T(512)} %dynamic_slice.308.kern_ref, f32[8]{0:T(128)} %dynamic_slice.309.mix_ref, bf16[1,512,1536]{2,1,0:T(8,128)(2,1)} %fusion.36.qkv_ref, f32[1,512]{1,0:T(1,128)} %bitcast.167, ...), custom_call_target="tpu_custom_call" | custom-call | tf_op jit(solution)/shard_map/attend_bwd/pallas_call | solution.py:314
  802.2 7.4 fusion.12
  819.2 7.7 convolution_convert_fusion
  877.6 7.3 collective-permute-done.121
  888.0 5.7 collective-permute-start.97
  909.9 7.6 collective-permute-done.135
  921.1 7.4 collective-permute-done.138
  (732 shorter events, 709.7 us)
Async XLA Ops:
  0.7 65.4 %collective-permute-start.40 = (bf16[192,1024]{1,0:T(8,128)(2,1)}, bf16[192,1024]{1,0:T(8,128)(2,1)}, u32[]{:S(2)}, u32[]{:S(2)}) collective-permute-start(bf16[192,1024]{1,0:T(8,128)(2,1)} %bitcast.157), channel_id=1, source_target_pairs={{0,4},{4,0},{8,12},{12,8},{16,20},{20,16},{24,28},{28,24},{1,5},{5... | collective-permute-start | bytes 1179656 | tf_op jit(solution)/shard_map/ppermute | solution.py:351
  1.2 66.9 %collective-permute-start.41 = (bf16[192,1024]{1,0:T(8,128)(2,1)}, bf16[192,1024]{1,0:T(8,128)(2,1)}, u32[]{:S(2)}, u32[]{:S(2)}) collective-permute-start(bf16[192,1024]{1,0:T(8,128)(2,1)} %bitcast.158), channel_id=1, source_target_pairs={{0,8},{4,12},{8,0},{12,4},{16,24},{20,28},{24,16},{28,20},{1,9},{5... | collective-permute-start | bytes 1179656 | tf_op jit(solution)/shard_map/ppermute | solution.py:351
  3.8 66.7 %collective-permute-start.43 = (bf16[192,1024]{1,0:T(8,128)(2,1)}, bf16[192,1024]{1,0:T(8,128)(2,1)S(1)}, u32[]{:S(2)}, u32[]{:S(2)}) collective-permute-start(bf16[192,1024]{1,0:T(8,128)(2,1)} %bitcast.159), channel_id=1, source_target_pairs={{0,16},{4,20},{8,24},{12,28},{16,0},{20,4},{24,8},{28,12},{1,17},{... | collective-permute-start | bytes 1179656 | tf_op jit(solution)/shard_map/ppermute | solution.py:351
  87.0 29.9 %collective-permute-start.32 = (bf16[192,2048]{1,0:T(8,128)(2,1)S(1)}, bf16[192,2048]{1,0:T(8,128)(2,1)}, u32[]{:S(2)}, u32[]{:S(2)}) collective-permute-start(bf16[192,2048]{1,0:T(8,128)(2,1)S(1)} %copy-done.19), channel_id=1, source_target_pairs={{0,8},{4,12},{8,0},{12,4},{16,24},{20,28},{24,16},{28,20},{1,9},{5... | collective-permute-start | bytes 2359304 | tf_op jit(solution)/shard_map/ppermute | solution.py:351
  89.6 36.0 %collective-permute-start.34 = (bf16[192,2048]{1,0:T(8,128)(2,1)S(1)}, bf16[192,2048]{1,0:T(8,128)(2,1)}, u32[]{:S(2)}, u32[]{:S(2)}) collective-permute-start(bf16[192,2048]{1,0:T(8,128)(2,1)S(1)} %copy-done.19), channel_id=1, source_target_pairs={{0,16},{4,20},{8,24},{12,28},{16,0},{20,4},{24,8},{28,12},{1,17},{... | collective-permute-start | bytes 2359304 | tf_op jit(solution)/shard_map/ppermute | solution.py:351
  163.6 39.0 %collective-permute-start.107 = (bf16[128,1536]{1,0:T(8,128)(2,1)S(1)}, bf16[128,1536]{1,0:T(8,128)(2,1)S(1)}, u32[]{:S(2)}, u32[]{:S(2)}) collective-permute-start(bf16[128,1536]{1,0:T(8,128)(2,1)S(1)} %collective-permute-done.103), channel_id=1, source_target_pairs={{0,1},{1,2},{2,3},{4,5},{5,6},{6,7},{8,9},{9,10},{10,11},{12,13},{... | collective-permute-start | bytes 1179656 | tf_op jit(solution)/shard_map/ppermute | solution.py:452
  167.6 47.5 %collective-permute-start.81 = (bf16[128,1536]{1,0:T(8,128)(2,1)S(1)}, bf16[128,1536]{1,0:T(8,128)(2,1)S(1)}, u32[]{:S(2)}, u32[]{:S(2)}) collective-permute-start(bf16[128,1536]{1,0:T(8,128)(2,1)S(1)} %collective-permute-done.80), channel_id=1, source_target_pairs={{1,0},{2,1},{3,2},{5,4},{6,5},{7,6},{9,8},{10,9},{11,10},{13,12},{... | collective-permute-start | bytes 1179656 | tf_op jit(solution)/shard_map/ppermute | solution.py:453
  174.8 49.8 %collective-permute-start.83 = (bf16[128,1536]{1,0:T(8,128)(2,1)S(1)}, bf16[128,1536]{1,0:T(8,128)(2,1)S(1)}, u32[]{:S(2)}, u32[]{:S(2)}) collective-permute-start(bf16[128,1536]{1,0:T(8,128)(2,1)S(1)} %collective-permute-done.79), channel_id=1, source_target_pairs={{0,1},{1,2},{2,3},{4,5},{5,6},{6,7},{8,9},{9,10},{10,11},{12,13},{... | collective-permute-start | bytes 1179656 | tf_op jit(solution)/shard_map/ppermute | solution.py:452
  184.8 61.3 %collective-permute-start.15 = (bf16[136,1152]{1,0:T(8,128)(2,1)S(1)}, bf16[136,1152]{1,0:T(8,128)(2,1)S(1)}, u32[]{:S(2)}, u32[]{:S(2)}) collective-permute-start(bf16[136,1152]{1,0:T(8,128)(2,1)S(1)} %slice.272), channel_id=1, source_target_pairs={{0,16},{4,20},{8,24},{12,28},{16,0},{20,4},{24,8},{28,12},{1,17},{... | collective-permute-start | bytes 940040 | tf_op jit(solution)/shard_map/ppermute | solution.py:351
  202.5 44.2 %collective-permute-start.16 = (bf16[136,1152]{1,0:T(8,128)(2,1)S(1)}, bf16[136,1152]{1,0:T(8,128)(2,1)S(1)}, u32[]{:S(2)}, u32[]{:S(2)}) collective-permute-start(bf16[136,1152]{1,0:T(8,128)(2,1)S(1)} %slice.273), channel_id=1, source_target_pairs={{0,8},{4,12},{8,0},{12,4},{16,24},{20,28},{24,16},{28,20},{1,9},{5... | collective-permute-start | bytes 940040 | tf_op jit(solution)/shard_map/ppermute | solution.py:351
  215.0 29.4 %collective-permute-start.12 = (bf16[272,1152]{1,0:T(8,128)(2,1)}, bf16[272,1152]{1,0:T(8,128)(2,1)S(1)}, u32[]{:S(2)}, u32[]{:S(2)}) collective-permute-start(bf16[272,1152]{1,0:T(8,128)(2,1)} %collective-permute-done.11), channel_id=1, source_target_pairs={{0,4},{4,0},{8,12},{12,8},{16,20},{20,16},{24,28},{28,24},{1,5},{5... | collective-permute-start | bytes 1880072 | tf_op jit(solution)/shard_map/ppermute | solution.py:351
  238.6 160.1 %collective-permute-start.36 = (bf16[96,2048]{1,0:T(8,128)(2,1)}, bf16[96,2048]{1,0:T(8,128)(2,1)}, u32[]{:S(2)}, u32[]{:S(2)}) collective-permute-start(bf16[96,2048]{1,0:T(8,128)(2,1)} %slice.280), channel_id=1, source_target_pairs={{0,16},{4,20},{8,24},{12,28},{16,0},{20,4},{24,8},{28,12},{1,17},{... | collective-permute-start | bytes 1179656 | tf_op jit(solution)/shard_map/ppermute | solution.py:351
  244.4 101.0 %collective-permute-start.33 = (bf16[192,2048]{1,0:T(8,128)(2,1)}, bf16[192,2048]{1,0:T(8,128)(2,1)}, u32[]{:S(2)}, u32[]{:S(2)}) collective-permute-start(bf16[192,2048]{1,0:T(8,128)(2,1)} %collective-permute-done.32), channel_id=1, source_target_pairs={{0,4},{4,0},{8,12},{12,8},{16,20},{20,16},{24,28},{28,24},{1,5},{5... | collective-permute-start | bytes 2359304 | tf_op jit(solution)/shard_map/ppermute | solution.py:351
  246.2 147.0 %collective-permute-start.35 = (bf16[192,2048]{1,0:T(8,128)(2,1)}, bf16[192,2048]{1,0:T(8,128)(2,1)}, u32[]{:S(2)}, u32[]{:S(2)}) collective-permute-start(bf16[192,2048]{1,0:T(8,128)(2,1)} %collective-permute-done.34), channel_id=1, source_target_pairs={{0,4},{4,0},{8,12},{12,8},{16,20},{20,16},{24,28},{28,24},{1,5},{5... | collective-permute-start | bytes 2359304 | tf_op jit(solution)/shard_map/ppermute | solution.py:351
  314.9 37.4 %collective-permute-start.61 = (bf16[128,1536]{1,0:T(8,128)(2,1)}, bf16[128,1536]{1,0:T(8,128)(2,1)}, u32[]{:S(2)}, u32[]{:S(2)}) collective-permute-start(bf16[128,1536]{1,0:T(8,128)(2,1)} %get-tuple-element.206), channel_id=1, source_target_pairs={{0,1},{1,2},{2,3},{4,5},{5,6},{6,7},{8,9},{9,10},{10,11},{12,13},{... | collective-permute-start | bytes 1179656 | tf_op jit(solution)/shard_map/ppermute | solution.py:478
  320.0 42.7 %collective-permute-start.64 = (bf16[128,1536]{1,0:T(8,128)(2,1)}, bf16[128,1536]{1,0:T(8,128)(2,1)}, u32[]{:S(2)}, u32[]{:S(2)}) collective-permute-start(bf16[128,1536]{1,0:T(8,128)(2,1)} %get-tuple-element.207), channel_id=1, source_target_pairs={{1,0},{2,1},{3,2},{5,4},{6,5},{7,6},{9,8},{10,9},{11,10},{13,12},{... | collective-permute-start | bytes 1179656 | tf_op jit(solution)/shard_map/ppermute | solution.py:479
  523.0 63.1 %collective-permute-start.153 = (bf16[192,2048]{1,0:T(8,128)(2,1)S(1)}, bf16[192,2048]{1,0:T(8,128)(2,1)S(1)}, u32[]{:S(2)}, u32[]{:S(2)}) collective-permute-start(bf16[192,2048]{1,0:T(8,128)(2,1)S(1)} %get-tuple-element.142), channel_id=1, source_target_pairs={{0,4},{4,0},{8,12},{12,8},{16,20},{20,16},{24,28},{28,24},{1,5},{5... | collective-permute-start | bytes 2359304 | tf_op jit(solution)/shard_map/ppermute | solution.py:351
  523.5 63.9 %collective-permute-start.154 = (bf16[192,2048]{1,0:T(8,128)(2,1)S(1)}, bf16[192,2048]{1,0:T(8,128)(2,1)S(1)}, u32[]{:S(2)}, u32[]{:S(2)}) collective-permute-start(bf16[192,2048]{1,0:T(8,128)(2,1)S(1)} %get-tuple-element.141), channel_id=1, source_target_pairs={{0,4},{4,0},{8,12},{12,8},{16,20},{20,16},{24,28},{28,24},{1,5},{5... | collective-permute-start | bytes 2359304 | tf_op jit(solution)/shard_map/ppermute | solution.py:351
  525.1 63.7 %collective-permute-start.157 = (bf16[192,2048]{1,0:T(8,128)(2,1)S(1)}, bf16[192,2048]{1,0:T(8,128)(2,1)S(1)}, u32[]{:S(2)}, u32[]{:S(2)}) collective-permute-start(bf16[192,2048]{1,0:T(8,128)(2,1)S(1)} %get-tuple-element.140), channel_id=1, source_target_pairs={{0,4},{4,0},{8,12},{12,8},{16,20},{20,16},{24,28},{28,24},{1,5},{5... | collective-permute-start | bytes 2359304 | tf_op jit(solution)/shard_map/ppermute | solution.py:351
  529.6 66.4 %collective-permute-start.112 = (bf16[128,1536]{1,0:T(8,128)(2,1)S(1)}, bf16[128,1536]{1,0:T(8,128)(2,1)S(1)}, u32[]{:S(2)}, u32[]{:S(2)}) collective-permute-start(bf16[128,1536]{1,0:T(8,128)(2,1)S(1)} %get-tuple-element.191), channel_id=1, source_target_pairs={{1,0},{2,1},{3,2},{5,4},{6,5},{7,6},{9,8},{10,9},{11,10},{13,12},{... | collective-permute-start | bytes 1179656 | tf_op jit(solution)/shard_map/ppermute | solution.py:479
  587.4 35.4 %collective-permute-start.88 = (bf16[128,1536]{1,0:T(8,128)(2,1)S(1)}, bf16[128,1536]{1,0:T(8,128)(2,1)S(1)}, u32[]{:S(2)}, u32[]{:S(2)}) collective-permute-start(bf16[128,1536]{1,0:T(8,128)(2,1)S(1)} %get-tuple-element.183), channel_id=1, source_target_pairs={{1,0},{2,1},{3,2},{5,4},{6,5},{7,6},{9,8},{10,9},{11,10},{13,12},{... | collective-permute-start | bytes 1179656 | tf_op jit(solution)/shard_map/ppermute | solution.py:479
  622.9 36.1 %collective-permute-start.111 = (bf16[128,1536]{1,0:T(8,128)(2,1)S(1)}, bf16[128,1536]{1,0:T(8,128)(2,1)S(1)}, u32[]{:S(2)}, u32[]{:S(2)}) collective-permute-start(bf16[128,1536]{1,0:T(8,128)(2,1)S(1)} %get-tuple-element.188), channel_id=1, source_target_pairs={{0,1},{1,2},{2,3},{4,5},{5,6},{6,7},{8,9},{9,10},{10,11},{12,13},{... | collective-permute-start | bytes 1179656 | tf_op jit(solution)/shard_map/ppermute | solution.py:478
  691.7 30.6 %collective-permute-start.159 = (bf16[192,2048]{1,0:T(8,128)(2,1)S(1)}, bf16[192,2048]{1,0:T(8,128)(2,1)S(1)}, u32[]{:S(2)}, u32[]{:S(2)}) collective-permute-start(bf16[192,2048]{1,0:T(8,128)(2,1)S(1)} %pad_maximum_fusion.3), channel_id=1, source_target_pairs={{0,16},{4,20},{8,24},{12,28},{16,0},{20,4},{24,8},{28,12},{1,17},{... | collective-permute-start | bytes 2359304 | tf_op jit(solution)/shard_map/ppermute | solution.py:351
  817.4 55.3 %collective-permute-start.143 = (bf16[48,1536]{1,0:T(8,128)(2,1)}, bf16[48,1536]{1,0:T(8,128)(2,1)}, u32[]{:S(2)}, u32[]{:S(2)}) collective-permute-start(bf16[48,1536]{1,0:T(8,128)(2,1)} %get-tuple-element.208), channel_id=1, source_target_pairs={{0,4},{4,0},{8,12},{12,8},{16,20},{20,16},{24,28},{28,24},{1,5},{5... | collective-permute-start | bytes 442376 | tf_op jit(solution)/shard_map/ppermute | solution.py:351
  834.6 53.4 %collective-permute-start.133 = (bf16[192,1152]{1,0:T(8,128)(2,1)}, bf16[192,1152]{1,0:T(8,128)(2,1)}, u32[]{:S(2)}, u32[]{:S(2)}) collective-permute-start(bf16[192,1152]{1,0:T(8,128)(2,1)} %copy.118), channel_id=1, source_target_pairs={{0,4},{4,0},{8,12},{12,8},{16,20},{20,16},{24,28},{28,24},{1,5},{5... | collective-permute-start | bytes 1327112 | tf_op jit(solution)/shard_map/ppermute | solution.py:351
  862.1 33.7 %collective-permute-start.134 = (bf16[192,1152]{1,0:T(8,128)(2,1)}, bf16[192,1152]{1,0:T(8,128)(2,1)}, u32[]{:S(2)}, u32[]{:S(2)}) collective-permute-start(bf16[192,1152]{1,0:T(8,128)(2,1)} %copy.120), channel_id=1, source_target_pairs={{0,4},{4,0},{8,12},{12,8},{16,20},{20,16},{24,28},{28,24},{1,5},{5... | collective-permute-start | bytes 1327112 | tf_op jit(solution)/shard_map/ppermute | solution.py:351
  873.2 80.1 %collective-permute-start.132 = (bf16[192,1152]{1,0:T(8,128)(2,1)}, bf16[192,1152]{1,0:T(8,128)(2,1)}, u32[]{:S(2)}, u32[]{:S(2)}) collective-permute-start(bf16[192,1152]{1,0:T(8,128)(2,1)} %copy.117), channel_id=1, source_target_pairs={{0,4},{4,0},{8,12},{12,8},{16,20},{20,16},{24,28},{28,24},{1,5},{5... | collective-permute-start | bytes 1327112 | tf_op jit(solution)/shard_map/ppermute | solution.py:351
  884.9 51.5 %collective-permute-start.124 = (bf16[128,1536]{1,0:T(8,128)(2,1)}, bf16[128,1536]{1,0:T(8,128)(2,1)}, u32[]{:S(2)}, u32[]{:S(2)}) collective-permute-start(bf16[128,1536]{1,0:T(8,128)(2,1)} %get-tuple-element.187), channel_id=1, source_target_pairs={{1,0},{2,1},{3,2},{5,4},{6,5},{7,6},{9,8},{10,9},{11,10},{13,12},{... | collective-permute-start | bytes 1179656 | tf_op jit(solution)/shard_map/ppermute | solution.py:479
  895.8 48.0 %collective-permute-start.100 = (bf16[128,1536]{1,0:T(8,128)(2,1)}, bf16[128,1536]{1,0:T(8,128)(2,1)}, u32[]{:S(2)}, u32[]{:S(2)}) collective-permute-start(bf16[128,1536]{1,0:T(8,128)(2,1)} %get-tuple-element.179), channel_id=1, source_target_pairs={{1,0},{2,1},{3,2},{5,4},{6,5},{7,6},{9,8},{10,9},{11,10},{13,12},{... | collective-permute-start | bytes 1179656 | tf_op jit(solution)/shard_map/ppermute | solution.py:479
  899.1 33.4 %collective-permute-start.151 = (f32[48,1536]{1,0:T(8,128)}, f32[48,1536]{1,0:T(8,128)}, u32[]{:S(2)}, u32[]{:S(2)}) collective-permute-start(f32[48,1536]{1,0:T(8,128)} %convert_add_fusion.11), channel_id=1, source_target_pairs={{0,0},{4,1},{8,2},{12,3},{16,4},{20,5},{24,6},{28,7},{1,8},{5,9},{... | collective-permute-start | bytes 884744 | tf_op jit(solution)/shard_map/ppermute | solution.py:660
  947.1 47.3 %collective-permute-start.123 = (bf16[128,1536]{1,0:T(8,128)(2,1)}, bf16[128,1536]{1,0:T(8,128)(2,1)S(1)}, u32[]{:S(2)}, u32[]{:S(2)}) collective-permute-start(bf16[128,1536]{1,0:T(8,128)(2,1)} %get-tuple-element.184), channel_id=1, source_target_pairs={{0,1},{1,2},{2,3},{4,5},{5,6},{6,7},{8,9},{9,10},{10,11},{12,13},{... | collective-permute-start | bytes 1179656 | tf_op jit(solution)/shard_map/ppermute | solution.py:478
  954.7 39.7 %collective-permute-start.99 = (bf16[128,1536]{1,0:T(8,128)(2,1)}, bf16[128,1536]{1,0:T(8,128)(2,1)S(1)}, u32[]{:S(2)}, u32[]{:S(2)}) collective-permute-start(bf16[128,1536]{1,0:T(8,128)(2,1)} %get-tuple-element.176), channel_id=1, source_target_pairs={{0,1},{1,2},{2,3},{4,5},{5,6},{6,7},{8,9},{9,10},{10,11},{12,13},{... | collective-permute-start | bytes 1179656 | tf_op jit(solution)/shard_map/ppermute | solution.py:478
  (197 other events, 2838.4 us)

commit v2 on v1

v2 whole, which is shorter than its diff:
```python
import math

import jax
import jax.numpy as jnp
from jax import lax
from jax.experimental import pallas as pl
from jax.experimental.pallas import tpu as pltpu
from jax.sharding import PartitionSpec as P

H = 16
DH = 96
QUERY_TAPS = 6
KEY_TAPS = 11
REACH = KEY_TAPS // 2
TILE = 128
PAD = 16
bf16 = jnp.bfloat16
f32 = jnp.float32


def nn(left, right):
    return lax.dot_general(left, right, (((1,), (0,)), ((), ())), preferred_element_type=f32)


def nt(left, right):
    return lax.dot_general(left, right, (((1,), (1,)), ((), ())), preferred_element_type=f32)


def tn(left, right):
    return lax.dot_general(left, right, (((0,), (0,)), ((), ())), preferred_element_type=f32)


def lanes_of(begin, width):
    lane = lax.broadcasted_iota(jnp.int32, (1, width), 1)
    return jnp.logical_and(lane >= begin, lane < begin + DH).astype(f32)


def split(value):
    high = value.astype(bf16)
    return high, (value - high.astype(f32)).astype(bf16)


def fill_bands(kern_ref, base, bands, low_bands, offset):
    row = lax.broadcasted_iota(jnp.int32, (2 * TILE, TILE), 0)
    col = lax.broadcasted_iota(jnp.int32, (2 * TILE, TILE), 1)
    tap = offset(row, col)
    for lag in range(QUERY_TAPS):
        band = jnp.zeros((2 * TILE, TILE), f32)
        for key_lag in range(KEY_TAPS):
            band = jnp.where(tap == key_lag, kern_ref[base + lag * KEY_TAPS + key_lag], band)
        high, low = split(band)
        bands[:, lag * TILE : (lag + 1) * TILE] = high
        if low_bands is not None:
            low_bands[:, lag * TILE : (lag + 1) * TILE] = low


def valid_keys(first_query, rows, first_key):
    query = lax.broadcasted_iota(jnp.int32, (rows, TILE), 0) + first_query
    key = lax.broadcasted_iota(jnp.int32, (rows, TILE), 1) + (first_key - REACH)
    return jnp.logical_and(key >= 0, key <= query)


def shift_keys(keys, kx_ref):
    tail = jnp.zeros((TILE, keys.shape[1]), f32)
    moved = jnp.concatenate([keys.astype(f32), tail], axis=0)
    kx_ref[...] = pltpu.roll(moved, REACH, 0).astype(bf16)


def norm_parts(heads):
    masks = [lanes_of(head * DH, heads.shape[1]) for head in range(heads.shape[1] // DH)]
    means = jnp.zeros_like(heads)
    for mask in masks:
        means = means + mask * (jnp.sum(heads * mask, axis=1, keepdims=True) / DH)
    centred = heads - means
    inverse = jnp.zeros_like(heads)
    for mask in masks:
        spread = jnp.sum(centred * centred * mask, axis=1, keepdims=True) / DH
        inverse = inverse + mask * lax.rsqrt(spread + 1e-05)
    return centred, inverse, masks


def pair_slice(pair, local, part):
    span = min(2 * TILE, local)
    start = (3 * pair) // 2 * TILE
    if not isinstance(pair, int):
        start = pl.multiple_of(start, TILE)
    return pl.ds(part * local + start, span), pair * 2 * DH - start


def attend_fwd_body(
    kern_ref, mix_ref, qkv_ref, gain_ref,
    joined_ref, heads_ref, p_ref,
    high_ref, low_ref, bands_ref, low_bands_ref, kx_ref,
):
    length = qkv_ref.shape[1]
    local = heads_ref.shape[2]
    span_pair = kx_ref.shape[1]
    tiles = length // TILE
    pairs = local // (2 * DH)
    scale = 1.0 / math.sqrt(DH)

    @pl.when(pl.program_id(0) == 0)
    def _():
        high_ref[...] = jnp.zeros_like(high_ref)
        low_ref[...] = jnp.zeros_like(low_ref)

    heads_ref[...] = jnp.zeros_like(heads_ref)

    def one_pair(pair, carry):
        q_at, offset = pair_slice(pair, local, 0)
        k_at, _ = pair_slice(pair, local, 1)
        v_at, _ = pair_slice(pair, local, 2)
        h_at, _ = pair_slice(pair, local, 0)
        shift_keys(qkv_ref[0, :, k_at], kx_ref)

        def one_head(head, inner):
            base = (pair * 2 + head) * (QUERY_TAPS * KEY_TAPS)
            fill_bands(
                kern_ref, base, bands_ref, low_bands_ref, lambda row, col: (KEY_TAPS - 1) - (row - col)
            )
            query = qkv_ref[0, :, q_at] * lanes_of(offset + head * DH, span_pair).astype(bf16)
            for tile in range(tiles + 1):
                at = slice(tile * TILE, (tile + 1) * TILE)
                first = max(0, tile * TILE - PAD)
                scores = nt(query[first:], kx_ref[at, :]) * scale
                masked = jnp.where(valid_keys(first, length - first, tile * TILE), scores, 0.0)
                high, low = split(masked)
                high_ref[first + PAD :, at] = high
                low_ref[first + PAD :, at] = low
            for tile in range(tiles):
                first = tile * TILE
                high = high_ref[first:, first : first + 2 * TILE]
                low = low_ref[first:, first : first + 2 * TILE]
                bands = bands_ref[...]
                wide = nn(high, bands) + nn(low, bands) + nn(high, low_bands_ref[...])
                total = wide[:, :TILE]
                for lag in range(1, QUERY_TAPS):
                    total = total + pltpu.roll(wide[:, lag * TILE : (lag + 1) * TILE], lag, 0)
                p_ref[0, pair, head, first:, first : first + TILE] = total[PAD:]
            return inner

        lax.fori_loop(0, 2, one_head, 0)
        for tile in range(tiles):
            first = tile * TILE
            span = first + TILE
            query = lax.broadcasted_iota(jnp.int32, (TILE, span), 0) + first
            key = lax.broadcasted_iota(jnp.int32, (TILE, span), 1)
            valid = key <= query
            probs = []
            for head in range(2):
                logits = jnp.where(valid, p_ref[0, pair, head, first:span, :span], -1e30)
                top = jnp.max(logits, axis=1, keepdims=True)
                expon = jnp.where(valid, jnp.exp(logits - top), 0.0)
                prob = expon / jnp.sum(expon, axis=1, keepdims=True)
                p_ref[0, pair, head, first:span, :span] = prob
                probs.append(prob)
            out = heads_ref[0, first:span, h_at]
            for head in range(2):
                spot = (pair * 2 + head) * 2
                mixed = (mix_ref[spot] * probs[0] + mix_ref[spot + 1] * probs[1]).astype(bf16)
                mask = lanes_of(offset + head * DH, span_pair).astype(bf16)
                out = out + nn(mixed, qkv_ref[0, :span, v_at] * mask)
            heads_ref[0, first:span, h_at] = out
        return carry

    if pairs == 1:
        one_pair(0, 0)
    else:
        lax.fori_loop(0, pairs, one_pair, 0)
    for tile in range(tiles):
        at = slice(tile * TILE, (tile + 1) * TILE)
        centred, inverse, _ = norm_parts(heads_ref[0, at, :])
        joined_ref[0, at, :] = (centred * inverse * gain_ref[...]).astype(bf16)


def attend_bwd_body(
    kern_ref, mix_ref, qkv_ref, gain_ref, heads_ref, p_ref, dj_ref,
    dqkv_ref, gk_ref, gmix_ref, ggain_ref,
    d_ref, dlow_ref, mixed_ref, mt_ref, bands_ref, do_ref, acc_ref, corr_ref, kx_ref, dka_ref,
):
    length = qkv_ref.shape[1]
    local = heads_ref.shape[2]
    span_pair = kx_ref.shape[1]
    tiles = length // TILE
    pairs = local // (2 * DH)
    scale = 1.0 / math.sqrt(DH)
    lane = lax.broadcasted_iota(jnp.int32, (1, TILE), 1)

    @pl.when(pl.program_id(0) == 0)
    def _():
        d_ref[...] = jnp.zeros_like(d_ref)
        dlow_ref[...] = jnp.zeros_like(dlow_ref)
        mt_ref[...] = jnp.zeros_like(mt_ref)
        corr_ref[...] = jnp.zeros_like(corr_ref)
        gmix_ref[...] = jnp.zeros_like(gmix_ref)
        ggain_ref[...] = jnp.zeros_like(ggain_ref)

    gain_total = jnp.zeros((1, local), f32)
    for tile in range(tiles):
        at = slice(tile * TILE, (tile + 1) * TILE)
        centred, inverse, masks = norm_parts(heads_ref[0, at, :])
        unit = centred * inverse
        outer = dj_ref[0, at, :].astype(f32)
        gain_total = gain_total + jnp.sum(outer * unit, axis=0, keepdims=True)
        inner = outer * gain_ref[...]
        result = inner
        for mask in masks:
            mean = jnp.sum(inner * mask, axis=1, keepdims=True) / DH
            along = jnp.sum(inner * unit * mask, axis=1, keepdims=True) / DH
            result = result - mask * (mean + unit * along)
        do_ref[at, :] = (result * inverse).astype(bf16)
    ggain_ref[...] = ggain_ref[...] + gain_total
    acc_ref[...] = jnp.zeros_like(acc_ref)

    def one_pair(pair, carry):
        q_at, offset = pair_slice(pair, local, 0)
        k_at, _ = pair_slice(pair, local, 1)
        v_at, _ = pair_slice(pair, local, 2)
        h_at, _ = pair_slice(pair, local, 0)
        shift_keys(qkv_ref[0, :, k_at], kx_ref)
        dka_ref[...] = jnp.zeros_like(dka_ref)
        sums = [[jnp.zeros((1, 1), f32) for _ in range(2)] for _ in range(2)]
        mix = [[mix_ref[(pair * 2 + head) * 2 + other] for other in range(2)] for head in range(2)]
        head_masks = [lanes_of(offset + head * DH, span_pair).astype(bf16) for head in range(2)]
        for tile in range(tiles):
            first = tile * TILE
            span = first + TILE
            query = lax.broadcasted_iota(jnp.int32, (TILE, span), 0) + first
            valid = lax.broadcasted_iota(jnp.int32, (TILE, span), 1) <= query
            probs = [
                jnp.where(valid, p_ref[0, pair, head, first:span, :span], 0.0) for head in range(2)
            ]
            grads = []
            for head in range(2):
                mixed = (mix[head][0] * probs[0] + mix[head][1] * probs[1]).astype(bf16)
                mixed_ref[head, first:span, :span] = mixed
                grads.append(nt(do_ref[first:span, h_at] * head_masks[head], qkv_ref[0, :span, v_at]))
            for other in range(2):
                row_sum = jnp.zeros((TILE, 1), f32)
                for head in range(2):
                    along = jnp.sum(grads[head] * probs[other], axis=1, keepdims=True)
                    sums[head][other] = sums[head][other] + jnp.sum(along, axis=0, keepdims=True)
                    row_sum = row_sum + mix[head][other] * along
                outer = mix[0][other] * grads[0] + mix[1][other] * grads[1]
                inner = probs[other] * (outer - row_sum)
                d_ref[other, first + PAD : span + PAD, :span] = inner
                dlow_ref[other, first + PAD : span + PAD, :span] = inner.astype(bf16)
        spread = jnp.zeros((1, TILE), f32)
        for head in range(2):
            for other in range(2):
                spread = spread + jnp.where(
                    lane == pair * 4 + head * 2 + other, sums[head][other], 0.0
                )
        gmix_ref[...] = gmix_ref[...] + spread

        for tile in range(tiles):
            first = tile * TILE
            at = slice(first, first + TILE)
            total = acc_ref[at, v_at]
            for head in range(2):
                total = total + tn(mixed_ref[head, first:, at], do_ref[first:, h_at] * head_masks[head])
            acc_ref[at, v_at] = total

        def one_head(head, inner):
            base = (pair * 2 + head) * (QUERY_TAPS * KEY_TAPS)
            fill_bands(
                kern_ref, base, bands_ref, None, lambda row, col: row - TILE - col + (KEY_TAPS - 1)
            )
            lanes = lanes_of(offset + head * DH, span_pair).astype(bf16)
            query = qkv_ref[0, :, q_at] * lanes
            for tile in range(tiles + 1):
                start = max(0, tile - 1) * TILE
                at = slice(tile * TILE, (tile + 1) * TILE)
                scores = nt(kx_ref[at, :], query[start:]) * scale
                key = lax.broadcasted_iota(jnp.int32, (TILE, length - start), 0) + (tile * TILE - REACH)
                pos = lax.broadcasted_iota(jnp.int32, (TILE, length - start), 1) + start
                valid = jnp.logical_and(key >= 0, key <= pos)
                mt_ref[at, start:] = jnp.where(valid, scores, 0.0).astype(bf16)
            total_corr = corr_ref[pair * 2 + head]
            for tile in range(tiles):
                start = max(0, tile - 1) * TILE
                count = length - start
                source = d_ref[head, start + PAD :, tile * TILE : (tile + 1) * TILE]
                moved = [source[:count].astype(bf16)]
                for lag in range(1, QUERY_TAPS):
                    moved.append(pltpu.roll(source, source.shape[0] - lag, 0)[:count].astype(bf16))
                stacked = jnp.concatenate(moved, axis=1)
                total_corr = total_corr + nn(mt_ref[tile * TILE : (tile + 2) * TILE, start:], stacked)
            corr_ref[pair * 2 + head] = total_corr
            for tile in range(tiles + 1):
                first = tile * TILE
                at = slice(first, first + TILE)
                if tile == 0:
                    wide = nn(dlow_ref[head, first:, :TILE], bands_ref[TILE:, :])
                elif tile == tiles:
                    wide = nn(dlow_ref[head, first:, first - TILE : first], bands_ref[:TILE, :])
                else:
                    wide = nn(dlow_ref[head, first:, first - TILE : first + TILE], bands_ref[...])
                total = wide[:, :TILE]
                rows = wide.shape[0]
                for lag in range(1, QUERY_TAPS):
                    total = total + pltpu.roll(wide[:, lag * TILE : (lag + 1) * TILE], rows - lag, 0)
                begin = max(0, first - PAD)
                total = total[begin - (first - PAD) : rows - PAD]
                grad = jnp.where(valid_keys(begin, length - begin, first), total, 0.0).astype(bf16)
                acc_ref[begin:, q_at] = acc_ref[begin:, q_at] + nn(grad, kx_ref[at, :] * lanes) * scale
                dka_ref[at, :] = dka_ref[at, :] + tn(grad, query[begin:])
            return inner

        lax.fori_loop(0, 2, one_head, 0)
        keys = dka_ref[...]
        back = pltpu.roll(keys, keys.shape[0] - REACH, 0)[:length] * scale
        acc_ref[:, k_at] = acc_ref[:, k_at] + back
        return carry

    if pairs == 1:
        one_pair(0, 0)
    else:
        lax.fori_loop(0, pairs, one_pair, 0)
    dqkv_ref[0] = acc_ref[...].astype(bf16)

    @pl.when(pl.program_id(0) == pl.num_programs(0) - 1)
    def _():
        row = lax.broadcasted_iota(jnp.int32, (2 * TILE, QUERY_TAPS * TILE), 0)
        col = lax.broadcasted_iota(jnp.int32, (2 * TILE, QUERY_TAPS * TILE), 1) % TILE

        def one_head(head, carry):
            corr = corr_ref[head]
            taps = [
                jnp.sum(jnp.where(row - col == (KEY_TAPS - 1) - key_lag, corr, 0.0), axis=0, keepdims=True)
                for key_lag in range(KEY_TAPS)
            ]
            taps.append(jnp.zeros((16 - KEY_TAPS, QUERY_TAPS * TILE), f32))
            gk_ref[head] = jnp.concatenate(taps, axis=0)
            return carry

        lax.fori_loop(0, 2 * pairs, one_head, 0)


def attend_fwd(kern, mix, qkv, gain):
    seqs, length, width = qkv.shape
    local = width // 3
    pairs = local // (2 * DH)
    smem = pl.BlockSpec(memory_space=pltpu.SMEM)
    one = pl.BlockSpec((1, length, local), lambda s: (s, 0, 0))
    return pl.pallas_call(
        attend_fwd_body,
        grid=(seqs,),
        in_specs=[
            smem,
            smem,
            pl.BlockSpec((1, length, width), lambda s: (s, 0, 0)),
            pl.BlockSpec((1, local), lambda s: (0, 0)),
        ],
        out_specs=[one, one, pl.BlockSpec((1, pairs, 2, length, length), lambda s: (s, 0, 0, 0, 0))],
        out_shape=[
            jax.ShapeDtypeStruct((seqs, length, local), bf16),
            jax.ShapeDtypeStruct((seqs, length, local), f32),
            jax.ShapeDtypeStruct((seqs, pairs, 2, length, length), f32),
        ],
        scratch_shapes=[
            pltpu.VMEM((length + PAD, length + TILE), bf16),
            pltpu.VMEM((length + PAD, length + TILE), bf16),
            pltpu.VMEM((2 * TILE, QUERY_TAPS * TILE), bf16),
            pltpu.VMEM((2 * TILE, QUERY_TAPS * TILE), bf16),
            pltpu.VMEM((length + TILE, min(2 * TILE, local)), bf16),
        ],
        name="attend_fwd",
    )(kern, mix, qkv, gain)


def attend_bwd(kern, mix, qkv, gain, heads, probs, outer):
    seqs, length, width = qkv.shape
    local = width // 3
    pairs = local // (2 * DH)
    span_pair = min(2 * TILE, local)
    smem = pl.BlockSpec(memory_space=pltpu.SMEM)
    one = pl.BlockSpec((1, length, local), lambda s: (s, 0, 0))
    wide = pl.BlockSpec((1, length, width), lambda s: (s, 0, 0))
    return pl.pallas_call(
        attend_bwd_body,
        grid=(seqs,),
        in_specs=[
            smem,
            smem,
            wide,
            pl.BlockSpec((1, local), lambda s: (0, 0)),
            one,
            pl.BlockSpec((1, pairs, 2, length, length), lambda s: (s, 0, 0, 0, 0)),
            one,
        ],
        out_specs=[
            wide,
            pl.BlockSpec((2 * pairs, 16, QUERY_TAPS * TILE), lambda s: (0, 0, 0)),
            pl.BlockSpec((1, TILE), lambda s: (0, 0)),
            pl.BlockSpec((1, local), lambda s: (0, 0)),
        ],
        out_shape=[
            jax.ShapeDtypeStruct(qkv.shape, bf16),
            jax.ShapeDtypeStruct((2 * pairs, 16, QUERY_TAPS * TILE), f32),
            jax.ShapeDtypeStruct((1, TILE), f32),
            jax.ShapeDtypeStruct((1, local), f32),
        ],
        scratch_shapes=[
            pltpu.VMEM((2, length + 2 * PAD, length), f32),
            pltpu.VMEM((2, length + 2 * PAD, length), bf16),
            pltpu.VMEM((2, length, length), bf16),
            pltpu.VMEM((length + TILE, length), bf16),
            pltpu.VMEM((2 * TILE, QUERY_TAPS * TILE), bf16),
            pltpu.VMEM((length, local), bf16),
            pltpu.VMEM((length, width), f32),
            pltpu.VMEM((2 * pairs, 2 * TILE, QUERY_TAPS * TILE), f32),
            pltpu.VMEM((length + TILE, span_pair), bf16),
            pltpu.VMEM((length + TILE, span_pair), f32),
        ],
        name="attend_bwd",
    )(kern, mix, qkv, gain, heads, probs, outer)


def xor_perm(count, bit):
    return [(index, index ^ bit) for index in range(count)]


def swap(value, axis, bit):
    return lax.ppermute(value, axis, xor_perm(lax.axis_size(axis), bit))


def batch_gather(value):
    return lax.all_gather(value, "batch", axis=0, tiled=True)


def batch_scatter(value):
    return lax.psum_scatter(value, "batch", scatter_dimension=0, tiled=True)


def ring_perms():
    count = lax.axis_size("seq")
    ahead = []
    for pair in range(lax.axis_size("batch") // 2):
        line = [2 * pair * count + index for index in range(count)]
        ring = line + [index + count for index in reversed(line)]
        ahead += [(here, ring[(step + 1) % len(ring)]) for step, here in enumerate(ring)]
    return ahead, [(there, here) for here, there in ahead]


def ring_side():
    return 1 - 2 * (lax.axis_index("batch") % 2)


def seq_gather(value, hops=None):
    count = lax.axis_size("seq")
    here = lax.axis_index("seq")
    side = ring_side()
    ahead, back = ring_perms()
    rows = value.shape[0]
    first, second = [value], [value]
    for _ in range(count - 1):
        first.append(lax.ppermute(first[-1], ("batch", "seq"), ahead))
        second.append(lax.ppermute(second[-1], ("batch", "seq"), back))
    if hops is not None:
        hops += [(one, two) for one, two in zip(first[1:], second[1:])]
    out = jnp.zeros((count * rows, value.shape[1]), value.dtype)
    out = lax.dynamic_update_slice(out, value, (here * rows, 0))
    for step in range(1, count):
        source = here - side * step
        near = jnp.logical_and(source >= 0, source < count)
        piece = jnp.where(near, first[step], second[count - step])
        out = lax.dynamic_update_slice(out, piece, ((source % count) * rows, 0))
    return out


def seq_scatter(value):
    count = lax.axis_size("seq")
    here = lax.axis_index("seq")
    side = ring_side()
    ahead, back = ring_perms()
    rows = value.shape[0] // count
    low, high = here == 0, here == count - 1
    skip_first = jnp.where(side > 0, low, high)
    skip_second = jnp.where(side > 0, high, low)

    def block(index):
        return lax.dynamic_slice_in_dim(value, jnp.clip(index, 0, count - 1) * rows, rows, 0)

    def came(piece, skip):
        return jnp.where(skip, 0.0, piece.astype(f32))

    first = second = None
    for step in range(1, count):
        far = side * (count - step)
        one, two = block(here + far), block(here - far)
        if first is not None:
            one = (one.astype(f32) + came(first, skip_first)).astype(bf16)
            two = (two.astype(f32) + came(second, skip_second)).astype(bf16)
        first = lax.ppermute(one, ("batch", "seq"), ahead)
        second = lax.ppermute(two, ("batch", "seq"), back)
    return block(here).astype(f32) + came(first, skip_first) + came(second, skip_second)


def seq_swap(blocks):
    count = lax.axis_size("seq")
    here = lax.axis_index("seq")
    out = jnp.zeros_like(blocks)
    own = lax.dynamic_index_in_dim(blocks, here, 0, True)
    out = lax.dynamic_update_slice_in_dim(out, own, here, 0)
    for step in range(1, count):
        piece = lax.dynamic_index_in_dim(blocks, (here + step) % count, 0, True)
        perm = [(index, (index + step) % count) for index in range(count)]
        piece = lax.ppermute(piece, "seq", perm)
        out = lax.dynamic_update_slice_in_dim(out, piece, (here - step) % count, 0)
    return out


def after(value, *others):
    return lax.optimization_barrier((value, *others))[0]


def all_sum(value, axes=("batch", "seq")):
    for axis in axes:
        bit = 1
        while bit < lax.axis_size(axis):
            value = value + swap(value, axis, bit)
            bit *= 2
    return value


def inverse_rms(values):
    return lax.rsqrt(jnp.mean(values * values, axis=-1, keepdims=True) + 1e-06)


def rms_back(values, inverse, inner):
    along = jnp.mean(values * inner, axis=-1, keepdims=True)
    return inverse * (inner - values * (inverse * inverse) * along)


def per_device(
    inputs,
    output_grad,
    source_tags,
    source_counts,
    gain_in,
    w_query,
    w_key,
    w_value,
    kernel,
    mixing,
    gain_head,
    w_out,
    gain_mid,
    w_gate,
    w_up,
    w_down,
):
    seqs, seg, width = inputs.shape
    parts = lax.axis_size("seq")
    lanes = lax.axis_size("batch")
    place_seq = lax.axis_index("seq")
    place_batch = lax.axis_index("batch")
    length = seg * parts
    groups = H // (2 * parts)
    local = groups * 2 * DH
    own = w_query.shape[0]
    blocks = parts * lanes

    gains = jnp.stack([gain_in, gain_head, gain_mid]).astype(f32)
    gains = lax.dynamic_update_slice_in_dim(
        jnp.zeros((3, width), f32), gains, (place_batch * parts + place_seq) * own, 1
    )
    gains = all_sum(gains.reshape(-1, 128), ("seq",))
    joint = jnp.stack([w_query, w_key, w_value], axis=1).reshape(own, 3, parts, local)
    joint = joint.transpose(2, 0, 1, 3).reshape(parts, own, 3 * local)
    joint = seq_swap(joint).reshape(parts * own, 3 * local)
    all_gains = all_sum(gains, ("batch",))
    hops = []
    x_all = [seq_gather(inputs[0], hops)]
    for index in range(1, seqs):
        x_all.append(seq_gather(after(inputs[index], hops[-2])))
    joint = after(joint, all_gains, hops[0])
    w_joint = batch_gather(joint)
    all_gains = all_gains.reshape(3, 1, width)
    gain_in32, gain_head32, gain_mid32 = all_gains[0], all_gains[1], all_gains[2]
    gain_own = lax.dynamic_slice_in_dim(gain_head32, place_seq * local, local, 1)
    kern_own = lax.dynamic_slice_in_dim(
        kernel.reshape(-1), place_seq * (2 * groups * QUERY_TAPS * KEY_TAPS), 2 * groups * QUERY_TAPS * KEY_TAPS, 0
    )
    mix_own = lax.dynamic_slice_in_dim(mixing.reshape(-1), place_seq * 4 * groups, 4 * groups, 0)

    order = [
        (index, (index % lanes) * parts + index // lanes) for index in range(blocks)
    ]
    w_join = batch_gather(lax.ppermute(after(w_out, x_all[0]), ("batch", "seq"), order))
    w_gate_up = batch_gather(jnp.concatenate([w_gate, w_up], axis=1))
    w_down_t = batch_gather(w_down.T)
    hidden_width = w_gate.shape[1]
    o_all = [lax.all_gather(output_grad[index], "seq", axis=0, tiled=True) for index in range(seqs)]

    source_ids = jnp.arange(source_counts.shape[0], dtype=jnp.int32)
    tag_count = jnp.sum(
        jnp.where(source_tags[:, None] == source_ids[None, :], source_counts[None, :], 0), axis=1
    )
    factor = length / tag_count.astype(f32)

    outputs, input_grads = [], []
    keep = []
    for index in range(seqs):
        x32 = x_all[index].astype(f32)
        x_inverse = inverse_rms(x32)
        normed = (x32 * x_inverse * gain_in32).astype(bf16)
        qkv = nn(normed, w_joint).astype(bf16)[None]
        joined, heads, probs = attend_fwd(kern_own, mix_own, qkv, gain_own)
        middle = inputs[index].astype(f32) + seq_scatter(nn(joined[0], w_join).astype(bf16))
        keep.append([x_inverse, normed, qkv, joined, heads, probs, middle])
    gain_mid_grad = jnp.zeros((1, width), f32)
    gain_in_grad = jnp.zeros((1, width), f32)
    ffn = []
    mid_parts = []
    results = []
    for index in range(seqs):
        middle = keep[index][-1]
        mid_inverse = inverse_rms(middle)
        n_all = seq_gather((middle * mid_inverse * gain_mid32).astype(bf16))
        both = nn(n_all, w_gate_up)
        gate, upward = both[:, :hidden_width], both[:, hidden_width:]
        sigma = 1.0 / (1.0 + jnp.exp(-gate))
        silu = gate * sigma
        hidden = (silu * upward).astype(bf16)
        down_in = (o_all[index].astype(f32) * factor[index]).astype(bf16)
        hidden_grad = nn(down_in, w_down_t)
        gate_grad = (hidden_grad * upward * (sigma * (1.0 + gate * (1.0 - sigma)))).astype(bf16)
        up_grad = (hidden_grad * silu).astype(bf16)
        grads = jnp.concatenate([gate_grad, up_grad], axis=1)
        mid_parts.append(seq_scatter(nt(grads, w_gate_up).astype(bf16)))
        ffn.append((n_all, hidden, down_in, grads))
    cat = lambda place: jnp.concatenate([item[place] for item in ffn], axis=0)
    all_n, all_hidden, all_down, all_grads = cat(0), cat(1), cat(2), cat(3)
    g_gate_up = tn(all_n, all_grads).astype(bf16)
    g_down_t = tn(all_down, all_hidden).astype(bf16)
    mid_parts = after(mid_parts, g_gate_up, g_down_t)
    g_gate_up = batch_scatter(g_gate_up)
    g_down_t = batch_scatter(g_down_t)
    for index in range(seqs):
        middle = keep[index][-1]
        mid_inverse = inverse_rms(middle)
        mid_grad = mid_parts[index]
        unit = middle * mid_inverse
        gain_mid_grad = gain_mid_grad + jnp.sum(mid_grad * unit, axis=0, keepdims=True)
        cotangent = output_grad[index].astype(f32) * factor[index]
        middle_grad = cotangent + rms_back(middle, mid_inverse, mid_grad * gain_mid32)
        a_all = seq_gather(after(middle_grad.astype(bf16), g_gate_up))
        keep[index] += [middle_grad, a_all]
        part = after(nt(ffn[index][1], w_down_t).astype(bf16), a_all)
        results.append(lax.psum_scatter(part, "seq", scatter_dimension=0, tiled=True))
    back = []
    for index in range(seqs):
        x_inverse, normed, qkv, joined, heads, probs, middle, middle_grad, a_all = keep[index]
        outer = nt(a_all, w_join)[None]
        outer = after(outer, n_part, results[0]) if back else after(outer, g_down_t)
        dqkv, corr, mix_sum, head_sum = attend_bwd(
            kern_own, mix_own, qkv, gain_own, heads, probs, outer
        )
        n_part = nt(dqkv[0], w_joint)
        unit_all = x_all[index].astype(f32) * x_inverse
        gain_in_grad = gain_in_grad + jnp.sum(n_part * unit_all, axis=0, keepdims=True)
        n_grad = seq_scatter(n_part.astype(bf16))
        x32 = inputs[index].astype(f32)
        inner = rms_back(x32, inverse_rms(x32), n_grad * gain_in32)
        input_grads.append((middle_grad + inner).astype(bf16))
        back.append((normed, dqkv[0], joined[0], a_all, corr, mix_sum, head_sum))
    cat = lambda place: jnp.concatenate([item[place] for item in back], axis=0)
    all_normed, all_dqkv, all_joined, all_a = cat(0), cat(1), cat(2), cat(3)
    all_dqkv = after(all_dqkv, results[-1])
    all_a = after(all_a, all_dqkv)
    for index in range(seqs):
        middle = after(keep[index][6], back[-1][1])
        outputs.append((middle + results[index].astype(f32)).astype(bf16))
    g_out = batch_scatter(tn(all_joined, all_a).astype(bf16))
    g_out = lax.ppermute(g_out, ("batch", "seq"), [(there, here) for here, there in order])
    g_out = g_out.astype(f32)
    g_joint = batch_scatter(tn(all_normed, all_dqkv).astype(bf16))
    g_joint = seq_swap(g_joint.reshape(parts, own, 3 * local)).astype(f32)
    g_joint = g_joint.reshape(parts, own, 3, local).transpose(2, 1, 0, 3).reshape(3, own, width)

    corr = sum(item[4] for item in back)
    mix_sum = sum(item[5] for item in back)
    head_sum = sum(item[6] for item in back)
    taps = corr[:, :KEY_TAPS].reshape(2 * groups, KEY_TAPS, QUERY_TAPS, TILE)
    kern_grad = taps.sum(-1).transpose(0, 2, 1)
    mix_grad = mix_sum[0, : 4 * groups]
    head_grad = head_sum[0]

    def spread(value, total):
        return lax.dynamic_update_slice_in_dim(
            jnp.zeros((total,), f32), value.reshape(-1), place_seq * value.size, 0
        )

    small = jnp.concatenate(
        [
            gain_in_grad[0],
            gain_mid_grad[0],
            spread(head_grad, width),
            spread(kern_grad, H * QUERY_TAPS * KEY_TAPS),
            spread(mix_grad, H * 2),
        ]
    )
    size = small.size
    small = jnp.pad(small, (0, -size % 1024)).reshape(-1, 128)
    small = all_sum(small).reshape(-1)
    start = (place_batch * parts + place_seq) * own
    cuts = [lax.dynamic_slice_in_dim(small, start + step * width, own, 0) for step in range(3)]
    kernel_sum = small[3 * width : 3 * width + H * QUERY_TAPS * KEY_TAPS].reshape(kernel.shape)
    mixing_sum = small[3 * width + H * QUERY_TAPS * KEY_TAPS : size].reshape(mixing.shape)
    return (
        jnp.stack(outputs),
        jnp.stack(input_grads),
        cuts[0],
        g_joint[0],
        g_joint[1],
        g_joint[2],
        kernel_sum,
        mixing_sum,
        cuts[2],
        g_out,
        cuts[1],
        g_gate_up[:, :hidden_width].astype(f32),
        g_gate_up[:, hidden_width:].astype(f32),
        g_down_t.T.astype(f32),
    )


def solution(mesh):
    rows = P(("batch", "seq"))
    mats = P(("batch", "seq"), None)
    tokens = P("batch", "seq", None)
    in_specs = (
        tokens,
        tokens,
        P("batch"),
        P(),
        rows,
        mats,
        mats,
        mats,
        P(),
        P(),
        rows,
        mats,
        rows,
        P("batch", "seq"),
        P("batch", "seq"),
        P("seq", "batch"),
    )
    out_specs = (
        tokens,
        tokens,
        rows,
        mats,
        mats,
        mats,
        P(),
        P(),
        rows,
        mats,
        rows,
        P("batch", "seq"),
        P("batch", "seq"),
        P("seq", "batch"),
    )
    return jax.shard_map(
        per_device, mesh=mesh, in_specs=in_specs, out_specs=out_specs, check_vma=False
    )
```

time: 1020 us -> 726 us (0.71)
  starting transfers between devices: 339 us -> 143 us
  local copies, waits for them, and re-layouts: 179 us -> 40.9 us
  matrix products: 101 us -> 126 us
  between operations: 3.54 us -> 16.2 us
  other arithmetic: 73.9 us -> 84.3 us
    ppermute x97 -> x73, starting transfers between devices: 277 us -> 111 us  [the longest x18 35.4 us: seq_gather(): second.append(lax.ppermute(second[-1], ('batch', 'seq'), back))]
    ppermute x64 -> x10, waiting for transfers between devices: 48.3 us -> 7.44 us  [swap(): return lax.ppermute(value, axis, xor_perm(lax.axis_size(axis), bit))]
    dynamic_update_slice x29 -> x1, local copies, waits for them, and re-layouts: 33.6 us -> 0.16 us  [per_device(): lax.dynamic_update_slice_in_dim(jnp.zeros((3, width), f32), gains, (place...]
    ppermute x64 -> x10, starting transfers between devices: 51.4 us -> 18.1 us  [swap(): return lax.ppermute(value, axis, xor_perm(lax.axis_size(axis), bit))]
    slice x32 -> x4, local copies, waits for them, and re-layouts: 31.3 us -> 4.94 us  [the longest x2 4.15 us: per_device(): small[3 * width + H * QUERY_TAPS * KEY_TAPS:size].reshape(mixing.shape)]
    dot_general x20, matrix products: 101 us -> 126 us  [the longest x8 43.2 us: nt(): lax.dot_general(left, right, (((1,), (1,)), ((), ())), preferred_element_...]
    reduce_scatter x0 -> x6, waiting for transfers between devices: none -> 15.5 us  [the longest x4 15.5 us: batch_scatter(): return lax.psum_scatter(value, 'batch', scatter_dimension=0, tiled=True)]
    ppermute x97 -> x73, waiting for transfers between devices: 174 us -> 188 us  [the longest x18 102 us: seq_gather(): second.append(lax.ppermute(second[-1], ('batch', 'seq'), back))]
  transfers between devices with their start and end apart: 168 -> 102, of which waited for: 54 -> 41; matrix products, arithmetic and copies ran while one was open for 27% -> 29% of each run, Pallas kernels for 3% -> 11%
where the time goes in v2:
time: 726 us; the launch traced here: 717 us
  waiting for transfers between devices  228 us (31%)
  starting transfers between devices  143 us (20%)
  matrix products  126 us (17%)
  other arithmetic  84.3 us (12%)
  Pallas kernels  79 us (11%)
  local copies, waits for them, and re-layouts  40.9 us (6%)
  between operations  16.2 us (2%)
    ppermute x18, waiting for transfers between devices, seq_gather(): second.append(lax.ppermute(second[-1], ('batch', 'seq'), back))  102 us
    pallas_call x2, Pallas kernels, attend_bwd(): pl.pallas_call(attend_bwd_body, grid=(seqs,), in_specs=[smem, smem, wide,...  48.5 us
    dot_general x8, matrix products, nt(): lax.dot_general(left, right, (((1,), (1,)), ((), ())), preferred_element_...  43.2 us
    ppermute x18, waiting for transfers between devices, seq_scatter(): second = lax.ppermute(two, ('batch', 'seq'), back)  41.8 us
    dot_general x8, matrix products, nn(): lax.dot_general(left, right, (((1,), (0,)), ((), ())), preferred_element_...  41.5 us
    dot_general x4, matrix products, tn(): lax.dot_general(left, right, (((0,), (0,)), ((), ())), preferred_element_...  41.3 us
    ppermute x18, waiting for transfers between devices, seq_scatter(): first = lax.ppermute(one, ('batch', 'seq'), ahead)  35.7 us
    ppermute x18, starting transfers between devices, seq_gather(): second.append(lax.ppermute(second[-1], ('batch', 'seq'), back))  35.4 us
  transfers between devices with their start and end apart: 102, of which 41 were waited for; matrix products, arithmetic and copies ran while one was open for 29% of the time, Pallas kernels for 11%

profile of v2, /device:TPU:0, one launch (start us, length us, event | category | flops | bytes accessed | tf_op | source)
XLA Modules:
  0.0 717.0 jit_solution(15294604799718795853)
XLA Ops:
  32.5 11.0 %collective-permute-done.12 = bf16[1,48,1152]{2,1,0:T(8,128)(2,1)S(1)} collective-permute-done((bf16[1,48,1152]{2,1,0:T(8,128)(2,1)S(1)}, bf16[1,48,1152]{2,1,0:T(8,128)(2,1)S(1)}, u32[]{:S(2)}, u32[]{:S(2)}) %collective-permute-start.12) | collective-permute-done | bytes 110624 | tf_op jit(solution)/shard_map/ppermute | solution.py:509
  46.4 8.5 %collective-permute-done.2 = bf16[128,1536]{1,0:T(8,128)(2,1)} collective-permute-done((bf16[128,1536]{1,0:T(8,128)(2,1)S(1)}, bf16[128,1536]{1,0:T(8,128)(2,1)}, u32[]{:S(2)}, u32[]{:S(2)}) %collective-permute-start.2) | collective-permute-done | bytes 393248 | tf_op jit(solution)/shard_map/ppermute | solution.py:459
  57.4 8.1 %collective-permute-done.3 = bf16[128,1536]{1,0:T(8,128)(2,1)S(1)} collective-permute-done((bf16[128,1536]{1,0:T(8,128)(2,1)}, bf16[128,1536]{1,0:T(8,128)(2,1)S(1)}, u32[]{:S(2)}, u32[]{:S(2)}) %collective-permute-start.3) | collective-permute-done | bytes 393248 | tf_op jit(solution)/shard_map/ppermute | solution.py:459
  72.0 11.5 %collective-permute-start.22 = (bf16[128,1536]{1,0:T(8,128)(2,1)S(1)}, bf16[128,1536]{1,0:T(8,128)(2,1)S(1)}, u32[]{:S(2)}, u32[]{:S(2)}) collective-permute-start(bf16[128,1536]{1,0:T(8,128)(2,1)S(1)} %get-tuple-element.46), channel_id=1, source_target_pairs={{1,0},{2,1},{3,2},{7,3},{6,7},{5,6},{4,5},{0,4},{9,8},{10,9},{11,1... | collective-permute-start | bytes 1179656 | tf_op jit(solution)/shard_map/ppermute | solution.py:459
  89.3 6.2 collective-permute-start.23
  100.5 6.1 collective-permute-start.24
  111.1 6.7 collective-permute-done.26
  121.5 5.7 fusion.27.qkv_ref
  127.2 15.2 %attend_fwd.3 = (bf16[1,512,384]{2,1,0:T(8,128)(2,1)}, f32[1,512,384]{2,1,0:T(8,128)}, f32[1,2,2,512,512]{4,3,2,1,0:T(8,128)}) custom-call(f32[264]{0:T(512)} %dynamic_slice.169.kern_ref, f32[8]{0:T(128)} %dynamic_slice.170.mix_ref, bf16[1,512,1152]{2,1,0:T(8,128)(2,1)} %fusion.27.qkv_ref, f32[1,384]{1,0:T(1,128)} %constant_dynamic-slice_fusion.15.gain_ref), custom_call_target="tpu_custom_call" | custom-call | tf_op jit(solution)/shard_map/attend_fwd/pallas_call | solution.py:346
  153.6 15.3 %attend_fwd.2 = (bf16[1,512,384]{2,1,0:T(8,128)(2,1)}, f32[1,512,384]{2,1,0:T(8,128)}, f32[1,2,2,512,512]{4,3,2,1,0:T(8,128)}) custom-call(f32[264]{0:T(512)} %dynamic_slice.169.kern_ref, f32[8]{0:T(128)} %dynamic_slice.170.mix_ref, bf16[1,512,1152]{2,1,0:T(8,128)(2,1)} %fusion.26.qkv_ref, f32[1,384]{1,0:T(1,128)} %constant_dynamic-slice_fusion.15.gain_ref), custom_call_target="tpu_custom_call" | custom-call | tf_op jit(solution)/shard_map/attend_fwd/pallas_call | solution.py:346
  176.2 14.1 %collective-permute-done.15 = bf16[128,1536]{1,0:T(8,128)(2,1)S(1)} collective-permute-done((bf16[128,1536]{1,0:T(8,128)(2,1)S(1)}, bf16[128,1536]{1,0:T(8,128)(2,1)S(1)}, u32[]{:S(2)}, u32[]{:S(2)}) %collective-permute-start.15) | collective-permute-done | bytes 393248 | tf_op jit(solution)/shard_map/ppermute | solution.py:495
  190.5 5.8 collective-permute-start.16
  259.9 6.1 collective-permute-done.47
  276.7 6.1 collective-permute-done.48
  297.5 8.9 %fusion.87 = f32[512,2048]{1,0:T(8,128)} fusion(bf16[512,1536]{1,0:T(8,128)(2,1)} %select_dynamic-update-slice_fusion.6, bf16[1536,2048]{1,0:T(8,128)(2,1)} %all-gather.15.cloned.1.call-done), kind=kOutput, calls=%fused_computation.246 | convolution fusion | flops 3221225472 | bytes 12058624 | tf_op jit(solution)/shard_map/dot_general | solution.py:22
  306.3 6.5 fusion.86
  312.9 7.2 %multiply_convert_fusion.5 = (bf16[512,1024]{1,0:T(8,128)(2,1)S(1)}, bf16[512,1024]{1,0:T(8,128)(2,1)S(1)}, bf16[512,1024]{1,0:T(8,128)(2,1)}) fusion(f32[512,2048]{1,0:T(8,128)} %fusion.87, bf16[512,1536]{1,0:T(8,128)(2,1)} %fusion.40, bf16[1536,1024]{1,0:T(8,128)(2,1)} %all-gather.13.cloned.1.call-done), kind=kOutput, calls=%fused_computation.60 | convolution fusion | flops 1618477056 | bytes 12058624 | tf_op jit(solution)/shard_map/dot_general | solution.py:22
  325.0 23.7 %convolution_convert_fusion.1 = bf16[1536,2048]{1,0:T(8,128)(2,1)} fusion(bf16[512,1024]{1,0:T(8,128)(2,1)S(1)} %get-tuple-element.149, bf16[512,1024]{1,0:T(8,128)(2,1)S(1)} %get-tuple-element.148, bf16[512,1024]{1,0:T(8,128)(2,1)S(1)} %get-tuple-element.151, bf16[512,1024]{1,0:T(8,128)(2,1)S(1)} %get-tuple-element.150, ...), kind=kOutput, calls=%fused_computation.1 | convolution fusion | flops 6468665344 | bytes 13631488 | tf_op jit(solution)/shard_map/dot_general | solution.py:30
  349.1 6.9 convolution_convert_fusion.7
  359.8 7.2 %convolution_convert_fusion.8 = bf16[512,1536]{1,0:T(8,128)(2,1)S(1)} fusion(bf16[1536,2048]{1,0:T(8,128)(2,1)} %all-gather.15.cloned.1.call-done, bf16[512,1024]{1,0:T(8,128)(2,1)S(1)} %copy-done.69, bf16[512,1024]{1,0:T(8,128)(2,1)S(1)} %copy-done.67), kind=kOutput, calls=%fused_computation.41 | convolution fusion | flops 3226206208 | bytes 9961472 | tf_op jit(solution)/shard_map/dot_general | solution.py:26
  419.0 7.4 %collective-permute-done.64 = bf16[128,1536]{1,0:T(8,128)(2,1)S(1)} collective-permute-done((bf16[128,1536]{1,0:T(8,128)(2,1)}, bf16[128,1536]{1,0:T(8,128)(2,1)S(1)}, u32[]{:S(2)}, u32[]{:S(2)}) %collective-permute-start.64) | collective-permute-done | bytes 393248 | tf_op jit(solution)/shard_map/ppermute | solution.py:459
  457.9 9.2 %collective-permute-done.58 = bf16[128,1536]{1,0:T(8,128)(2,1)} collective-permute-done((bf16[128,1536]{1,0:T(8,128)(2,1)}, bf16[128,1536]{1,0:T(8,128)(2,1)}, u32[]{:S(2)}, u32[]{:S(2)}) %collective-permute-start.58) | collective-permute-done | bytes 393248 | tf_op jit(solution)/shard_map/ppermute | solution.py:459
  476.1 19.3 %collective-permute-done.59 = bf16[128,1536]{1,0:T(8,128)(2,1)} collective-permute-done((bf16[128,1536]{1,0:T(8,128)(2,1)}, bf16[128,1536]{1,0:T(8,128)(2,1)}, u32[]{:S(2)}, u32[]{:S(2)}) %collective-permute-start.59) | collective-permute-done | bytes 393248 | tf_op jit(solution)/shard_map/ppermute | solution.py:459
  504.7 8.0 %collective-permute-done.60 = bf16[128,1536]{1,0:T(8,128)(2,1)} collective-permute-done((bf16[128,1536]{1,0:T(8,128)(2,1)}, bf16[128,1536]{1,0:T(8,128)(2,1)}, u32[]{:S(2)}, u32[]{:S(2)}) %collective-permute-start.60) | collective-permute-done | bytes 393248 | tf_op jit(solution)/shard_map/ppermute | solution.py:459
  518.4 24.2 %attend_bwd.2 = (bf16[1,512,1152]{2,1,0:T(8,128)(2,1)}, f32[4,16,768]{2,1,0:T(8,128)}, f32[1,128]{1,0:T(1,128)}, f32[1,384]{1,0:T(1,128)}) custom-call(f32[264]{0:T(512)} %dynamic_slice.169.kern_ref, f32[8]{0:T(128)} %dynamic_slice.170.mix_ref, bf16[1,512,1152]{2,1,0:T(8,128)(2,1)} %fusion.26.qkv_ref, f32[1,384]{1,0:T(1,128)} %constant_dynamic-slice_fusion.15.gain_ref, ...), custom_call_target="tpu_custom_call" | custom-call | tf_op jit(solution)/shard_map/attend_bwd/pallas_call | solution.py:380
  542.6 5.7 fusion.14
  552.1 6.6 collective-permute-done.69
  571.5 24.3 %attend_bwd.3 = (bf16[1,512,1152]{2,1,0:T(8,128)(2,1)}, f32[4,16,768]{2,1,0:T(8,128)}, f32[1,128]{1,0:T(1,128)}, f32[1,384]{1,0:T(1,128)}) custom-call(f32[264]{0:T(512)} %dynamic_slice.169.kern_ref, f32[8]{0:T(128)} %dynamic_slice.170.mix_ref, bf16[1,512,1152]{2,1,0:T(8,128)(2,1)} %fusion.27.qkv_ref, f32[1,384]{1,0:T(1,128)} %constant_dynamic-slice_fusion.15.gain_ref, ...), custom_call_target="tpu_custom_call" | custom-call | tf_op jit(solution)/shard_map/attend_bwd/pallas_call | solution.py:380
  605.8 6.3 fusion.12
  615.5 8.3 %convolution_convert_fusion = bf16[1536,1152]{1,0:T(8,128)(2,1)} fusion(bf16[1024,1152]{1,0:T(8,128)(2,1)} %pad_maximum_fusion.1, bf16[512,1536]{1,0:T(8,128)(2,1)} %get-tuple-element.212, bf16[512,1536]{1,0:T(8,128)(2,1)S(1)} %copy-done.19), kind=kOutput, calls=%fused_computation | convolution fusion | flops 3631939584 | bytes 9043968 | tf_op jit(solution)/shard_map/dot_general | solution.py:30
  641.8 8.5 %collective-permute-done.79 = bf16[128,1536]{1,0:T(8,128)(2,1)S(1)} collective-permute-done((bf16[128,1536]{1,0:T(8,128)(2,1)S(1)}, bf16[128,1536]{1,0:T(8,128)(2,1)S(1)}, u32[]{:S(2)}, u32[]{:S(2)}) %collective-permute-start.79) | collective-permute-done | bytes 393248 | tf_op jit(solution)/shard_map/ppermute | solution.py:496
  677.7 15.5 %reduce-scatter.15.cloned.1.call-done = bf16[192,1152]{1,0:T(8,128)(2,1)} async-done(((bf16[1536,1152]{1,0:T(8,128)(2,1)}), bf16[192,1152]{1,0:T(8,128)(2,1)}) %reduce-scatter.15.cloned.1.call-update) | async-done | bytes 442384 | tf_op jit(solution)/shard_map/reduce_scatter | solution.py:433
  (517 shorter events, 370.5 us)
Async XLA Ops:
  7.2 114.3 %all-gather.9.cloned.1.call-start = ((), (), s32[]{:S(2)}) async-start(), calls=%async_computation.6 | async-start | bytes 3981312 | tf_op jit(solution)/shard_map/all_gather | solution.py:429
  44.3 98.1 %all-gather.11.cloned.1.call-start = ((), (), s32[]{:S(2)}) async-start(), calls=%async_computation.7 | async-start | bytes 1327104 | tf_op jit(solution)/shard_map/all_gather | solution.py:429
  68.2 180.9 %all-gather.19.cloned.1.call-start = ((), (), s32[]{:S(2)}) async-start(), calls=%async_computation.17 | async-start | bytes 1966080 | tf_op jit(solution)/shard_map/all_gather | solution.py:595
  69.2 196.7 %all-gather.17.cloned.1.call-start = ((), (), s32[]{:S(2)}) async-start(), calls=%async_computation.16 | async-start | bytes 1966080 | tf_op jit(solution)/shard_map/all_gather | solution.py:595
  69.8 227.7 %all-gather.15.cloned.1.call-start = ((), (), s32[]{:S(2)}) async-start(), calls=%async_computation.9 | async-start | bytes 7077888 | tf_op jit(solution)/shard_map/all_gather | solution.py:429
  71.9 240.9 %all-gather.13.cloned.1.call-start = ((), (), s32[]{:S(2)}) async-start(), calls=%async_computation.8 | async-start | bytes 3538944 | tf_op jit(solution)/shard_map/all_gather | solution.py:429
  83.5 333.4 %reduce-scatter.7.cloned.1.call-start = ((), (), s32[]{:S(2)}) async-start(), calls=%async_computation.10 | async-start | bytes 7077888 | tf_op jit(solution)/shard_map/reduce_scatter | solution.py:433
  145.8 27.3 %collective-permute-start.27 = (bf16[128,1536]{1,0:T(8,128)(2,1)}, bf16[128,1536]{1,0:T(8,128)(2,1)}, u32[]{:S(2)}, u32[]{:S(2)}) collective-permute-start(bf16[128,1536]{1,0:T(8,128)(2,1)} %get-tuple-element.180), channel_id=1, source_target_pairs={{0,1},{1,2},{2,3},{3,7},{7,6},{6,5},{5,4},{4,0},{8,9},{9,10},{10,1... | collective-permute-start | bytes 1179656 | tf_op jit(solution)/shard_map/ppermute | solution.py:495
  148.3 48.0 %collective-permute-start.30 = (bf16[128,1536]{1,0:T(8,128)(2,1)}, bf16[128,1536]{1,0:T(8,128)(2,1)}, u32[]{:S(2)}, u32[]{:S(2)}) collective-permute-start(bf16[128,1536]{1,0:T(8,128)(2,1)} %get-tuple-element.181), channel_id=1, source_target_pairs={{1,0},{2,1},{3,2},{7,3},{6,7},{5,6},{4,5},{0,4},{9,8},{10,9},{11,1... | collective-permute-start | bytes 1179656 | tf_op jit(solution)/shard_map/ppermute | solution.py:496
  171.0 19.4 %collective-permute-start.15 = (bf16[128,1536]{1,0:T(8,128)(2,1)S(1)}, bf16[128,1536]{1,0:T(8,128)(2,1)S(1)}, u32[]{:S(2)}, u32[]{:S(2)}) collective-permute-start(bf16[128,1536]{1,0:T(8,128)(2,1)S(1)} %get-tuple-element.176), channel_id=1, source_target_pairs={{0,1},{1,2},{2,3},{3,7},{7,6},{6,5},{5,4},{4,0},{8,9},{9,10},{10,1... | collective-permute-start | bytes 1179656 | tf_op jit(solution)/shard_map/ppermute | solution.py:495
  173.0 31.4 %collective-permute-start.18 = (bf16[128,1536]{1,0:T(8,128)(2,1)S(1)}, bf16[128,1536]{1,0:T(8,128)(2,1)S(1)}, u32[]{:S(2)}, u32[]{:S(2)}) collective-permute-start(bf16[128,1536]{1,0:T(8,128)(2,1)S(1)} %get-tuple-element.177), channel_id=1, source_target_pairs={{1,0},{2,1},{3,2},{7,3},{6,7},{5,6},{4,5},{0,4},{9,8},{10,9},{11,1... | collective-permute-start | bytes 1179656 | tf_op jit(solution)/shard_map/ppermute | solution.py:496
  174.2 25.8 %collective-permute-start.28 = (bf16[128,1536]{1,0:T(8,128)(2,1)S(1)}, bf16[128,1536]{1,0:T(8,128)(2,1)S(1)}, u32[]{:S(2)}, u32[]{:S(2)}) collective-permute-start(bf16[128,1536]{1,0:T(8,128)(2,1)S(1)} %add_convert_fusion.21), channel_id=1, source_target_pairs={{0,1},{1,2},{2,3},{3,7},{7,6},{6,5},{5,4},{4,0},{8,9},{9,10},{10,1... | collective-permute-start | bytes 1179656 | tf_op jit(solution)/shard_map/ppermute | solution.py:495
  203.9 19.7 %collective-permute-start.29 = (bf16[128,1536]{1,0:T(8,128)(2,1)}, bf16[128,1536]{1,0:T(8,128)(2,1)}, u32[]{:S(2)}, u32[]{:S(2)}) collective-permute-start(bf16[128,1536]{1,0:T(8,128)(2,1)} %get-tuple-element.178), channel_id=1, source_target_pairs={{0,1},{1,2},{2,3},{3,7},{7,6},{6,5},{5,4},{4,0},{8,9},{9,10},{10,1... | collective-permute-start | bytes 1179656 | tf_op jit(solution)/shard_map/ppermute | solution.py:495
  269.4 24.4 %collective-permute-start.50 = (bf16[128,1536]{1,0:T(8,128)(2,1)}, bf16[128,1536]{1,0:T(8,128)(2,1)S(1)}, u32[]{:S(2)}, u32[]{:S(2)}) collective-permute-start(bf16[128,1536]{1,0:T(8,128)(2,1)} %collective-permute-done.49), channel_id=1, source_target_pairs={{0,1},{1,2},{2,3},{3,7},{7,6},{6,5},{5,4},{4,0},{8,9},{9,10},{10,1... | collective-permute-start | bytes 1179656 | tf_op jit(solution)/shard_map/ppermute | solution.py:458
  274.4 21.3 %collective-permute-start.38 = (bf16[128,1536]{1,0:T(8,128)(2,1)}, bf16[128,1536]{1,0:T(8,128)(2,1)S(1)}, u32[]{:S(2)}, u32[]{:S(2)}) collective-permute-start(bf16[128,1536]{1,0:T(8,128)(2,1)} %collective-permute-done.37), channel_id=1, source_target_pairs={{0,1},{1,2},{2,3},{3,7},{7,6},{6,5},{5,4},{4,0},{8,9},{9,10},{10,1... | collective-permute-start | bytes 1179656 | tf_op jit(solution)/shard_map/ppermute | solution.py:458
  348.8 155.9 %reduce-scatter.9.cloned.1.call-start = ((), (), s32[]{:S(2)}) async-start(), calls=%async_computation.11 | async-start | bytes 3538944 | tf_op jit(solution)/shard_map/reduce_scatter | solution.py:433
  357.0 18.9 %collective-permute-start.51 = (bf16[128,1536]{1,0:T(8,128)(2,1)}, bf16[128,1536]{1,0:T(8,128)(2,1)}, u32[]{:S(2)}, u32[]{:S(2)}) collective-permute-start(bf16[128,1536]{1,0:T(8,128)(2,1)} %get-tuple-element.168), channel_id=1, source_target_pairs={{0,1},{1,2},{2,3},{3,7},{7,6},{6,5},{5,4},{4,0},{8,9},{9,10},{10,1... | collective-permute-start | bytes 1179656 | tf_op jit(solution)/shard_map/ppermute | solution.py:495
  359.7 22.1 %collective-permute-start.54 = (bf16[128,1536]{1,0:T(8,128)(2,1)}, bf16[128,1536]{1,0:T(8,128)(2,1)}, u32[]{:S(2)}, u32[]{:S(2)}) collective-permute-start(bf16[128,1536]{1,0:T(8,128)(2,1)} %get-tuple-element.169), channel_id=1, source_target_pairs={{1,0},{2,1},{3,2},{7,3},{6,7},{5,6},{4,5},{0,4},{9,8},{10,9},{11,1... | collective-permute-start | bytes 1179656 | tf_op jit(solution)/shard_map/ppermute | solution.py:496
  375.4 196.1 %reduce-scatter.11.cloned.1.call-start = ((), (), s32[]{:S(2)}) async-start(), calls=%async_computation.12 | async-start | bytes 1966080 | tf_op jit(solution)/shard_map/reduce_scatter | solution.py:652
  385.9 18.3 %collective-permute-start.53 = (bf16[128,1536]{1,0:T(8,128)(2,1)S(1)}, bf16[128,1536]{1,0:T(8,128)(2,1)S(1)}, u32[]{:S(2)}, u32[]{:S(2)}) collective-permute-start(bf16[128,1536]{1,0:T(8,128)(2,1)S(1)} %get-tuple-element.166), channel_id=1, source_target_pairs={{0,1},{1,2},{2,3},{3,7},{7,6},{6,5},{5,4},{4,0},{8,9},{9,10},{10,1... | collective-permute-start | bytes 1179656 | tf_op jit(solution)/shard_map/ppermute | solution.py:495
  455.1 144.0 %reduce-scatter.13.cloned.1.call-start = ((), (), s32[]{:S(2)}) async-start(), calls=%async_computation.13 | async-start | bytes 1966080 | tf_op jit(solution)/shard_map/reduce_scatter | solution.py:652
  467.1 28.4 %collective-permute-start.59 = (bf16[128,1536]{1,0:T(8,128)(2,1)}, bf16[128,1536]{1,0:T(8,128)(2,1)}, u32[]{:S(2)}, u32[]{:S(2)}) collective-permute-start(bf16[128,1536]{1,0:T(8,128)(2,1)} %collective-permute-done.58), channel_id=1, source_target_pairs={{1,0},{2,1},{3,2},{7,3},{6,7},{5,6},{4,5},{0,4},{9,8},{10,9},{11,1... | collective-permute-start | bytes 1179656 | tf_op jit(solution)/shard_map/ppermute | solution.py:459
  467.1 30.4 %collective-permute-start.61 = (bf16[128,1536]{1,0:T(8,128)(2,1)}, bf16[128,1536]{1,0:T(8,128)(2,1)}, u32[]{:S(2)}, u32[]{:S(2)}) collective-permute-start(bf16[128,1536]{1,0:T(8,128)(2,1)} %collective-permute-done.57), channel_id=1, source_target_pairs={{0,1},{1,2},{2,3},{3,7},{7,6},{6,5},{5,4},{4,0},{8,9},{9,10},{10,1... | collective-permute-start | bytes 1179656 | tf_op jit(solution)/shard_map/ppermute | solution.py:458
  497.5 18.9 %collective-permute-start.62 = (bf16[128,1536]{1,0:T(8,128)(2,1)}, bf16[128,1536]{1,0:T(8,128)(2,1)}, u32[]{:S(2)}, u32[]{:S(2)}) collective-permute-start(bf16[128,1536]{1,0:T(8,128)(2,1)} %collective-permute-done.61), channel_id=1, source_target_pairs={{0,1},{1,2},{2,3},{3,7},{7,6},{6,5},{5,4},{4,0},{8,9},{9,10},{10,1... | collective-permute-start | bytes 1179656 | tf_op jit(solution)/shard_map/ppermute | solution.py:458
  518.3 157.9 %reduce-scatter.17.cloned.1.call-start = ((), (), s32[]{:S(2)}) async-start(), calls=%async_computation.15 | async-start | bytes 1327104 | tf_op jit(solution)/shard_map/reduce_scatter | solution.py:433
  569.5 59.3 %collective-permute-start.73 = (bf16[128,1536]{1,0:T(8,128)(2,1)}, bf16[128,1536]{1,0:T(8,128)(2,1)}, u32[]{:S(2)}, u32[]{:S(2)}) collective-permute-start(bf16[128,1536]{1,0:T(8,128)(2,1)} %get-tuple-element.163), channel_id=1, source_target_pairs={{1,0},{2,1},{3,2},{7,3},{6,7},{5,6},{4,5},{0,4},{9,8},{10,9},{11,1... | collective-permute-start | bytes 1179656 | tf_op jit(solution)/shard_map/ppermute | solution.py:496
  569.5 101.6 %collective-permute-start.71 = (bf16[128,1536]{1,0:T(8,128)(2,1)}, bf16[128,1536]{1,0:T(8,128)(2,1)S(1)}, u32[]{:S(2)}, u32[]{:S(2)}) collective-permute-start(bf16[128,1536]{1,0:T(8,128)(2,1)} %get-tuple-element.162), channel_id=1, source_target_pairs={{0,1},{1,2},{2,3},{3,7},{7,6},{6,5},{5,4},{4,0},{8,9},{9,10},{10,1... | collective-permute-start | bytes 1179656 | tf_op jit(solution)/shard_map/ppermute | solution.py:495
  603.5 89.8 %reduce-scatter.15.cloned.1.call-start = ((), (), s32[]{:S(2)}) async-start(), calls=%async_computation.14 | async-start | bytes 3981312 | tf_op jit(solution)/shard_map/reduce_scatter | solution.py:433
  630.8 40.3 %collective-permute-start.74 = (bf16[128,1536]{1,0:T(8,128)(2,1)}, bf16[128,1536]{1,0:T(8,128)(2,1)S(1)}, u32[]{:S(2)}, u32[]{:S(2)}) collective-permute-start(bf16[128,1536]{1,0:T(8,128)(2,1)} %add_convert_fusion.4), channel_id=1, source_target_pairs={{1,0},{2,1},{3,2},{7,3},{6,7},{5,6},{4,5},{0,4},{9,8},{10,9},{11,1... | collective-permute-start | bytes 1179656 | tf_op jit(solution)/shard_map/ppermute | solution.py:496
  641.4 29.7 %collective-permute-start.77 = (bf16[128,1536]{1,0:T(8,128)(2,1)}, bf16[128,1536]{1,0:T(8,128)(2,1)S(1)}, u32[]{:S(2)}, u32[]{:S(2)}) collective-permute-start(bf16[128,1536]{1,0:T(8,128)(2,1)} %get-tuple-element.158), channel_id=1, source_target_pairs={{0,1},{1,2},{2,3},{3,7},{7,6},{6,5},{5,4},{4,0},{8,9},{9,10},{10,1... | collective-permute-start | bytes 1179656 | tf_op jit(solution)/shard_map/ppermute | solution.py:495
  651.2 19.9 %collective-permute-start.80 = (bf16[128,1536]{1,0:T(8,128)(2,1)}, bf16[128,1536]{1,0:T(8,128)(2,1)}, u32[]{:S(2)}, u32[]{:S(2)}) collective-permute-start(bf16[128,1536]{1,0:T(8,128)(2,1)} %add_convert_fusion), channel_id=1, source_target_pairs={{1,0},{2,1},{3,2},{7,3},{6,7},{5,6},{4,5},{0,4},{9,8},{10,9},{11,1... | collective-permute-start | bytes 1179656 | tf_op jit(solution)/shard_map/ppermute | solution.py:496
  676.2 20.7 %collective-permute-start.89 = (bf16[48,1536]{1,0:T(8,128)(2,1)}, bf16[48,1536]{1,0:T(8,128)(2,1)S(1)}, u32[]{:S(2)}, u32[]{:S(2)}) collective-permute-start(bf16[48,1536]{1,0:T(8,128)(2,1)} %reduce-scatter.17.cloned.1.call-done), channel_id=1, source_target_pairs={{0,0},{4,1},{8,2},{12,3},{16,4},{20,5},{24,6},{28,7},{1,8},{5,9},{... | collective-permute-start | bytes 442376 | tf_op jit(solution)/shard_map/ppermute | solution.py:677
  (142 other events, 1493.4 us)
Sparse Core Ops, SparseCore 0:
  44.5 36.4 all-gather.8
  82.8 27.4 all-gather.10
  111.9 37.0 all-gather.18
  150.4 48.2 all-gather.16
  201.0 52.5 all-gather.14
  255.3 32.1 all-gather.12
  348.9 61.7 reduce-scatter.6
  414.1 46.0 reduce-scatter.8
  462.5 49.4 reduce-scatter.10
  518.4 37.3 reduce-scatter.12
  603.6 36.6 reduce-scatter.16
  643.7 49.5 reduce-scatter.14

commit v3 on v2

--- a/solution.py
+++ b/solution.py
@@ -447,16 +447,19 @@
     return 1 - 2 * (lax.axis_index("batch") % 2)
 
 
-def seq_gather(value, hops=None):
+def seq_gather(value, hops=None, gates=None):
     count = lax.axis_size("seq")
     here = lax.axis_index("seq")
     side = ring_side()
     ahead, back = ring_perms()
     rows = value.shape[0]
     first, second = [value], [value]
-    for _ in range(count - 1):
-        first.append(lax.ppermute(first[-1], ("batch", "seq"), ahead))
-        second.append(lax.ppermute(second[-1], ("batch", "seq"), back))
+    for step in range(count - 1):
+        one, two = first[-1], second[-1]
+        if gates is not None and step == count - 2:
+            one, two = after((one, two), gates)
+        first.append(lax.ppermute(one, ("batch", "seq"), ahead))
+        second.append(lax.ppermute(two, ("batch", "seq"), back))
     if hops is not None:
         hops += [(one, two) for one, two in zip(first[1:], second[1:])]
     out = jnp.zeros((count * rows, value.shape[1]), value.dtype)
@@ -469,7 +472,7 @@
     return out
 
 
-def seq_scatter(value):
+def seq_scatter(value, hops=None):
     count = lax.axis_size("seq")
     here = lax.axis_index("seq")
     side = ring_side()
@@ -494,6 +497,8 @@
             two = (two.astype(f32) + came(second, skip_second)).astype(bf16)
         first = lax.ppermute(one, ("batch", "seq"), ahead)
         second = lax.ppermute(two, ("batch", "seq"), back)
+        if hops is not None:
+            hops.append((first, second))
     return block(here).astype(f32) + came(first, skip_first) + came(second, skip_second)
 
 
@@ -573,9 +578,11 @@
     all_gains = all_sum(gains, ("batch",))
     hops = []
     x_all = [seq_gather(inputs[0], hops)]
-    for index in range(1, seqs):
-        x_all.append(seq_gather(after(inputs[index], hops[-2])))
-    joint = after(joint, all_gains, hops[0])
+    order = [
+        (index, (index % lanes) * parts + index // lanes) for index in range(blocks)
+    ]
+    out_rows = lax.ppermute(w_out, ("batch", "seq"), order)
+    joint = after(joint, all_gains, hops[0], out_rows)
     w_joint = batch_gather(joint)
     all_gains = all_gains.reshape(3, 1, width)
     gain_in32, gain_head32, gain_mid32 = all_gains[0], all_gains[1], all_gains[2]
@@ -585,10 +592,7 @@
     )
     mix_own = lax.dynamic_slice_in_dim(mixing.reshape(-1), place_seq * 4 * groups, 4 * groups, 0)
 
-    order = [
-        (index, (index % lanes) * parts + index // lanes) for index in range(blocks)
-    ]
-    w_join = batch_gather(lax.ppermute(after(w_out, x_all[0]), ("batch", "seq"), order))
+    w_join = batch_gather(out_rows)
     w_gate_up = batch_gather(jnp.concatenate([w_gate, w_up], axis=1))
     w_down_t = batch_gather(w_down.T)
     hidden_width = w_gate.shape[1]
@@ -603,6 +607,8 @@
     outputs, input_grads = [], []
     keep = []
     for index in range(seqs):
+        if index:
+            x_all.append(seq_gather(after(inputs[index], hops[-2]), gates=qkv))
         x32 = x_all[index].astype(f32)
         x_inverse = inverse_rms(x32)
         normed = (x32 * x_inverse * gain_in32).astype(bf16)
@@ -613,52 +619,65 @@
     gain_mid_grad = jnp.zeros((1, width), f32)
     gain_in_grad = jnp.zeros((1, width), f32)
     ffn = []
-    mid_parts = []
     results = []
+    n_all = []
+    scattered = []
+    gate_by = []
+    mid_inverses = []
     for index in range(seqs):
         middle = keep[index][-1]
-        mid_inverse = inverse_rms(middle)
-        n_all = seq_gather((middle * mid_inverse * gain_mid32).astype(bf16))
-        both = nn(n_all, w_gate_up)
+        mid_inverses.append(inverse_rms(middle))
+        n_own = (middle * mid_inverses[-1] * gain_mid32).astype(bf16)
+        n_all.append(seq_gather(n_own, gates=gate_by[-1] if gate_by else None))
+        whole = after(n_all[index], ffn[-1][4]) if ffn else n_all[index]
+        both = nn(whole, w_gate_up)
+        gate_by.append(both)
         gate, upward = both[:, :hidden_width], both[:, hidden_width:]
         sigma = 1.0 / (1.0 + jnp.exp(-gate))
         silu = gate * sigma
         hidden = (silu * upward).astype(bf16)
-        down_in = (o_all[index].astype(f32) * factor[index]).astype(bf16)
+        o_here = after(o_all[index], scattered[-1][0]) if scattered else o_all[index]
+        down_in = (o_here.astype(f32) * factor[index]).astype(bf16)
         hidden_grad = nn(down_in, w_down_t)
         gate_grad = (hidden_grad * upward * (sigma * (1.0 + gate * (1.0 - sigma)))).astype(bf16)
         up_grad = (hidden_grad * silu).astype(bf16)
-        grads = jnp.concatenate([gate_grad, up_grad], axis=1)
-        mid_parts.append(seq_scatter(nt(grads, w_gate_up).astype(bf16)))
-        ffn.append((n_all, hidden, down_in, grads))
+        grads = lax.optimization_barrier(jnp.concatenate([gate_grad, up_grad], axis=1))
+        mid_part = nt(after(grads, scattered[-1][1]) if scattered else grads, w_gate_up)
+        mid_part = mid_part.astype(bf16)
+        ffn.append((n_all[index], hidden, down_in, grads, mid_part))
+        scattered.append([])
+        scattered[-1].append(seq_scatter(mid_part, scattered[-1]))
     cat = lambda place: jnp.concatenate([item[place] for item in ffn], axis=0)
-    all_n, all_hidden, all_down, all_grads = cat(0), cat(1), cat(2), cat(3)
-    g_gate_up = tn(all_n, all_grads).astype(bf16)
-    g_down_t = tn(all_down, all_hidden).astype(bf16)
-    mid_parts = after(mid_parts, g_gate_up, g_down_t)
-    g_gate_up = batch_scatter(g_gate_up)
-    g_down_t = batch_scatter(g_down_t)
+    all_hidden, all_down = cat(1), cat(2)
+    g_gate_up = sum(tn(item[0], item[3]) for item in ffn).astype(bf16)
+    g_down_t = tn(after(all_down, g_gate_up, scattered[-1][0]), all_hidden).astype(bf16)
+    outers = []
     for index in range(seqs):
-        middle = keep[index][-1]
-        mid_inverse = inverse_rms(middle)
-        mid_grad = mid_parts[index]
+        middle, mid_inverse = keep[index][-1], mid_inverses[index]
+        mid_grad = after(scattered[index][-1], g_down_t if index else g_gate_up)
         unit = middle * mid_inverse
         gain_mid_grad = gain_mid_grad + jnp.sum(mid_grad * unit, axis=0, keepdims=True)
         cotangent = output_grad[index].astype(f32) * factor[index]
         middle_grad = cotangent + rms_back(middle, mid_inverse, mid_grad * gain_mid32)
-        a_all = seq_gather(after(middle_grad.astype(bf16), g_gate_up))
+        a_all = seq_gather(middle_grad.astype(bf16), gates=outers[-1] if outers else None)
+        outers.append(nt(a_all, w_join))
         keep[index] += [middle_grad, a_all]
-        part = after(nt(ffn[index][1], w_down_t).astype(bf16), a_all)
-        results.append(lax.psum_scatter(part, "seq", scatter_dimension=0, tiled=True))
+    g_gate_up = batch_scatter(g_gate_up)
+    g_down_t = batch_scatter(g_down_t)
+    parts_out = [nt(item[1], w_down_t).astype(bf16).reshape(parts, seg, width) for item in ffn]
+    parts_out = jnp.concatenate(parts_out, axis=1).reshape(parts * seqs * seg, width)
+    parts_out = after(parts_out, outers[0])
+    results = lax.psum_scatter(parts_out, "seq", scatter_dimension=0, tiled=True)
+    results = results.reshape(seqs, seg, width)
     back = []
     for index in range(seqs):
         x_inverse, normed, qkv, joined, heads, probs, middle, middle_grad, a_all = keep[index]
-        outer = nt(a_all, w_join)[None]
-        outer = after(outer, n_part, results[0]) if back else after(outer, g_down_t)
+        outer = outers[index][None]
+        outer = after(outer, n_part, g_gate_up) if back else outer
         dqkv, corr, mix_sum, head_sum = attend_bwd(
             kern_own, mix_own, qkv, gain_own, heads, probs, outer
         )
-        n_part = nt(dqkv[0], w_joint)
+        n_part = nt(after(dqkv, g_down_t)[0] if back else dqkv[0], w_joint)
         unit_all = x_all[index].astype(f32) * x_inverse
         gain_in_grad = gain_in_grad + jnp.sum(n_part * unit_all, axis=0, keepdims=True)
         n_grad = seq_scatter(n_part.astype(bf16))
@@ -668,16 +687,18 @@
         back.append((normed, dqkv[0], joined[0], a_all, corr, mix_sum, head_sum))
     cat = lambda place: jnp.concatenate([item[place] for item in back], axis=0)
     all_normed, all_dqkv, all_joined, all_a = cat(0), cat(1), cat(2), cat(3)
-    all_dqkv = after(all_dqkv, results[-1])
-    all_a = after(all_a, all_dqkv)
+    g_joint = tn(all_normed, all_dqkv).astype(bf16)
     for index in range(seqs):
         middle = after(keep[index][6], back[-1][1])
         outputs.append((middle + results[index].astype(f32)).astype(bf16))
-    g_out = batch_scatter(tn(all_joined, all_a).astype(bf16))
+    g_out = tn(all_joined, all_a).astype(bf16)
+    span = parts * own
+    packed = [g_joint.reshape(lanes, span, 3 * local), g_out.reshape(lanes, -1, 3 * local)]
+    packed = batch_scatter(jnp.concatenate(packed, axis=1).reshape(-1, 3 * local))
+    g_out = packed[span:].reshape(own, width)
     g_out = lax.ppermute(g_out, ("batch", "seq"), [(there, here) for here, there in order])
     g_out = g_out.astype(f32)
-    g_joint = batch_scatter(tn(all_normed, all_dqkv).astype(bf16))
-    g_joint = seq_swap(g_joint.reshape(parts, own, 3 * local)).astype(f32)
+    g_joint = seq_swap(packed[:span].reshape(parts, own, 3 * local)).astype(f32)
     g_joint = g_joint.reshape(parts, own, 3, local).transpose(2, 1, 0, 3).reshape(3, own, width)
 
     corr = sum(item[4] for item in back)

time: 726 us -> 664 us (0.915)
  starting transfers between devices: 143 us -> 116 us
  matrix products: 126 us -> 100 us
  other arithmetic: 84.3 us -> 76.1 us
    ppermute x18, waiting for transfers between devices: 35.7 us -> 70.1 us  [seq_scatter(): first = lax.ppermute(one, ('batch', 'seq'), ahead)]
    ppermute x37, starting transfers between devices: 66.3 us -> 39.3 us  [the longest x18 34.6 us: seq_gather(): first.append(lax.ppermute(one, ('batch', 'seq'), ahead))]
    ppermute x37, waiting for transfers between devices: 111 us -> 87.3 us  [the longest x18 66.6 us: seq_gather(): second.append(lax.ppermute(two, ('batch', 'seq'), back))]
    reduce_scatter x4 -> x3, waiting for transfers between devices: 15.5 us -> 0.02 us  [batch_scatter(): return lax.psum_scatter(value, 'batch', scatter_dimension=0, tiled=True)]
    dot_general x4 -> x5, matrix products: 41.3 us -> 28.6 us  [tn(): lax.dot_general(left, right, (((0,), (0,)), ((), ())), preferred_element_...]
    dot_general x8, matrix products: 43.2 us -> 31.8 us  [nt(): lax.dot_general(left, right, (((1,), (1,)), ((), ())), preferred_element_...]
  transfers between devices with their start and end apart: 102 -> 100, of which waited for: 41 -> 45; matrix products, arithmetic and copies ran while one was open for 29% -> 28% of each run, Pallas kernels for 11% -> 12%
where the time goes in v3:
time: 664 us; the launch traced here: 654 us
  waiting for transfers between devices  225 us (34%)
  starting transfers between devices  116 us (17%)
  matrix products  100 us (15%)
  Pallas kernels  79.2 us (12%)
  other arithmetic  76.1 us (11%)
  local copies, waits for them, and re-layouts  41.4 us (6%)
  between operations  16.3 us (2%)
    ppermute x18, waiting for transfers between devices, seq_scatter(): first = lax.ppermute(one, ('batch', 'seq'), ahead)  70.1 us
    ppermute x18, waiting for transfers between devices, seq_gather(): second.append(lax.ppermute(two, ('batch', 'seq'), back))  66.6 us
    pallas_call x2, Pallas kernels, attend_bwd(): pl.pallas_call(attend_bwd_body, grid=(seqs,), in_specs=[smem, smem, wide,...  48.6 us
    ppermute x18, starting transfers between devices, seq_scatter(): first = lax.ppermute(one, ('batch', 'seq'), ahead)  41.4 us
    dot_general x8, matrix products, nn(): lax.dot_general(left, right, (((1,), (0,)), ((), ())), preferred_element_...  40.1 us
    ppermute x18, waiting for transfers between devices, seq_scatter(): second = lax.ppermute(two, ('batch', 'seq'), back)  37.5 us
    ppermute x18, starting transfers between devices, seq_gather(): first.append(lax.ppermute(one, ('batch', 'seq'), ahead))  34.6 us
    dot_general x8, matrix products, nt(): lax.dot_general(left, right, (((1,), (1,)), ((), ())), preferred_element_...  31.8 us
  transfers between devices with their start and end apart: 100, of which 45 were waited for; matrix products, arithmetic and copies ran while one was open for 28% of the time, Pallas kernels for 12%

profile of v3, /device:TPU:0, one launch (start us, length us, event | category | flops | bytes accessed | tf_op | source)
XLA Modules:
  0.0 654.0 jit_solution(5850613200717619604)
XLA Ops:
  35.2 13.8 %collective-permute-done.12 = bf16[1,48,1152]{2,1,0:T(8,128)(2,1)} collective-permute-done((bf16[1,48,1152]{2,1,0:T(8,128)(2,1)}, bf16[1,48,1152]{2,1,0:T(8,128)(2,1)}, u32[]{:S(2)}, u32[]{:S(2)}) %collective-permute-start.12) | collective-permute-done | bytes 110624 | tf_op jit(solution)/shard_map/ppermute | solution.py:514
  58.2 7.5 %collective-permute-done.2 = bf16[128,1536]{1,0:T(8,128)(2,1)S(1)} collective-permute-done((bf16[128,1536]{1,0:T(8,128)(2,1)}, bf16[128,1536]{1,0:T(8,128)(2,1)S(1)}, u32[]{:S(2)}, u32[]{:S(2)}) %collective-permute-start.2) | collective-permute-done | bytes 393248 | tf_op jit(solution)/shard_map/ppermute | solution.py:462
  70.5 7.2 %collective-permute-done.3 = bf16[128,1536]{1,0:T(8,128)(2,1)S(1)} collective-permute-done((bf16[128,1536]{1,0:T(8,128)(2,1)S(1)}, bf16[128,1536]{1,0:T(8,128)(2,1)S(1)}, u32[]{:S(2)}, u32[]{:S(2)}) %collective-permute-start.3) | collective-permute-done | bytes 393248 | tf_op jit(solution)/shard_map/ppermute | solution.py:462
  100.2 15.5 %attend_fwd.2 = (bf16[1,512,384]{2,1,0:T(8,128)(2,1)}, f32[1,512,384]{2,1,0:T(8,128)}, f32[1,2,2,512,512]{4,3,2,1,0:T(8,128)}) custom-call(f32[264]{0:T(512)} %dynamic_slice.169.kern_ref, f32[8]{0:T(128)} %dynamic_slice.170.mix_ref, bf16[1,512,1152]{2,1,0:T(8,128)(2,1)} %fusion.20.qkv_ref, f32[1,384]{1,0:T(1,128)} %constant_dynamic-slice_fusion.15.gain_ref), custom_call_target="tpu_custom_call" | custom-call | tf_op jit(solution)/shard_map/attend_fwd/pallas_call | solution.py:346
  129.5 15.1 %attend_fwd.3 = (bf16[1,512,384]{2,1,0:T(8,128)(2,1)}, f32[1,512,384]{2,1,0:T(8,128)}, f32[1,2,2,512,512]{4,3,2,1,0:T(8,128)}) custom-call(f32[264]{0:T(512)} %dynamic_slice.169.kern_ref, f32[8]{0:T(128)} %dynamic_slice.170.mix_ref, bf16[1,512,1152]{2,1,0:T(8,128)(2,1)} %fusion.21.qkv_ref, f32[1,384]{1,0:T(1,128)} %constant_dynamic-slice_fusion.15.gain_ref), custom_call_target="tpu_custom_call" | custom-call | tf_op jit(solution)/shard_map/attend_fwd/pallas_call | solution.py:346
  151.9 10.7 %collective-permute-done.27 = bf16[128,1536]{1,0:T(8,128)(2,1)S(1)} collective-permute-done((bf16[128,1536]{1,0:T(8,128)(2,1)S(1)}, bf16[128,1536]{1,0:T(8,128)(2,1)S(1)}, u32[]{:S(2)}, u32[]{:S(2)}) %collective-permute-start.27) | collective-permute-done | bytes 393248 | tf_op jit(solution)/shard_map/ppermute | solution.py:498
  174.5 5.9 collective-permute-done.19
  181.2 7.5 %collective-permute-done.31 = bf16[128,1536]{1,0:T(8,128)(2,1)S(1)} collective-permute-done((bf16[128,1536]{1,0:T(8,128)(2,1)S(1)}, bf16[128,1536]{1,0:T(8,128)(2,1)S(1)}, u32[]{:S(2)}, u32[]{:S(2)}) %collective-permute-start.31) | collective-permute-done | bytes 393248 | tf_op jit(solution)/shard_map/ppermute | solution.py:499
  205.9 8.4 %collective-permute-done.34 = bf16[128,1536]{1,0:T(8,128)(2,1)S(1)} collective-permute-done((bf16[128,1536]{1,0:T(8,128)(2,1)S(1)}, bf16[128,1536]{1,0:T(8,128)(2,1)S(1)}, u32[]{:S(2)}, u32[]{:S(2)}) %collective-permute-start.34) | collective-permute-done | bytes 393248 | tf_op jit(solution)/shard_map/ppermute | solution.py:462
  220.8 5.7 collective-permute-done.35
  248.2 9.1 %fusion.71 = f32[512,2048]{1,0:T(8,128)} fusion(bf16[512,1536]{1,0:T(8,128)(2,1)} %select_dynamic-update-slice_fusion.9, bf16[1536,2048]{1,0:T(8,128)(2,1)} %all-gather.15.cloned.1.call-done), kind=kOutput, calls=%fused_computation.229 | convolution fusion | flops 3221225472 | bytes 12058624 | tf_op jit(solution)/shard_map/dot_general | solution.py:22
  257.3 7.2 %multiply_convert_fusion.7 = (bf16[512,1024]{1,0:T(8,128)(2,1)S(1)}, bf16[512,1024]{1,0:T(8,128)(2,1)S(1)}, bf16[512,1024]{1,0:T(8,128)(2,1)}) fusion(f32[512,2048]{1,0:T(8,128)} %fusion.71, bf16[512,1536]{1,0:T(8,128)(2,1)} %fusion.30, bf16[1536,1024]{1,0:T(8,128)(2,1)} %all-gather.13.cloned.1.call-done), kind=kOutput, calls=%fused_computation.55 | convolution fusion | flops 1618477056 | bytes 12058624 | tf_op jit(solution)/shard_map/dot_general | solution.py:22
  275.2 6.1 all-gather.17.cloned.1.call-done
  286.9 8.4 %collective-permute-done.45 = bf16[128,1536]{1,0:T(8,128)(2,1)} collective-permute-done((bf16[128,1536]{1,0:T(8,128)(2,1)}, bf16[128,1536]{1,0:T(8,128)(2,1)}, u32[]{:S(2)}, u32[]{:S(2)}) %collective-permute-start.45) | collective-permute-done | bytes 393248 | tf_op jit(solution)/shard_map/ppermute | solution.py:462
  300.8 6.9 %fusion.72 = f32[512,2048]{1,0:T(8,128)S(1)} fusion(bf16[512,1536]{1,0:T(8,128)(2,1)} %select_dynamic-update-slice_fusion.6, bf16[1536,2048]{1,0:T(8,128)(2,1)} %all-gather.15.cloned.1.call-done), kind=kOutput, calls=%fused_computation.230 | convolution fusion | flops 3221225472 | bytes 12058624 | tf_op jit(solution)/shard_map/dot_general | solution.py:22
  317.2 7.2 %add_convert_fusion = bf16[1536,2048]{1,0:T(8,128)(2,1)} fusion(f32[1536,2048]{1,0:T(8,128)S(1)} %fusion.73, bf16[512,1536]{1,0:T(8,128)(2,1)} %select_dynamic-update-slice_fusion.9, bf16[512,2048]{1,0:T(8,128)(2,1)S(1)} %copy-done.26), kind=kOutput, calls=%fused_computation | convolution fusion | flops 3227516928 | bytes 22544384 | tf_op jit(solution)/shard_map/dot_general | solution.py:30
  327.2 8.8 %collective-permute-done.47 = bf16[128,1536]{1,0:T(8,128)(2,1)S(1)} collective-permute-done((bf16[128,1536]{1,0:T(8,128)(2,1)S(1)}, bf16[128,1536]{1,0:T(8,128)(2,1)S(1)}, u32[]{:S(2)}, u32[]{:S(2)}) %collective-permute-start.47) | collective-permute-done | bytes 393248 | tf_op jit(solution)/shard_map/ppermute | solution.py:498
  336.0 7.1 %convolution_convert_fusion.6 = bf16[512,1536]{1,0:T(8,128)(2,1)S(1)} fusion(bf16[512,2048]{1,0:T(8,128)(2,1)S(1)} %copy-done.28, bf16[1536,2048]{1,0:T(8,128)(2,1)} %all-gather.15.cloned.1.call-done), kind=kOutput, calls=%fused_computation.33 | convolution fusion | flops 3222011904 | bytes 9961472 | tf_op jit(solution)/shard_map/dot_general | solution.py:26
  345.8 8.6 %collective-permute-done.49 = bf16[128,1536]{1,0:T(8,128)(2,1)S(1)} collective-permute-done((bf16[128,1536]{1,0:T(8,128)(2,1)S(1)}, bf16[128,1536]{1,0:T(8,128)(2,1)S(1)}, u32[]{:S(2)}, u32[]{:S(2)}) %collective-permute-start.49) | collective-permute-done | bytes 393248 | tf_op jit(solution)/shard_map/ppermute | solution.py:498
  358.3 8.2 %collective-permute-done.50 = bf16[128,1536]{1,0:T(8,128)(2,1)S(1)} collective-permute-done((bf16[128,1536]{1,0:T(8,128)(2,1)S(1)}, bf16[128,1536]{1,0:T(8,128)(2,1)S(1)}, u32[]{:S(2)}, u32[]{:S(2)}) %collective-permute-start.50) | collective-permute-done | bytes 393248 | tf_op jit(solution)/shard_map/ppermute | solution.py:498
  366.7 8.1 %collective-permute-done.59 = bf16[128,1536]{1,0:T(8,128)(2,1)S(1)} collective-permute-done((bf16[128,1536]{1,0:T(8,128)(2,1)S(1)}, bf16[128,1536]{1,0:T(8,128)(2,1)S(1)}, u32[]{:S(2)}, u32[]{:S(2)}) %collective-permute-start.59) | collective-permute-done | bytes 393248 | tf_op jit(solution)/shard_map/ppermute | solution.py:498
  394.6 8.9 %collective-permute-done.62 = bf16[128,1536]{1,0:T(8,128)(2,1)S(1)} collective-permute-done((bf16[128,1536]{1,0:T(8,128)(2,1)S(1)}, bf16[128,1536]{1,0:T(8,128)(2,1)S(1)}, u32[]{:S(2)}, u32[]{:S(2)}) %collective-permute-start.62) | collective-permute-done | bytes 393248 | tf_op jit(solution)/shard_map/ppermute | solution.py:462
  407.5 6.3 collective-permute-done.63
  433.9 7.0 %collective-permute-done.55 = bf16[128,1536]{1,0:T(8,128)(2,1)S(1)} collective-permute-done((bf16[128,1536]{1,0:T(8,128)(2,1)S(1)}, bf16[128,1536]{1,0:T(8,128)(2,1)S(1)}, u32[]{:S(2)}, u32[]{:S(2)}) %collective-permute-start.55) | collective-permute-done | bytes 393248 | tf_op jit(solution)/shard_map/ppermute | solution.py:461
  443.4 24.3 %attend_bwd.2 = (bf16[1,512,1152]{2,1,0:T(8,128)(2,1)}, f32[4,16,768]{2,1,0:T(8,128)}, f32[1,128]{1,0:T(1,128)}, f32[1,384]{1,0:T(1,128)}) custom-call(f32[264]{0:T(512)} %dynamic_slice.169.kern_ref, f32[8]{0:T(128)} %dynamic_slice.170.mix_ref, bf16[1,512,1152]{2,1,0:T(8,128)(2,1)} %fusion.20.qkv_ref, f32[1,384]{1,0:T(1,128)} %constant_dynamic-slice_fusion.15.gain_ref, ...), custom_call_target="tpu_custom_call" | custom-call | tf_op jit(solution)/shard_map/attend_bwd/pallas_call | solution.py:380
  480.8 14.9 %collective-permute-done.69 = bf16[128,1536]{1,0:T(8,128)(2,1)} collective-permute-done((bf16[128,1536]{1,0:T(8,128)(2,1)}, bf16[128,1536]{1,0:T(8,128)(2,1)}, u32[]{:S(2)}, u32[]{:S(2)}) %collective-permute-start.69) | collective-permute-done | bytes 393248 | tf_op jit(solution)/shard_map/ppermute | solution.py:498
  497.7 7.3 %collective-permute-start.70 = (bf16[128,1536]{1,0:T(8,128)(2,1)}, bf16[128,1536]{1,0:T(8,128)(2,1)}, u32[]{:S(2)}, u32[]{:S(2)}) collective-permute-start(bf16[128,1536]{1,0:T(8,128)(2,1)} %add_convert_fusion.8), channel_id=1, source_target_pairs={{0,1},{1,2},{2,3},{3,7},{7,6},{6,5},{5,4},{4,0},{8,9},{9,10},{10,1... | collective-permute-start | bytes 1179656 | tf_op jit(solution)/shard_map/ppermute | solution.py:498
  531.3 24.3 %attend_bwd.3 = (bf16[1,512,1152]{2,1,0:T(8,128)(2,1)}, f32[4,16,768]{2,1,0:T(8,128)}, f32[1,128]{1,0:T(1,128)}, f32[1,384]{1,0:T(1,128)}) custom-call(f32[264]{0:T(512)} %dynamic_slice.169.kern_ref, f32[8]{0:T(128)} %dynamic_slice.170.mix_ref, bf16[1,512,1152]{2,1,0:T(8,128)(2,1)} %fusion.21.qkv_ref, f32[1,384]{1,0:T(1,128)} %constant_dynamic-slice_fusion.15.gain_ref, ...), custom_call_target="tpu_custom_call" | custom-call | tf_op jit(solution)/shard_map/attend_bwd/pallas_call | solution.py:380
  555.6 6.9 %convolution_convert_fusion = bf16[1536,1152]{1,0:T(8,128)(2,1)S(1)} fusion(bf16[512,1536]{1,0:T(8,128)(2,1)} %copy-done.33, bf16[512,1536]{1,0:T(8,128)(2,1)} %fusion.6, bf16[512,1152]{1,0:T(8,128)(2,1)} %bitcast.174, bf16[512,1152]{1,0:T(8,128)(2,1)} %bitcast.173), kind=kOutput, calls=%fused_computation.1 | convolution fusion | flops 3636658176 | bytes 9043968 | tf_op jit(solution)/shard_map/dot_general | solution.py:30
  566.2 6.2 fusion.5
  590.5 5.8 collective-permute-done.78
  600.8 6.2 collective-permute-done.79
  (527 shorter events, 336.4 us)
Async XLA Ops:
  7.2 81.8 %all-gather.9.cloned.1.call-start = ((), (), s32[]{:S(2)}) async-start(), calls=%async_computation.4 | async-start | bytes 3981312 | tf_op jit(solution)/shard_map/all_gather | solution.py:429
  26.7 23.2 %collective-permute-start = (bf16[128,1536]{1,0:T(8,128)(2,1)}, bf16[128,1536]{1,0:T(8,128)(2,1)}, u32[]{:S(2)}, u32[]{:S(2)}) collective-permute-start(bf16[128,1536]{1,0:T(8,128)(2,1)} %get-tuple-element.205), channel_id=1, source_target_pairs={{0,1},{1,2},{2,3},{3,7},{7,6},{6,5},{5,4},{4,0},{8,9},{9,10},{10,1... | collective-permute-start | bytes 1179656 | tf_op jit(solution)/shard_map/ppermute | solution.py:461
  28.2 21.7 %collective-permute-start.1 = (bf16[128,1536]{1,0:T(8,128)(2,1)}, bf16[128,1536]{1,0:T(8,128)(2,1)}, u32[]{:S(2)}, u32[]{:S(2)}) collective-permute-start(bf16[128,1536]{1,0:T(8,128)(2,1)} %get-tuple-element.205), channel_id=1, source_target_pairs={{1,0},{2,1},{3,2},{7,3},{6,7},{5,6},{4,5},{0,4},{9,8},{10,9},{11,1... | collective-permute-start | bytes 1179656 | tf_op jit(solution)/shard_map/ppermute | solution.py:462
  50.7 65.0 %all-gather.11.cloned.1.call-start = ((), (), s32[]{:S(2)}) async-start(), calls=%async_computation.5 | async-start | bytes 1327104 | tf_op jit(solution)/shard_map/all_gather | solution.py:429
  51.4 175.1 %all-gather.19.cloned.1.call-start = ((), (), s32[]{:S(2)}) async-start(), calls=%async_computation.13 | async-start | bytes 1966080 | tf_op jit(solution)/shard_map/all_gather | solution.py:599
  52.4 195.8 %all-gather.15.cloned.1.call-start = ((), (), s32[]{:S(2)}) async-start(), calls=%async_computation.7 | async-start | bytes 7077888 | tf_op jit(solution)/shard_map/all_gather | solution.py:429
  53.5 203.8 %all-gather.13.cloned.1.call-start = ((), (), s32[]{:S(2)}) async-start(), calls=%async_computation.6 | async-start | bytes 3538944 | tf_op jit(solution)/shard_map/all_gather | solution.py:429
  54.1 227.2 %all-gather.17.cloned.1.call-start = ((), (), s32[]{:S(2)}) async-start(), calls=%async_computation.12 | async-start | bytes 1966080 | tf_op jit(solution)/shard_map/all_gather | solution.py:599
  98.2 22.6 %collective-permute-start.25 = (bf16[128,1536]{1,0:T(8,128)(2,1)S(1)}, bf16[128,1536]{1,0:T(8,128)(2,1)}, u32[]{:S(2)}, u32[]{:S(2)}) collective-permute-start(bf16[128,1536]{1,0:T(8,128)(2,1)S(1)} %collective-permute-done.24), channel_id=1, source_target_pairs={{1,0},{2,1},{3,2},{7,3},{6,7},{5,6},{4,5},{0,4},{9,8},{10,9},{11,1... | collective-permute-start | bytes 1179656 | tf_op jit(solution)/shard_map/ppermute | solution.py:462
  98.2 23.9 %collective-permute-start.26 = (bf16[128,1536]{1,0:T(8,128)(2,1)S(1)}, bf16[128,1536]{1,0:T(8,128)(2,1)S(1)}, u32[]{:S(2)}, u32[]{:S(2)}) collective-permute-start(bf16[128,1536]{1,0:T(8,128)(2,1)S(1)} %collective-permute-done.22), channel_id=1, source_target_pairs={{0,1},{1,2},{2,3},{3,7},{7,6},{6,5},{5,4},{4,0},{8,9},{9,10},{10,1... | collective-permute-start | bytes 1179656 | tf_op jit(solution)/shard_map/ppermute | solution.py:461
  119.0 29.6 %collective-permute-start.15 = (bf16[128,1536]{1,0:T(8,128)(2,1)}, bf16[128,1536]{1,0:T(8,128)(2,1)}, u32[]{:S(2)}, u32[]{:S(2)}) collective-permute-start(bf16[128,1536]{1,0:T(8,128)(2,1)} %get-tuple-element.188), channel_id=1, source_target_pairs={{0,1},{1,2},{2,3},{3,7},{7,6},{6,5},{5,4},{4,0},{8,9},{9,10},{10,1... | collective-permute-start | bytes 1179656 | tf_op jit(solution)/shard_map/ppermute | solution.py:498
  120.8 44.4 %collective-permute-start.18 = (bf16[128,1536]{1,0:T(8,128)(2,1)}, bf16[128,1536]{1,0:T(8,128)(2,1)}, u32[]{:S(2)}, u32[]{:S(2)}) collective-permute-start(bf16[128,1536]{1,0:T(8,128)(2,1)} %get-tuple-element.189), channel_id=1, source_target_pairs={{1,0},{2,1},{3,2},{7,3},{6,7},{5,6},{4,5},{0,4},{9,8},{10,9},{11,1... | collective-permute-start | bytes 1179656 | tf_op jit(solution)/shard_map/ppermute | solution.py:499
  148.7 22.6 %collective-permute-start.30 = (bf16[128,1536]{1,0:T(8,128)(2,1)S(1)}, bf16[128,1536]{1,0:T(8,128)(2,1)S(1)}, u32[]{:S(2)}, u32[]{:S(2)}) collective-permute-start(bf16[128,1536]{1,0:T(8,128)(2,1)S(1)} %get-tuple-element.193), channel_id=1, source_target_pairs={{1,0},{2,1},{3,2},{7,3},{6,7},{5,6},{4,5},{0,4},{9,8},{10,9},{11,1... | collective-permute-start | bytes 1179656 | tf_op jit(solution)/shard_map/ppermute | solution.py:499
  169.1 20.7 %collective-permute-start.17 = (bf16[128,1536]{1,0:T(8,128)(2,1)}, bf16[128,1536]{1,0:T(8,128)(2,1)S(1)}, u32[]{:S(2)}, u32[]{:S(2)}) collective-permute-start(bf16[128,1536]{1,0:T(8,128)(2,1)} %get-tuple-element.186), channel_id=1, source_target_pairs={{0,1},{1,2},{2,3},{3,7},{7,6},{6,5},{5,4},{4,0},{8,9},{9,10},{10,1... | collective-permute-start | bytes 1179656 | tf_op jit(solution)/shard_map/ppermute | solution.py:498
  189.0 342.3 %reduce-scatter.5.cloned.1.call-start = ((), (), s32[]{:S(2)}) async-start(), calls=%async_computation.8 | async-start | bytes 7077888 | tf_op jit(solution)/shard_map/reduce_scatter | solution.py:433
  230.0 43.2 %collective-permute-start.42 = (bf16[128,1536]{1,0:T(8,128)(2,1)S(1)}, bf16[128,1536]{1,0:T(8,128)(2,1)S(1)}, u32[]{:S(2)}, u32[]{:S(2)}) collective-permute-start(bf16[128,1536]{1,0:T(8,128)(2,1)S(1)} %collective-permute-done.41), channel_id=1, source_target_pairs={{0,1},{1,2},{2,3},{3,7},{7,6},{6,5},{5,4},{4,0},{8,9},{9,10},{10,1... | collective-permute-start | bytes 1179656 | tf_op jit(solution)/shard_map/ppermute | solution.py:461
  234.9 38.3 %collective-permute-start.44 = (bf16[128,1536]{1,0:T(8,128)(2,1)S(1)}, bf16[128,1536]{1,0:T(8,128)(2,1)}, u32[]{:S(2)}, u32[]{:S(2)}) collective-permute-start(bf16[128,1536]{1,0:T(8,128)(2,1)S(1)} %collective-permute-done.43), channel_id=1, source_target_pairs={{1,0},{2,1},{3,2},{7,3},{6,7},{5,6},{4,5},{0,4},{9,8},{10,9},{11,1... | collective-permute-start | bytes 1179656 | tf_op jit(solution)/shard_map/ppermute | solution.py:462
  273.2 22.0 %collective-permute-start.45 = (bf16[128,1536]{1,0:T(8,128)(2,1)}, bf16[128,1536]{1,0:T(8,128)(2,1)}, u32[]{:S(2)}, u32[]{:S(2)}) collective-permute-start(bf16[128,1536]{1,0:T(8,128)(2,1)} %collective-permute-done.44), channel_id=1, source_target_pairs={{1,0},{2,1},{3,2},{7,3},{6,7},{5,6},{4,5},{0,4},{9,8},{10,9},{11,1... | collective-permute-start | bytes 1179656 | tf_op jit(solution)/shard_map/ppermute | solution.py:462
  274.6 24.4 %collective-permute-start.46 = (bf16[128,1536]{1,0:T(8,128)(2,1)S(1)}, bf16[128,1536]{1,0:T(8,128)(2,1)}, u32[]{:S(2)}, u32[]{:S(2)}) collective-permute-start(bf16[128,1536]{1,0:T(8,128)(2,1)S(1)} %collective-permute-done.42), channel_id=1, source_target_pairs={{0,1},{1,2},{2,3},{3,7},{7,6},{6,5},{5,4},{4,0},{8,9},{9,10},{10,1... | collective-permute-start | bytes 1179656 | tf_op jit(solution)/shard_map/ppermute | solution.py:461
  324.5 231.1 %reduce-scatter.9.cloned.1.call-start = ((), (), s32[]{:S(2)}) async-start(), calls=%async_computation.10 | async-start | bytes 3538944 | tf_op jit(solution)/shard_map/reduce_scatter | solution.py:433
  383.9 213.4 %reduce-scatter.7.cloned.1.call-start = ((), (), s32[]{:S(2)}) async-start(), calls=%async_computation.9 | async-start | bytes 3932160 | tf_op jit(solution)/shard_map/reduce_scatter | solution.py:670
  427.0 204.5 %reduce-scatter.11.cloned.1.call-start = ((), (), s32[]{:S(2)}) async-start(), calls=%async_computation.11 | async-start | bytes 5308416 | tf_op jit(solution)/shard_map/reduce_scatter | solution.py:433
  440.9 37.9 %collective-permute-start.56 = (bf16[128,1536]{1,0:T(8,128)(2,1)S(1)}, bf16[128,1536]{1,0:T(8,128)(2,1)S(1)}, u32[]{:S(2)}, u32[]{:S(2)}) collective-permute-start(bf16[128,1536]{1,0:T(8,128)(2,1)S(1)} %collective-permute-done.55), channel_id=1, source_target_pairs={{0,1},{1,2},{2,3},{3,7},{7,6},{6,5},{5,4},{4,0},{8,9},{9,10},{10,1... | collective-permute-start | bytes 1179656 | tf_op jit(solution)/shard_map/ppermute | solution.py:461
  443.4 35.4 %collective-permute-start.58 = (bf16[128,1536]{1,0:T(8,128)(2,1)S(1)}, bf16[128,1536]{1,0:T(8,128)(2,1)}, u32[]{:S(2)}, u32[]{:S(2)}) collective-permute-start(bf16[128,1536]{1,0:T(8,128)(2,1)S(1)} %collective-permute-done.57), channel_id=1, source_target_pairs={{1,0},{2,1},{3,2},{7,3},{6,7},{5,6},{4,5},{0,4},{9,8},{10,9},{11,1... | collective-permute-start | bytes 1179656 | tf_op jit(solution)/shard_map/ppermute | solution.py:462
  478.8 26.9 %collective-permute-start.67 = (bf16[128,1536]{1,0:T(8,128)(2,1)}, bf16[128,1536]{1,0:T(8,128)(2,1)S(1)}, u32[]{:S(2)}, u32[]{:S(2)}) collective-permute-start(bf16[128,1536]{1,0:T(8,128)(2,1)} %collective-permute-done.58), channel_id=1, source_target_pairs={{1,0},{2,1},{3,2},{7,3},{6,7},{5,6},{4,5},{0,4},{9,8},{10,9},{11,1... | collective-permute-start | bytes 1179656 | tf_op jit(solution)/shard_map/ppermute | solution.py:462
  478.8 33.6 %collective-permute-start.68 = (bf16[128,1536]{1,0:T(8,128)(2,1)S(1)}, bf16[128,1536]{1,0:T(8,128)(2,1)S(1)}, u32[]{:S(2)}, u32[]{:S(2)}) collective-permute-start(bf16[128,1536]{1,0:T(8,128)(2,1)S(1)} %collective-permute-done.56), channel_id=1, source_target_pairs={{0,1},{1,2},{2,3},{3,7},{7,6},{6,5},{5,4},{4,0},{8,9},{9,10},{10,1... | collective-permute-start | bytes 1179656 | tf_op jit(solution)/shard_map/ppermute | solution.py:461
  480.8 42.3 %collective-permute-start.72 = (bf16[128,1536]{1,0:T(8,128)(2,1)}, bf16[128,1536]{1,0:T(8,128)(2,1)}, u32[]{:S(2)}, u32[]{:S(2)}) collective-permute-start(bf16[128,1536]{1,0:T(8,128)(2,1)} %get-tuple-element.175), channel_id=1, source_target_pairs={{1,0},{2,1},{3,2},{7,3},{6,7},{5,6},{4,5},{0,4},{9,8},{10,9},{11,1... | collective-permute-start | bytes 1179656 | tf_op jit(solution)/shard_map/ppermute | solution.py:499
  497.7 25.4 %collective-permute-start.70 = (bf16[128,1536]{1,0:T(8,128)(2,1)}, bf16[128,1536]{1,0:T(8,128)(2,1)}, u32[]{:S(2)}, u32[]{:S(2)}) collective-permute-start(bf16[128,1536]{1,0:T(8,128)(2,1)} %add_convert_fusion.8), channel_id=1, source_target_pairs={{0,1},{1,2},{2,3},{3,7},{7,6},{6,5},{5,4},{4,0},{8,9},{9,10},{10,1... | collective-permute-start | bytes 1179656 | tf_op jit(solution)/shard_map/ppermute | solution.py:498
  525.3 52.4 %collective-permute-start.73 = (bf16[128,1536]{1,0:T(8,128)(2,1)}, bf16[128,1536]{1,0:T(8,128)(2,1)}, u32[]{:S(2)}, u32[]{:S(2)}) collective-permute-start(bf16[128,1536]{1,0:T(8,128)(2,1)} %get-tuple-element.173), channel_id=1, source_target_pairs={{1,0},{2,1},{3,2},{7,3},{6,7},{5,6},{4,5},{0,4},{9,8},{10,9},{11,1... | collective-permute-start | bytes 1179656 | tf_op jit(solution)/shard_map/ppermute | solution.py:499
  527.8 98.1 %collective-permute-start.71 = (bf16[128,1536]{1,0:T(8,128)(2,1)}, bf16[128,1536]{1,0:T(8,128)(2,1)}, u32[]{:S(2)}, u32[]{:S(2)}) collective-permute-start(bf16[128,1536]{1,0:T(8,128)(2,1)} %get-tuple-element.172), channel_id=1, source_target_pairs={{0,1},{1,2},{2,3},{3,7},{7,6},{6,5},{5,4},{4,0},{8,9},{9,10},{10,1... | collective-permute-start | bytes 1179656 | tf_op jit(solution)/shard_map/ppermute | solution.py:498
  579.8 46.2 %collective-permute-start.74 = (bf16[128,1536]{1,0:T(8,128)(2,1)}, bf16[128,1536]{1,0:T(8,128)(2,1)S(1)}, u32[]{:S(2)}, u32[]{:S(2)}) collective-permute-start(bf16[128,1536]{1,0:T(8,128)(2,1)} %add_convert_fusion.5), channel_id=1, source_target_pairs={{1,0},{2,1},{3,2},{7,3},{6,7},{5,6},{4,5},{0,4},{9,8},{10,9},{11,1... | collective-permute-start | bytes 1179656 | tf_op jit(solution)/shard_map/ppermute | solution.py:499
  600.8 25.2 %collective-permute-start.77 = (bf16[128,1536]{1,0:T(8,128)(2,1)}, bf16[128,1536]{1,0:T(8,128)(2,1)S(1)}, u32[]{:S(2)}, u32[]{:S(2)}) collective-permute-start(bf16[128,1536]{1,0:T(8,128)(2,1)} %get-tuple-element.168), channel_id=1, source_target_pairs={{0,1},{1,2},{2,3},{3,7},{7,6},{6,5},{5,4},{4,0},{8,9},{9,10},{10,1... | collective-permute-start | bytes 1179656 | tf_op jit(solution)/shard_map/ppermute | solution.py:498
  (146 other events, 1421.8 us)
Sparse Core Ops, SparseCore 0:
  50.8 34.1 all-gather.8
  87.4 24.1 all-gather.10
  113.1 46.8 all-gather.18
  162.3 44.9 all-gather.14
  209.0 32.1 all-gather.12
  242.7 38.5 all-gather.16
  324.6 61.1 reduce-scatter.4
  389.2 46.0 reduce-scatter.8
  437.6 84.5 reduce-scatter.6
  565.2 55.1 reduce-scatter.10

commit v4 on v3

--- a/solution.py
+++ b/solution.py
@@ -462,8 +462,7 @@
         second.append(lax.ppermute(two, ("batch", "seq"), back))
     if hops is not None:
         hops += [(one, two) for one, two in zip(first[1:], second[1:])]
-    out = jnp.zeros((count * rows, value.shape[1]), value.dtype)
-    out = lax.dynamic_update_slice(out, value, (here * rows, 0))
+    out = jnp.broadcast_to(value[None], (count, *value.shape)).reshape(count * rows, -1)
     for step in range(1, count):
         source = here - side * step
         near = jnp.logical_and(source >= 0, source < count)

time: 664 us -> 679 us (1.023)
  local copies, waits for them, and re-layouts: 41.4 us -> 54.5 us
    ppermute x18, waiting for transfers between devices: 70.1 us -> 55.6 us  [seq_scatter(): first = lax.ppermute(one, ('batch', 'seq'), ahead)]
    ppermute x18, waiting for transfers between devices: 66.6 us -> 80.5 us  [seq_gather(): second.append(lax.ppermute(two, ('batch', 'seq'), back))]
    ppermute x18, waiting for transfers between devices: 20.8 us -> 10.9 us  [seq_gather(): first.append(lax.ppermute(one, ('batch', 'seq'), ahead))]
    unnamed x160 -> x166, local copies, waits for them, and re-layouts: 13.6 us -> 14.6 us
  transfers between devices with their start and end apart: 100 -> 100, of which waited for: 45 -> 45; matrix products, arithmetic and copies ran while one was open for 28% -> 29% of each run, Pallas kernels for 12% -> 12%
where the time goes in v4:
time: 679 us; the launch traced here: 668 us
  waiting for transfers between devices  220 us (32%)
  starting transfers between devices  117 us (17%)
  matrix products  98.3 us (14%)
  other arithmetic  82.4 us (12%)
  Pallas kernels  79.1 us (12%)
  local copies, waits for them, and re-layouts  54.5 us (8%)
  between operations  16.3 us (2%)
    ppermute x18, waiting for transfers between devices, seq_gather(): second.append(lax.ppermute(two, ('batch', 'seq'), back))  80.5 us
    ppermute x18, waiting for transfers between devices, seq_scatter(): first = lax.ppermute(one, ('batch', 'seq'), ahead)  55.6 us
    pallas_call x2, Pallas kernels, attend_bwd(): pl.pallas_call(attend_bwd_body, grid=(seqs,), in_specs=[smem, smem, wide,...  48.6 us
    ppermute x18, waiting for transfers between devices, seq_scatter(): second = lax.ppermute(two, ('batch', 'seq'), back)  44.3 us
    ppermute x18, starting transfers between devices, seq_scatter(): first = lax.ppermute(one, ('batch', 'seq'), ahead)  41.6 us
    dot_general x8, matrix products, nn(): lax.dot_general(left, right, (((1,), (0,)), ((), ())), preferred_element_...  39.8 us
    ppermute x18, starting transfers between devices, seq_gather(): first.append(lax.ppermute(one, ('batch', 'seq'), ahead))  34.7 us
    dot_general x8, matrix products, nt(): lax.dot_general(left, right, (((1,), (1,)), ((), ())), preferred_element_...  31.3 us
  transfers between devices with their start and end apart: 100, of which 45 were waited for; matrix products, arithmetic and copies ran while one was open for 29% of the time, Pallas kernels for 12%

profile of v4, /device:TPU:0, one launch (start us, length us, event | category | flops | bytes accessed | tf_op | source)
XLA Modules:
  0.0 668.4 jit_solution(8905208562884717660)
XLA Ops:
  34.7 17.1 %collective-permute-done.12 = bf16[1,48,1152]{2,1,0:T(8,128)(2,1)S(1)} collective-permute-done((bf16[1,48,1152]{2,1,0:T(8,128)(2,1)}, bf16[1,48,1152]{2,1,0:T(8,128)(2,1)S(1)}, u32[]{:S(2)}, u32[]{:S(2)}) %collective-permute-start.12) | collective-permute-done | bytes 110624 | tf_op jit(solution)/shard_map/ppermute | solution.py:513
  58.2 6.6 collective-permute-done.2
  71.4 5.4 collective-permute-done.3
  87.7 5.2 fusion.20.qkv_ref
  98.8 15.4 %attend_fwd.2 = (bf16[1,512,384]{2,1,0:T(8,128)(2,1)}, f32[1,512,384]{2,1,0:T(8,128)}, f32[1,2,2,512,512]{4,3,2,1,0:T(8,128)}) custom-call(f32[264]{0:T(512)} %dynamic_slice.169.kern_ref, f32[8]{0:T(128)} %dynamic_slice.170.mix_ref, bf16[1,512,1152]{2,1,0:T(8,128)(2,1)} %fusion.20.qkv_ref, f32[1,384]{1,0:T(1,128)} %constant_dynamic-slice_fusion.15.gain_ref), custom_call_target="tpu_custom_call" | custom-call | tf_op jit(solution)/shard_map/attend_fwd/pallas_call | solution.py:346
  128.8 15.1 %attend_fwd.3 = (bf16[1,512,384]{2,1,0:T(8,128)(2,1)}, f32[1,512,384]{2,1,0:T(8,128)}, f32[1,2,2,512,512]{4,3,2,1,0:T(8,128)}) custom-call(f32[264]{0:T(512)} %dynamic_slice.169.kern_ref, f32[8]{0:T(128)} %dynamic_slice.170.mix_ref, bf16[1,512,1152]{2,1,0:T(8,128)(2,1)} %fusion.21.qkv_ref, f32[1,384]{1,0:T(1,128)} %constant_dynamic-slice_fusion.15.gain_ref), custom_call_target="tpu_custom_call" | custom-call | tf_op jit(solution)/shard_map/attend_fwd/pallas_call | solution.py:346
  151.6 9.5 %collective-permute-done.27 = bf16[128,1536]{1,0:T(8,128)(2,1)S(1)} collective-permute-done((bf16[128,1536]{1,0:T(8,128)(2,1)S(1)}, bf16[128,1536]{1,0:T(8,128)(2,1)S(1)}, u32[]{:S(2)}, u32[]{:S(2)}) %collective-permute-start.27) | collective-permute-done | bytes 393248 | tf_op jit(solution)/shard_map/ppermute | solution.py:497
  173.0 8.8 %collective-permute-done.19 = bf16[128,1536]{1,0:T(8,128)(2,1)S(1)} collective-permute-done((bf16[128,1536]{1,0:T(8,128)(2,1)S(1)}, bf16[128,1536]{1,0:T(8,128)(2,1)S(1)}, u32[]{:S(2)}, u32[]{:S(2)}) %collective-permute-start.19) | collective-permute-done | bytes 393248 | tf_op jit(solution)/shard_map/ppermute | solution.py:498
  202.4 9.5 %collective-permute-done.34 = bf16[128,1536]{1,0:T(8,128)(2,1)} collective-permute-done((bf16[128,1536]{1,0:T(8,128)(2,1)}, bf16[128,1536]{1,0:T(8,128)(2,1)}, u32[]{:S(2)}, u32[]{:S(2)}) %collective-permute-start.34) | collective-permute-done | bytes 393248 | tf_op jit(solution)/shard_map/ppermute | solution.py:462
  247.9 8.9 %fusion.73 = f32[512,2048]{1,0:T(8,128)} fusion(bf16[512,1536]{1,0:T(8,128)(2,1)} %select_dynamic-update-slice_fusion.9, bf16[1536,2048]{1,0:T(8,128)(2,1)} %all-gather.15.cloned.1.call-done), kind=kOutput, calls=%fused_computation.225 | convolution fusion | flops 3221225472 | bytes 12058624 | tf_op jit(solution)/shard_map/dot_general | solution.py:22
  259.2 7.2 %multiply_convert_fusion.7 = (bf16[512,1024]{1,0:T(8,128)(2,1)S(1)}, bf16[512,1024]{1,0:T(8,128)(2,1)S(1)}, bf16[512,1024]{1,0:T(8,128)(2,1)}) fusion(f32[512,2048]{1,0:T(8,128)} %fusion.73, bf16[512,1536]{1,0:T(8,128)(2,1)} %fusion.30, bf16[1536,1024]{1,0:T(8,128)(2,1)} %all-gather.13.cloned.1.call-done), kind=kOutput, calls=%fused_computation.55 | convolution fusion | flops 1618477056 | bytes 12058624 | tf_op jit(solution)/shard_map/dot_general | solution.py:22
  273.5 10.7 %collective-permute-done.45 = bf16[128,1536]{1,0:T(8,128)(2,1)} collective-permute-done((bf16[128,1536]{1,0:T(8,128)(2,1)}, bf16[128,1536]{1,0:T(8,128)(2,1)}, u32[]{:S(2)}, u32[]{:S(2)}) %collective-permute-start.45) | collective-permute-done | bytes 393248 | tf_op jit(solution)/shard_map/ppermute | solution.py:462
  295.0 6.9 %fusion.74 = f32[512,2048]{1,0:T(8,128)S(1)} fusion(bf16[512,1536]{1,0:T(8,128)(2,1)} %select_dynamic-update-slice_fusion.6, bf16[1536,2048]{1,0:T(8,128)(2,1)} %all-gather.15.cloned.1.call-done), kind=kOutput, calls=%fused_computation.226 | convolution fusion | flops 3221225472 | bytes 12058624 | tf_op jit(solution)/shard_map/dot_general | solution.py:22
  305.7 5.7 fusion.75
  311.4 7.2 %add_convert_fusion = bf16[1536,2048]{1,0:T(8,128)(2,1)} fusion(f32[1536,2048]{1,0:T(8,128)S(1)} %fusion.75, bf16[512,1536]{1,0:T(8,128)(2,1)} %select_dynamic-update-slice_fusion.9, bf16[512,2048]{1,0:T(8,128)(2,1)S(1)} %copy-done.23), kind=kOutput, calls=%fused_computation | convolution fusion | flops 3227516928 | bytes 22544384 | tf_op jit(solution)/shard_map/dot_general | solution.py:30
  322.8 9.0 %collective-permute-done.48 = bf16[128,1536]{1,0:T(8,128)(2,1)S(1)} collective-permute-done((bf16[128,1536]{1,0:T(8,128)(2,1)S(1)}, bf16[128,1536]{1,0:T(8,128)(2,1)S(1)}, u32[]{:S(2)}, u32[]{:S(2)}) %collective-permute-start.48) | collective-permute-done | bytes 393248 | tf_op jit(solution)/shard_map/ppermute | solution.py:498
  331.9 7.0 %convolution_convert_fusion.6 = bf16[512,1536]{1,0:T(8,128)(2,1)S(1)} fusion(bf16[512,2048]{1,0:T(8,128)(2,1)S(1)} %copy-done.25, bf16[1536,2048]{1,0:T(8,128)(2,1)} %all-gather.15.cloned.1.call-done), kind=kOutput, calls=%fused_computation.33 | convolution fusion | flops 3222011904 | bytes 9961472 | tf_op jit(solution)/shard_map/dot_general | solution.py:26
  341.7 7.5 %collective-permute-done.49 = bf16[128,1536]{1,0:T(8,128)(2,1)S(1)} collective-permute-done((bf16[128,1536]{1,0:T(8,128)(2,1)S(1)}, bf16[128,1536]{1,0:T(8,128)(2,1)S(1)}, u32[]{:S(2)}, u32[]{:S(2)}) %collective-permute-start.49) | collective-permute-done | bytes 393248 | tf_op jit(solution)/shard_map/ppermute | solution.py:497
  354.1 7.1 %collective-permute-done.50 = bf16[128,1536]{1,0:T(8,128)(2,1)S(1)} collective-permute-done((bf16[128,1536]{1,0:T(8,128)(2,1)S(1)}, bf16[128,1536]{1,0:T(8,128)(2,1)S(1)}, u32[]{:S(2)}, u32[]{:S(2)}) %collective-permute-start.50) | collective-permute-done | bytes 393248 | tf_op jit(solution)/shard_map/ppermute | solution.py:497
  362.2 7.4 %collective-permute-done.59 = bf16[128,1536]{1,0:T(8,128)(2,1)S(1)} collective-permute-done((bf16[128,1536]{1,0:T(8,128)(2,1)S(1)}, bf16[128,1536]{1,0:T(8,128)(2,1)S(1)}, u32[]{:S(2)}, u32[]{:S(2)}) %collective-permute-start.59) | collective-permute-done | bytes 393248 | tf_op jit(solution)/shard_map/ppermute | solution.py:497
  391.0 7.9 %collective-permute-done.62 = bf16[128,1536]{1,0:T(8,128)(2,1)S(1)} collective-permute-done((bf16[128,1536]{1,0:T(8,128)(2,1)S(1)}, bf16[128,1536]{1,0:T(8,128)(2,1)S(1)}, u32[]{:S(2)}, u32[]{:S(2)}) %collective-permute-start.62) | collective-permute-done | bytes 393248 | tf_op jit(solution)/shard_map/ppermute | solution.py:462
  402.7 5.3 collective-permute-done.63
  424.6 9.8 %collective-permute-done.57 = bf16[128,1536]{1,0:T(8,128)(2,1)} collective-permute-done((bf16[128,1536]{1,0:T(8,128)(2,1)S(1)}, bf16[128,1536]{1,0:T(8,128)(2,1)}, u32[]{:S(2)}, u32[]{:S(2)}) %collective-permute-start.57) | collective-permute-done | bytes 393248 | tf_op jit(solution)/shard_map/ppermute | solution.py:462
  436.4 24.5 %attend_bwd.2 = (bf16[1,512,1152]{2,1,0:T(8,128)(2,1)}, f32[4,16,768]{2,1,0:T(8,128)}, f32[1,128]{1,0:T(1,128)}, f32[1,384]{1,0:T(1,128)}) custom-call(f32[264]{0:T(512)} %dynamic_slice.169.kern_ref, f32[8]{0:T(128)} %dynamic_slice.170.mix_ref, bf16[1,512,1152]{2,1,0:T(8,128)(2,1)} %fusion.20.qkv_ref, f32[1,384]{1,0:T(1,128)} %constant_dynamic-slice_fusion.15.gain_ref, ...), custom_call_target="tpu_custom_call" | custom-call | tf_op jit(solution)/shard_map/attend_bwd/pallas_call | solution.py:380
  471.1 15.8 %collective-permute-done.69 = bf16[128,1536]{1,0:T(8,128)(2,1)S(1)} collective-permute-done((bf16[128,1536]{1,0:T(8,128)(2,1)S(1)}, bf16[128,1536]{1,0:T(8,128)(2,1)S(1)}, u32[]{:S(2)}, u32[]{:S(2)}) %collective-permute-start.69) | collective-permute-done | bytes 393248 | tf_op jit(solution)/shard_map/ppermute | solution.py:497
  488.8 6.9 %collective-permute-start.70 = (bf16[128,1536]{1,0:T(8,128)(2,1)}, bf16[128,1536]{1,0:T(8,128)(2,1)}, u32[]{:S(2)}, u32[]{:S(2)}) collective-permute-start(bf16[128,1536]{1,0:T(8,128)(2,1)} %add_convert_fusion.8), channel_id=1, source_target_pairs={{0,1},{1,2},{2,3},{3,7},{7,6},{6,5},{5,4},{4,0},{8,9},{9,10},{10,1... | collective-permute-start | bytes 1179656 | tf_op jit(solution)/shard_map/ppermute | solution.py:497
  497.5 5.9 collective-permute-done.68
  516.5 5.6 collective-permute-start.71
  522.0 24.1 %attend_bwd.3 = (bf16[1,512,1152]{2,1,0:T(8,128)(2,1)}, f32[4,16,768]{2,1,0:T(8,128)}, f32[1,128]{1,0:T(1,128)}, f32[1,384]{1,0:T(1,128)}) custom-call(f32[264]{0:T(512)} %dynamic_slice.169.kern_ref, f32[8]{0:T(128)} %dynamic_slice.170.mix_ref, bf16[1,512,1152]{2,1,0:T(8,128)(2,1)} %fusion.21.qkv_ref, f32[1,384]{1,0:T(1,128)} %constant_dynamic-slice_fusion.15.gain_ref, ...), custom_call_target="tpu_custom_call" | custom-call | tf_op jit(solution)/shard_map/attend_bwd/pallas_call | solution.py:380
  548.8 6.9 %convolution_convert_fusion = bf16[1536,1152]{1,0:T(8,128)(2,1)S(1)} fusion(bf16[512,1536]{1,0:T(8,128)(2,1)} %copy-done.28, bf16[512,1536]{1,0:T(8,128)(2,1)} %copy-done.27, bf16[512,1152]{1,0:T(8,128)(2,1)} %bitcast.182, bf16[512,1152]{1,0:T(8,128)(2,1)} %bitcast.181), kind=kOutput, calls=%fused_computation.1 | convolution fusion | flops 3636658176 | bytes 9043968 | tf_op jit(solution)/shard_map/dot_general | solution.py:30
  559.6 6.3 fusion.5
  610.3 6.0 collective-permute-done.79
  (529 shorter events, 350.0 us)
Async XLA Ops:
  7.2 80.5 %all-gather.9.cloned.1.call-start = ((), (), s32[]{:S(2)}) async-start(), calls=%async_computation.4 | async-start | bytes 3981312 | tf_op jit(solution)/shard_map/all_gather | solution.py:429
  26.0 26.4 %collective-permute-start = (bf16[128,1536]{1,0:T(8,128)(2,1)S(1)}, bf16[128,1536]{1,0:T(8,128)(2,1)}, u32[]{:S(2)}, u32[]{:S(2)}) collective-permute-start(bf16[128,1536]{1,0:T(8,128)(2,1)S(1)} %get-tuple-element.203), channel_id=1, source_target_pairs={{0,1},{1,2},{2,3},{3,7},{7,6},{6,5},{5,4},{4,0},{8,9},{9,10},{10,1... | collective-permute-start | bytes 1179656 | tf_op jit(solution)/shard_map/ppermute | solution.py:461
  27.5 25.0 %collective-permute-start.1 = (bf16[128,1536]{1,0:T(8,128)(2,1)S(1)}, bf16[128,1536]{1,0:T(8,128)(2,1)S(1)}, u32[]{:S(2)}, u32[]{:S(2)}) collective-permute-start(bf16[128,1536]{1,0:T(8,128)(2,1)S(1)} %get-tuple-element.203), channel_id=1, source_target_pairs={{1,0},{2,1},{3,2},{7,3},{6,7},{5,6},{4,5},{0,4},{9,8},{10,9},{11,1... | collective-permute-start | bytes 1179656 | tf_op jit(solution)/shard_map/ppermute | solution.py:462
  27.5 24.9 %collective-permute-start.14 = (bf16[48,1536]{1,0:T(8,128)(2,1)}, bf16[48,1536]{1,0:T(8,128)(2,1)S(1)}, u32[]{:S(2)}, u32[]{:S(2)}) collective-permute-start(bf16[48,1536]{1,0:T(8,128)(2,1)} %param.27), channel_id=1, source_target_pairs={{0,0},{1,4},{2,8},{3,12},{4,16},{5,20},{6,24},{7,28},{8,1},{9,5},{... | collective-permute-start | bytes 442376 | tf_op jit(solution)/shard_map/ppermute | solution.py:583
  29.1 23.3 %collective-permute-start.13 = (bf16[1,48,1152]{2,1,0:T(8,128)(2,1)}, bf16[1,48,1152]{2,1,0:T(8,128)(2,1)S(1)}, u32[]{:S(2)}, u32[]{:S(2)}) collective-permute-start(bf16[1,48,1152]{2,1,0:T(8,128)(2,1)} %get-tuple-element.209), channel_id=1, source_target_pairs={{0,3},{1,0},{2,1},{3,2},{4,7},{5,4},{6,5},{7,6},{8,11},{9,8},{10,9... | collective-permute-start | bytes 331784 | tf_op jit(solution)/shard_map/ppermute | solution.py:513
  53.2 61.0 %all-gather.11.cloned.1.call-start = ((), (), s32[]{:S(2)}) async-start(), calls=%async_computation.5 | async-start | bytes 1327104 | tf_op jit(solution)/shard_map/all_gather | solution.py:429
  54.0 168.5 %all-gather.19.cloned.1.call-start = ((), (), s32[]{:S(2)}) async-start(), calls=%async_computation.13 | async-start | bytes 1966080 | tf_op jit(solution)/shard_map/all_gather | solution.py:598
  55.0 192.9 %all-gather.15.cloned.1.call-start = ((), (), s32[]{:S(2)}) async-start(), calls=%async_computation.7 | async-start | bytes 7077888 | tf_op jit(solution)/shard_map/all_gather | solution.py:429
  56.1 203.1 %all-gather.13.cloned.1.call-start = ((), (), s32[]{:S(2)}) async-start(), calls=%async_computation.6 | async-start | bytes 3538944 | tf_op jit(solution)/shard_map/all_gather | solution.py:429
  64.8 226.2 %all-gather.17.cloned.1.call-start = ((), (), s32[]{:S(2)}) async-start(), calls=%async_computation.12 | async-start | bytes 1966080 | tf_op jit(solution)/shard_map/all_gather | solution.py:598
  96.7 22.2 %collective-permute-start.25 = (bf16[128,1536]{1,0:T(8,128)(2,1)}, bf16[128,1536]{1,0:T(8,128)(2,1)}, u32[]{:S(2)}, u32[]{:S(2)}) collective-permute-start(bf16[128,1536]{1,0:T(8,128)(2,1)} %collective-permute-done.24), channel_id=1, source_target_pairs={{1,0},{2,1},{3,2},{7,3},{6,7},{5,6},{4,5},{0,4},{9,8},{10,9},{11,1... | collective-permute-start | bytes 1179656 | tf_op jit(solution)/shard_map/ppermute | solution.py:462
  97.3 24.0 %collective-permute-start.26 = (bf16[128,1536]{1,0:T(8,128)(2,1)}, bf16[128,1536]{1,0:T(8,128)(2,1)}, u32[]{:S(2)}, u32[]{:S(2)}) collective-permute-start(bf16[128,1536]{1,0:T(8,128)(2,1)} %collective-permute-done.22), channel_id=1, source_target_pairs={{0,1},{1,2},{2,3},{3,7},{7,6},{6,5},{5,4},{4,0},{8,9},{9,10},{10,1... | collective-permute-start | bytes 1179656 | tf_op jit(solution)/shard_map/ppermute | solution.py:461
  117.6 30.8 %collective-permute-start.15 = (bf16[128,1536]{1,0:T(8,128)(2,1)}, bf16[128,1536]{1,0:T(8,128)(2,1)}, u32[]{:S(2)}, u32[]{:S(2)}) collective-permute-start(bf16[128,1536]{1,0:T(8,128)(2,1)} %get-tuple-element.184), channel_id=1, source_target_pairs={{0,1},{1,2},{2,3},{3,7},{7,6},{6,5},{5,4},{4,0},{8,9},{9,10},{10,1... | collective-permute-start | bytes 1179656 | tf_op jit(solution)/shard_map/ppermute | solution.py:497
  118.9 44.8 %collective-permute-start.18 = (bf16[128,1536]{1,0:T(8,128)(2,1)}, bf16[128,1536]{1,0:T(8,128)(2,1)}, u32[]{:S(2)}, u32[]{:S(2)}) collective-permute-start(bf16[128,1536]{1,0:T(8,128)(2,1)} %get-tuple-element.185), channel_id=1, source_target_pairs={{1,0},{2,1},{3,2},{7,3},{6,7},{5,6},{4,5},{0,4},{9,8},{10,9},{11,1... | collective-permute-start | bytes 1179656 | tf_op jit(solution)/shard_map/ppermute | solution.py:498
  200.3 321.7 %reduce-scatter.5.cloned.1.call-start = ((), (), s32[]{:S(2)}) async-start(), calls=%async_computation.8 | async-start | bytes 7077888 | tf_op jit(solution)/shard_map/reduce_scatter | solution.py:433
  230.9 25.9 %collective-permute-start.44 = (bf16[128,1536]{1,0:T(8,128)(2,1)}, bf16[128,1536]{1,0:T(8,128)(2,1)}, u32[]{:S(2)}, u32[]{:S(2)}) collective-permute-start(bf16[128,1536]{1,0:T(8,128)(2,1)} %collective-permute-done.43), channel_id=1, source_target_pairs={{1,0},{2,1},{3,2},{7,3},{6,7},{5,6},{4,5},{0,4},{9,8},{10,9},{11,1... | collective-permute-start | bytes 1179656 | tf_op jit(solution)/shard_map/ppermute | solution.py:462
  230.9 25.9 %collective-permute-start.42 = (bf16[128,1536]{1,0:T(8,128)(2,1)}, bf16[128,1536]{1,0:T(8,128)(2,1)}, u32[]{:S(2)}, u32[]{:S(2)}) collective-permute-start(bf16[128,1536]{1,0:T(8,128)(2,1)} %collective-permute-done.41), channel_id=1, source_target_pairs={{0,1},{1,2},{2,3},{3,7},{7,6},{6,5},{5,4},{4,0},{8,9},{9,10},{10,1... | collective-permute-start | bytes 1179656 | tf_op jit(solution)/shard_map/ppermute | solution.py:461
  256.8 27.4 %collective-permute-start.45 = (bf16[128,1536]{1,0:T(8,128)(2,1)}, bf16[128,1536]{1,0:T(8,128)(2,1)}, u32[]{:S(2)}, u32[]{:S(2)}) collective-permute-start(bf16[128,1536]{1,0:T(8,128)(2,1)} %collective-permute-done.44), channel_id=1, source_target_pairs={{1,0},{2,1},{3,2},{7,3},{6,7},{5,6},{4,5},{0,4},{9,8},{10,9},{11,1... | collective-permute-start | bytes 1179656 | tf_op jit(solution)/shard_map/ppermute | solution.py:462
  258.8 30.4 %collective-permute-start.46 = (bf16[128,1536]{1,0:T(8,128)(2,1)}, bf16[128,1536]{1,0:T(8,128)(2,1)}, u32[]{:S(2)}, u32[]{:S(2)}) collective-permute-start(bf16[128,1536]{1,0:T(8,128)(2,1)} %collective-permute-done.42), channel_id=1, source_target_pairs={{0,1},{1,2},{2,3},{3,7},{7,6},{6,5},{5,4},{4,0},{8,9},{9,10},{10,1... | collective-permute-start | bytes 1179656 | tf_op jit(solution)/shard_map/ppermute | solution.py:461
  318.6 227.5 %reduce-scatter.9.cloned.1.call-start = ((), (), s32[]{:S(2)}) async-start(), calls=%async_computation.10 | async-start | bytes 3538944 | tf_op jit(solution)/shard_map/reduce_scatter | solution.py:433
  379.8 226.2 %reduce-scatter.7.cloned.1.call-start = ((), (), s32[]{:S(2)}) async-start(), calls=%async_computation.9 | async-start | bytes 3932160 | tf_op jit(solution)/shard_map/reduce_scatter | solution.py:669
  421.8 223.3 %reduce-scatter.11.cloned.1.call-start = ((), (), s32[]{:S(2)}) async-start(), calls=%async_computation.11 | async-start | bytes 5308416 | tf_op jit(solution)/shard_map/reduce_scatter | solution.py:433
  434.4 34.7 %collective-permute-start.58 = (bf16[128,1536]{1,0:T(8,128)(2,1)}, bf16[128,1536]{1,0:T(8,128)(2,1)}, u32[]{:S(2)}, u32[]{:S(2)}) collective-permute-start(bf16[128,1536]{1,0:T(8,128)(2,1)} %collective-permute-done.57), channel_id=1, source_target_pairs={{1,0},{2,1},{3,2},{7,3},{6,7},{5,6},{4,5},{0,4},{9,8},{10,9},{11,1... | collective-permute-start | bytes 1179656 | tf_op jit(solution)/shard_map/ppermute | solution.py:462
  434.4 34.7 %collective-permute-start.56 = (bf16[128,1536]{1,0:T(8,128)(2,1)}, bf16[128,1536]{1,0:T(8,128)(2,1)}, u32[]{:S(2)}, u32[]{:S(2)}) collective-permute-start(bf16[128,1536]{1,0:T(8,128)(2,1)} %collective-permute-done.55), channel_id=1, source_target_pairs={{0,1},{1,2},{2,3},{3,7},{7,6},{6,5},{5,4},{4,0},{8,9},{9,10},{10,1... | collective-permute-start | bytes 1179656 | tf_op jit(solution)/shard_map/ppermute | solution.py:461
  469.1 27.0 %collective-permute-start.67 = (bf16[128,1536]{1,0:T(8,128)(2,1)}, bf16[128,1536]{1,0:T(8,128)(2,1)S(1)}, u32[]{:S(2)}, u32[]{:S(2)}) collective-permute-start(bf16[128,1536]{1,0:T(8,128)(2,1)} %collective-permute-done.58), channel_id=1, source_target_pairs={{1,0},{2,1},{3,2},{7,3},{6,7},{5,6},{4,5},{0,4},{9,8},{10,9},{11,1... | collective-permute-start | bytes 1179656 | tf_op jit(solution)/shard_map/ppermute | solution.py:462
  469.1 34.3 %collective-permute-start.68 = (bf16[128,1536]{1,0:T(8,128)(2,1)}, bf16[128,1536]{1,0:T(8,128)(2,1)S(1)}, u32[]{:S(2)}, u32[]{:S(2)}) collective-permute-start(bf16[128,1536]{1,0:T(8,128)(2,1)} %collective-permute-done.56), channel_id=1, source_target_pairs={{0,1},{1,2},{2,3},{3,7},{7,6},{6,5},{5,4},{4,0},{8,9},{9,10},{10,1... | collective-permute-start | bytes 1179656 | tf_op jit(solution)/shard_map/ppermute | solution.py:461
  471.1 43.1 %collective-permute-start.72 = (bf16[128,1536]{1,0:T(8,128)(2,1)S(1)}, bf16[128,1536]{1,0:T(8,128)(2,1)}, u32[]{:S(2)}, u32[]{:S(2)}) collective-permute-start(bf16[128,1536]{1,0:T(8,128)(2,1)S(1)} %get-tuple-element.167), channel_id=1, source_target_pairs={{1,0},{2,1},{3,2},{7,3},{6,7},{5,6},{4,5},{0,4},{9,8},{10,9},{11,1... | collective-permute-start | bytes 1179656 | tf_op jit(solution)/shard_map/ppermute | solution.py:498
  488.8 25.4 %collective-permute-start.70 = (bf16[128,1536]{1,0:T(8,128)(2,1)}, bf16[128,1536]{1,0:T(8,128)(2,1)}, u32[]{:S(2)}, u32[]{:S(2)}) collective-permute-start(bf16[128,1536]{1,0:T(8,128)(2,1)} %add_convert_fusion.8), channel_id=1, source_target_pairs={{0,1},{1,2},{2,3},{3,7},{7,6},{6,5},{5,4},{4,0},{8,9},{9,10},{10,1... | collective-permute-start | bytes 1179656 | tf_op jit(solution)/shard_map/ppermute | solution.py:497
  516.5 121.9 %collective-permute-start.71 = (bf16[128,1536]{1,0:T(8,128)(2,1)}, bf16[128,1536]{1,0:T(8,128)(2,1)S(1)}, u32[]{:S(2)}, u32[]{:S(2)}) collective-permute-start(bf16[128,1536]{1,0:T(8,128)(2,1)} %get-tuple-element.164), channel_id=1, source_target_pairs={{0,1},{1,2},{2,3},{3,7},{7,6},{6,5},{5,4},{4,0},{8,9},{9,10},{10,1... | collective-permute-start | bytes 1179656 | tf_op jit(solution)/shard_map/ppermute | solution.py:497
  522.0 64.6 %collective-permute-start.73 = (bf16[128,1536]{1,0:T(8,128)(2,1)}, bf16[128,1536]{1,0:T(8,128)(2,1)}, u32[]{:S(2)}, u32[]{:S(2)}) collective-permute-start(bf16[128,1536]{1,0:T(8,128)(2,1)} %get-tuple-element.165), channel_id=1, source_target_pairs={{1,0},{2,1},{3,2},{7,3},{6,7},{5,6},{4,5},{0,4},{9,8},{10,9},{11,1... | collective-permute-start | bytes 1179656 | tf_op jit(solution)/shard_map/ppermute | solution.py:498
  588.4 49.9 %collective-permute-start.74 = (bf16[128,1536]{1,0:T(8,128)(2,1)}, bf16[128,1536]{1,0:T(8,128)(2,1)}, u32[]{:S(2)}, u32[]{:S(2)}) collective-permute-start(bf16[128,1536]{1,0:T(8,128)(2,1)} %add_convert_fusion.5), channel_id=1, source_target_pairs={{1,0},{2,1},{3,2},{7,3},{6,7},{5,6},{4,5},{0,4},{9,8},{10,9},{11,1... | collective-permute-start | bytes 1179656 | tf_op jit(solution)/shard_map/ppermute | solution.py:498
  610.3 28.1 %collective-permute-start.77 = (bf16[128,1536]{1,0:T(8,128)(2,1)}, bf16[128,1536]{1,0:T(8,128)(2,1)S(1)}, u32[]{:S(2)}, u32[]{:S(2)}) collective-permute-start(bf16[128,1536]{1,0:T(8,128)(2,1)} %get-tuple-element.168), channel_id=1, source_target_pairs={{0,1},{1,2},{2,3},{3,7},{7,6},{6,5},{5,4},{4,0},{8,9},{9,10},{10,1... | collective-permute-start | bytes 1179656 | tf_op jit(solution)/shard_map/ppermute | solution.py:497
  (149 other events, 1576.3 us)
Sparse Core Ops, SparseCore 0:
  53.3 31.2 all-gather.8
  87.1 23.9 all-gather.10
  112.7 44.6 all-gather.18
  159.6 45.7 all-gather.14
  207.1 32.1 all-gather.12
  240.8 46.7 all-gather.16
  318.7 62.3 reduce-scatter.4
  384.5 46.1 reduce-scatter.8
  433.0 84.4 reduce-scatter.6
  558.4 56.7 reduce-scatter.10
